TPU v7x, 32 devices: a whole 2x2x4 slice. The times are simulated.
32 devices in a mesh: groups: 2 (over y), lon: 16 (over z, x, core).
Axes of the slice: x: 2, y: 2, z: 4, core: 2. Of those that a mesh axis runs over, the one named last changes fastest.
Arguments:
- ident_maps: bfloat16 [16, 128, 128, 128], P('groups', 'lon'), parts along dimension 0, may hold values from -6 to 6
- identity: int32 [4], P('groups'), parts along dimension 0, may hold values from 0 to 7
- audio: float32 [128, 256], P('groups'), parts along dimension 0, may hold values from -6 to 6
- audio_index: int32 [4], P('groups'), parts along dimension 0, may hold values from 0 to 63
- film_w: float32 [2, 256, 256], replicated, may hold values from -0.1875 to 0.1875
- conv_w: bfloat16 [2, 3, 3, 128, 128], replicated, may hold values from -0.1875 to 0.1875
- dout: bfloat16 [4, 128, 128, 128], P('groups', 'lon'), parts along dimension 0, may hold values from -18 to 18
Outputs:
- decoded: bfloat16 [4, 128, 128, 128], P('groups', 'lon'), parts along dimension 0
- conv_grad: float32 [4, 3, 3, 128, 128], P('groups'), parts along dimension 0
- film_grad: float32 [4, 256, 256], P('groups'), parts along dimension 0
There are 2 independent parts, one for each index of `groups`. A program takes and returns all parts, laid end to end along the dimension named above; an argument that names none is the same for every part. Nothing has to cross between parts.
All inputs are finite; a program needn't handle non-finite values.
Results may differ from a plain program's by a relative error of at most 0.0052.
Values may be sent and summed in bfloat16 or wider, within the bound.
No kernel may reach another device: no remote copies, remote signals or barrier semaphores. Data moves between devices by JAX's collectives and lax.ppermute only.
A program may use at most 64 MiB of HBM per device.

v0:
```python
import math

import jax
import jax.numpy as jnp
from jax import lax
from jax.sharding import PartitionSpec as P


def extended(block, sides, width):
    for axis, dim in sides:
        count = lax.axis_size(axis)
        forward = [(i, i + 1) for i in range(count - 1)]
        forward.append((count - 1, 0))
        backward = [(target, source) for source, target in forward]
        low = lax.ppermute(
            lax.slice_in_dim(block, block.shape[dim] - width, None, axis=dim), axis, forward
        )
        high = lax.ppermute(lax.slice_in_dim(block, 0, width, axis=dim), axis, backward)
        block = jnp.concatenate([low, block, high], axis=dim)
    return block


def conv_taps(padded, weight):
    frames, columns, rows, channels = padded.shape
    out_cols = columns - 2
    zero_row = jnp.zeros((frames, columns, 1, channels), padded.dtype)
    padded_rows = jnp.concatenate([zero_row, padded, zero_row], axis=2)
    stacked = jnp.concatenate(
        [
            padded_rows[:, :, 0:rows],
            padded_rows[:, :, 1 : rows + 1],
            padded_rows[:, :, 2 : rows + 2],
        ],
        axis=3,
    )
    summed = jnp.zeros((frames * out_cols * rows, weight.shape[2]), jnp.float32)
    for offset in range(3):
        window = stacked[:, offset : offset + out_cols].reshape(-1, 3 * channels)
        summed = summed + jnp.dot(window, weight[offset], preferred_element_type=jnp.float32)
    return (summed.reshape(frames, out_cols, rows, weight.shape[2]), stacked)


def tap_grads(stacked, grad_pre, columns):
    flat_grad = grad_pre.reshape(-1, grad_pre.shape[-1])
    pieces = []
    for offset in range(3):
        window = stacked[:, offset : offset + columns].reshape(-1, stacked.shape[-1])
        pieces.append(
            lax.dot_general(
                window, flat_grad, (((0,), (0,)), ((), ())), preferred_element_type=jnp.float32
            )
        )
    return jnp.stack(pieces)


def flip_taps(layer_w):
    channels = layer_w.shape[2]
    return layer_w[::-1, ::-1].swapaxes(2, 3).reshape(3, 3 * channels, channels)


def column_rim(field):
    return extended(field, (("lon", 1),), 1)


def local(ident_maps, identity, audio, audio_index, film_w, conv_w, dout):
    frames = identity.shape[0]
    layers = conv_w.shape[0]
    channels = conv_w.shape[3]
    columns = ident_maps.shape[1]
    rows = ident_maps.shape[2]
    weights = conv_w.reshape(layers, 3, 3 * channels, channels)
    factor = 1.0 / math.sqrt(frames * columns * lax.axis_size("lon") * rows)
    first_map = jnp.take(ident_maps, identity, axis=0)
    picker = (audio_index[:, None] == jnp.arange(audio.shape[0], dtype=jnp.int32)[None, :]).astype(
        jnp.float32
    )
    audio_rows = jnp.dot(picker, audio, precision=lax.Precision.HIGHEST)
    film_rows = jnp.einsum("fa,lak->lfk", audio_rows, film_w, precision=lax.Precision.HIGHEST)
    gains = 1.0 + film_rows[:, :, None, None, :channels]
    offsets = film_rows[:, :, None, None, channels:]
    saved_stack, saved_pre, saved_mod = ([], [], [])
    current = first_map
    for layer in range(layers):
        pre_act, stacked = conv_taps(column_rim(current), weights[layer])
        modulated = pre_act * gains[layer] + offsets[layer]
        current = jax.nn.silu(modulated).astype(jnp.bfloat16)
        saved_stack.append(stacked)
        saved_pre.append(pre_act)
        saved_mod.append(modulated)
    grad_h = dout.astype(jnp.float32) * factor
    wgrads = [None] * layers
    stats = [None] * layers
    for layer in reversed(range(layers)):
        modulated = saved_mod[layer]
        gate_sig = jax.nn.sigmoid(modulated)
        grad_mod = grad_h * (gate_sig * (1.0 + modulated * (1.0 - gate_sig)))
        grad_pre = (grad_mod * gains[layer]).astype(jnp.bfloat16)
        layer_stat = jnp.concatenate(
            [jnp.sum(grad_mod * saved_pre[layer], axis=(1, 2)), jnp.sum(grad_mod, axis=(1, 2))],
            axis=-1,
        )
        layer_wgrad = tap_grads(saved_stack[layer], grad_pre, columns)
        wgrads[layer] = layer_wgrad
        stats[layer] = layer_stat
        if layer > 0:
            padded_grad = extended(grad_pre, (("lon", 1),), 1)
            grad_h, unused = conv_taps(padded_grad, flip_taps(conv_w[layer]))
    all_wgrads = jnp.stack(wgrads)
    all_stats = jnp.stack(stats)
    all_wgrads, all_stats = lax.psum((all_wgrads, all_stats), "lon")
    film_grad = jnp.einsum("fa,lfk->lak", audio_rows, all_stats, precision=lax.Precision.HIGHEST)
    conv_grad = all_wgrads.reshape(layers, 3, 3, channels, channels)
    return (current, conv_grad, film_grad)


def solution(mesh):
    return jax.shard_map(
        local,
        mesh=mesh,
        in_specs=(
            P("groups", "lon", None, None),
            P("groups"),
            P("groups", None),
            P("groups"),
            P(),
            P(),
            P("groups", "lon", None, None),
        ),
        out_specs=(
            P("groups", "lon", None, None),
            P("groups", None, None, None, None),
            P("groups", None, None),
        ),
        check_vma=False,
    )
```

profile of v0, /device:TPU:0, one launch (start us, length us, event | category | flops | bytes accessed | tf_op | source)
XLA Modules:
  0.0 203.7 jit_solution(14544427251913030686)
XLA Ops:
  7.2 0.8 compare_select_fusion
  8.0 0.7 compare_and_fusion
  8.8 0.6 gather_fusion
  9.9 5.5 %collective-permute-start.1 = (bf16[2,1,128,128]{2,3,1,0:T(8,128)(2,1)S(1)}, bf16[2,1,128,128]{2,3,1,0:T(8,128)(2,1)S(1)}, u32[]{:S(2)}, u32[]{:S(2)}) collective-permute-start(bf16[2,1,128,128]{2,3,1,0:T(8,128)(2,1)S(1)} %get-tuple-element.42), channel_id=1, source_target_pairs={{1,0},{2,1},{3,2},{4,3},{5,4},{6,5},{7,6},{8,7},{9,8},{10,9},{11,1... | collective-permute-start | bytes 196616 | tf_op jit(solution)/shard_map/ppermute | solution.py:18
  15.4 0.8 fusion.6
  16.7 0.6 slice_bitcast_fusion
  17.6 0.7 reverse_bitcast_fusion
  18.3 3.4 %collective-permute-done = bf16[2,1,128,128]{2,3,1,0:T(8,128)(2,1)S(1)} collective-permute-done((bf16[2,1,128,128]{2,3,1,0:T(8,128)(2,1)S(1)}, bf16[2,1,128,128]{2,3,1,0:T(8,128)(2,1)S(1)}, u32[]{:S(2)}, u32[]{:S(2)}) %collective-permute-start) | collective-permute-done | bytes 65568 | tf_op jit(solution)/shard_map/ppermute | solution.py:15
  21.9 0.4 pad_slice_fusion.5
  22.4 2.7 %fusion.5 = (bf16[2,8,128,384]{2,3,1,0:T(8,128)(2,1)}, bf16[2,8,128,384]{2,3,1,0:T(8,128)(2,1)S(1)}, bf16[2,8,128,384]{2,3,1,0:T(8,128)(2,1)}) fusion(bf16[2,10,128,384]{2,3,1,0:T(8,128)(2,1)S(1)} %pad_maximum_fusion), kind=kLoop, calls=%fused_computation.61 | loop fusion | bytes 9437184 | tf_op jit(solution)/shard_map/slice | solution.py:38
  25.2 2.6 %copy.25 = bf16[2,8,128,384]{3,2,1,0:T(8,128)(2,1)} copy(bf16[2,8,128,384]{2,3,1,0:T(8,128)(2,1)} %get-tuple-element.23) | data formatting | bytes 3145728 | tf_op jit(solution)/shard_map/slice | solution.py:38
  27.8 1.6 copy.26
  29.4 1.9 copy.27
  31.3 2.1 %fusion.11 = f32[2048,128]{1,0:T(8,128)S(1)} fusion(bf16[2048,384]{1,0:T(8,128)(2,1)} %bitcast.124, bf16[384,128]{1,0:T(8,128)(2,1)} %bitcast.140), kind=kOutput, calls=%fused_computation.67 | convolution fusion | flops 201326592 | bytes 2719744 | tf_op jit(solution)/shard_map/dot_general | solution.py:39
  33.4 0.6 convolution_add_fusion.5
  34.3 1.5 convolution_add_fusion.4
  35.8 1.6 copy.28
  37.4 0.4 multiply_convert_fusion.3
  37.8 0.7 fusion.8
  38.5 1.0 collective-permute-start.3
  39.5 0.7 fusion.10
  40.2 2.0 %copy.33 = bf16[2,8,128,128]{2,3,1,0:T(8,128)(2,1)} copy(bf16[2,8,128,128]{3,2,1,0:T(8,128)(2,1)} %param.13) | data formatting | bytes 1048576 | tf_op args[6]
  42.3 3.9 %collective-permute-done.2 = bf16[2,1,128,128]{2,3,1,0:T(8,128)(2,1)} collective-permute-done((bf16[2,1,128,128]{2,3,1,0:T(8,128)(2,1)}, bf16[2,1,128,128]{2,3,1,0:T(8,128)(2,1)}, u32[]{:S(2)}, u32[]{:S(2)}) %collective-permute-start.2) | collective-permute-done | bytes 65568 | tf_op jit(solution)/shard_map/ppermute | solution.py:15
  46.2 1.0 pad_maximum_fusion.5
  47.6 1.0 pad_maximum_fusion.1
  48.6 2.7 %fusion.4 = (bf16[2,8,128,384]{2,3,1,0:T(8,128)(2,1)}, bf16[2,8,128,384]{2,3,1,0:T(8,128)(2,1)}, bf16[2,8,128,384]{2,3,1,0:T(8,128)(2,1)}) fusion(bf16[2,10,128,384]{2,3,1,0:T(8,128)(2,1)S(1)} %pad_maximum_fusion.1), kind=kLoop, calls=%fused_computation.60 | loop fusion | bytes 9437184 | tf_op jit(solution)/shard_map/slice | solution.py:38
  51.3 2.6 %copy.29 = bf16[2,8,128,384]{3,2,1,0:T(8,128)(2,1)} copy(bf16[2,8,128,384]{2,3,1,0:T(8,128)(2,1)} %get-tuple-element.20) | data formatting | bytes 3145728 | tf_op jit(solution)/shard_map/slice | solution.py:38
  53.9 2.6 %copy.30 = bf16[2,8,128,384]{3,2,1,0:T(8,128)(2,1)} copy(bf16[2,8,128,384]{2,3,1,0:T(8,128)(2,1)} %get-tuple-element.19) | data formatting | bytes 3145728 | tf_op jit(solution)/shard_map/slice | solution.py:38
  56.5 2.7 %copy.31 = bf16[2,8,128,384]{3,2,1,0:T(8,128)(2,1)} copy(bf16[2,8,128,384]{2,3,1,0:T(8,128)(2,1)} %get-tuple-element.18) | data formatting | bytes 3145728 | tf_op jit(solution)/shard_map/slice | solution.py:38
  59.2 2.1 %fusion.12 = f32[2048,128]{1,0:T(8,128)S(1)} fusion(bf16[2048,384]{1,0:T(8,128)(2,1)} %bitcast.125, bf16[384,128]{1,0:T(8,128)(2,1)S(1)} %bitcast.137), kind=kOutput, calls=%fused_computation.68 | convolution fusion | flops 201326592 | bytes 2719744 | tf_op jit(solution)/shard_map/dot_general | solution.py:39
  61.4 0.6 convolution_add_fusion.3
  62.0 0.8 copy-done.4
  62.8 1.5 convolution_add_fusion.2
  64.3 2.6 %copy.32 = f32[2,8,128,128]{2,3,1,0:T(8,128)} copy(f32[2,8,128,128]{3,2,1,0:T(8,128)} %bitcast.129) | data formatting | bytes 2097152 | tf_op jit(solution)/shard_map/reshape | solution.py:40
  66.9 2.9 %multiply_reduce_fusion = (f32[2,128]{1,0:T(2,128)}, f32[2,128]{1,0:T(2,128)}, f32[2,8,128,128]{2,3,1,0:T(8,128)S(1)}, bf16[2,8,128,128]{2,3,1,0:T(8,128)(2,1)S(1)}) fusion(f32[2,8,128,128]{2,3,1,0:T(8,128)} %copy.32, f32[2,128]{1,0:T(2,128)} %get-tuple-element.46, f32[2,128]{1,0:T(2,128)S(1)} %get-tuple-element.51, bf16[2,8,128,128]{2,3,1,0:T(8,128)(2,1)} %copy.33), kind=kLoop, calls=%fused_computation.26 | loop fusion | flops 4455936 | bytes 3149824 | tf_op jit(solution)/shard_map/reduce_sum | solution.py:99
  69.9 0.6 convolution_bitcast_fusion.1
  70.5 0.6 convolution_bitcast_fusion.2
  71.1 0.6 convolution_bitcast_fusion.3
  71.7 0.6 collective-permute-start.5
  72.3 0.9 maximum_bitcast_fusion.1
  73.1 1.0 collective-permute-done.5
  74.2 4.5 %collective-permute-done.4 = bf16[2,1,128,128]{2,3,1,0:T(8,128)(2,1)S(1)} collective-permute-done((bf16[2,1,128,128]{2,3,1,0:T(8,128)(2,1)S(1)}, bf16[2,1,128,128]{2,3,1,0:T(8,128)(2,1)S(1)}, u32[]{:S(2)}, u32[]{:S(2)}) %collective-permute-start.4) | collective-permute-done | bytes 65568 | tf_op jit(solution)/shard_map/ppermute | solution.py:15
  78.7 0.4 pad_slice_fusion.1
  79.3 2.5 %fusion.3 = (bf16[2,8,128,384]{2,3,1,0:T(8,128)(2,1)}, bf16[2,8,128,384]{2,3,1,0:T(8,128)(2,1)}, bf16[2,8,128,384]{2,3,1,0:T(8,128)(2,1)}) fusion(bf16[2,10,128,384]{2,3,1,0:T(8,128)(2,1)S(1)} %pad_maximum_fusion.2), kind=kLoop, calls=%fused_computation.59 | loop fusion | bytes 9437184 | tf_op jit(solution)/shard_map/slice | solution.py:38
  81.8 2.6 %copy.34 = bf16[2,8,128,384]{3,2,1,0:T(8,128)(2,1)} copy(bf16[2,8,128,384]{2,3,1,0:T(8,128)(2,1)} %get-tuple-element.17) | data formatting | bytes 3145728 | tf_op jit(solution)/shard_map/slice | solution.py:38
  84.4 2.6 %copy.36 = bf16[2,8,128,384]{3,2,1,0:T(8,128)(2,1)} copy(bf16[2,8,128,384]{2,3,1,0:T(8,128)(2,1)} %get-tuple-element.16) | data formatting | bytes 3145728 | tf_op jit(solution)/shard_map/slice | solution.py:38
  87.0 2.6 %copy.37 = bf16[2,8,128,384]{3,2,1,0:T(8,128)(2,1)} copy(bf16[2,8,128,384]{2,3,1,0:T(8,128)(2,1)} %get-tuple-element.15) | data formatting | bytes 3145728 | tf_op jit(solution)/shard_map/slice | solution.py:38
  89.6 2.1 %fusion.13 = f32[2048,128]{1,0:T(8,128)S(1)} fusion(bf16[2048,384]{1,0:T(8,128)(2,1)} %bitcast.126, bf16[384,128]{1,0:T(8,128)(2,1)} %bitcast.136), kind=kOutput, calls=%fused_computation.69 | convolution fusion | flops 201326592 | bytes 2719744 | tf_op jit(solution)/shard_map/dot_general | solution.py:39
  91.8 0.6 convolution_add_fusion.1
  92.4 0.8 copy-done.5
  93.2 1.5 convolution_add_fusion
  94.7 2.5 %copy.38 = f32[2,8,128,128]{2,3,1,0:T(8,128)} copy(f32[2,8,128,128]{3,2,1,0:T(8,128)} %bitcast.130) | data formatting | bytes 2097152 | tf_op jit(solution)/shard_map/reshape | solution.py:40
  97.2 2.4 %multiply_reduce_fusion.1 = (f32[2,128]{1,0:T(2,128)S(1)}, f32[2,128]{1,0:T(2,128)}, f32[2,8,128,128]{2,3,1,0:T(8,128)S(1)}) fusion(f32[2,8,128,128]{2,3,1,0:T(8,128)S(1)} %copy.28, f32[2,8,128,128]{2,3,1,0:T(8,128)} %copy.38, f32[2,128]{1,0:T(2,128)S(1)} %get-tuple-element.47, f32[2,128]{1,0:T(2,128)S(1)} %get-tuple-element.50), kind=kLoop, calls=%fused_computation.27 | loop fusion | flops 3407360 | bytes 3149824 | tf_op jit(solution)/shard_map/reduce_sum | solution.py:99
  99.9 0.6 convolution_bitcast_fusion.4
  100.4 0.6 convolution_bitcast_fusion.5
  101.0 0.6 convolution_bitcast_fusion.6
  101.6 0.4 copy-done.9
  102.1 1.1 pad_maximum_fusion.3
  103.2 1.0 copy.47
  104.3 30.1 %psum.15 = f32[2,2,256]{2,1,0:T(2,128)S(1)} all-reduce(f32[2,2,256]{2,1,0:T(2,128)S(1)} %pad_maximum_fusion.7), channel_id=1, replica_groups=mesh['groups'=2,'lon'=16] {'lon'}, use_global_device_ids=true, to_apply=%region_5.6 | all-reduce | flops 1024 | bytes 8192 | tf_op jit(solution)/shard_map/psum | solution.py:110
  134.4 0.6 convolution_bitcast_fusion
  135.1 1.0 copy.48
  136.1 58.4 %all-reduce.8.cloned.1.call-done = f32[2,3,3,128,128]{4,3,2,1,0:T(8,128)} async-done(((f32[2,3,3,128,128]{4,3,2,1,0:T(8,128)}), f32[2,3,3,128,128]{4,3,2,1,0:T(8,128)}) %all-reduce.8.cloned.1.call-update) | async-done | bytes 1179664 | tf_op jit(solution)/shard_map/psum | solution.py:110
  194.4 2.4 %copy.63 = f32[2,3,3,128,128]{4,3,2,1,0:T(8,128)} copy(f32[2,3,3,128,128]{4,3,2,1,0:T(8,128)} %all-reduce.8.cloned.1.call-done) | data formatting | bytes 2359296
  (76 shorter events, 3.0 us)
Async XLA Ops:
  7.2 1.6 copy-start
  7.2 8.2 %copy-start.10 = (bf16[2,3,3,128,128]{4,3,2,1,0:T(8,128)(2,1)S(1)}, bf16[2,3,3,128,128]{4,3,2,1,0:T(8,128)(2,1)}, u32[]{:S(2)}) copy-start(bf16[2,3,3,128,128]{4,3,2,1,0:T(8,128)(2,1)} %param.12) | copy-start | bytes 1769476
  7.2 187.2 %all-reduce.8.cloned.1.call-start = ((), (), s32[]{:S(2)}) async-start(), calls=%async_computation | async-start | bytes 2359296 | tf_op jit(solution)/shard_map/psum | solution.py:110
  9.4 6.8 %copy-start.20 = (f32[64,256]{1,0:T(8,128)S(1)}, f32[64,256]{1,0:T(8,128)}, u32[]{:S(2)}) copy-start(f32[64,256]{1,0:T(8,128)} %param.9) | copy-start | bytes 196612
  9.4 6.7 %copy-start.24 = (s32[2]{0:T(128)S(1)}, s32[2]{0:T(128)}, u32[]{:S(2)}) copy-start(s32[2]{0:T(128)} %param.10) | copy-start | bytes 28
  9.5 6.9 %copy-start.12 = (f32[2,256,256]{2,1,0:T(8,128)S(1)}, f32[2,256,256]{2,1,0:T(8,128)}, u32[]{:S(2)}) copy-start(f32[2,256,256]{2,1,0:T(8,128)} %param.11) | copy-start | bytes 1572868
  9.8 7.6 %slice-start = ((bf16[2,3,3,128,128]{4,3,2,1,0:T(8,128)(2,1)}), bf16[1,3,3,128,128]{4,3,2,1,0:T(8,128)(2,1)S(1)}, s32[]{:S(2)}) async-start(bf16[2,3,3,128,128]{4,3,2,1,0:T(8,128)(2,1)} %param.12), calls=%async_computation.1 | async-start | bytes 589824 | tf_op jit(solution)/shard_map/slice | solution.py:107
  9.9 8.4 %collective-permute-start.1 = (bf16[2,1,128,128]{2,3,1,0:T(8,128)(2,1)S(1)}, bf16[2,1,128,128]{2,3,1,0:T(8,128)(2,1)S(1)}, u32[]{:S(2)}, u32[]{:S(2)}) collective-permute-start(bf16[2,1,128,128]{2,3,1,0:T(8,128)(2,1)S(1)} %get-tuple-element.42), channel_id=1, source_target_pairs={{1,0},{2,1},{3,2},{4,3},{5,4},{6,5},{7,6},{8,7},{9,8},{10,9},{11,1... | collective-permute-start | bytes 196616 | tf_op jit(solution)/shard_map/ppermute | solution.py:18
  15.4 6.4 %collective-permute-start = (bf16[2,1,128,128]{2,3,1,0:T(8,128)(2,1)S(1)}, bf16[2,1,128,128]{2,3,1,0:T(8,128)(2,1)S(1)}, u32[]{:S(2)}, u32[]{:S(2)}) collective-permute-start(bf16[2,1,128,128]{2,3,1,0:T(8,128)(2,1)S(1)} %get-tuple-element.41), channel_id=1, source_target_pairs={{0,1},{1,2},{2,3},{3,4},{4,5},{5,6},{6,7},{7,8},{8,9},{9,10},{10,1... | collective-permute-start | bytes 196616 | tf_op jit(solution)/shard_map/ppermute | solution.py:15
  31.3 2.1 %copy-start.6 = (bf16[2,8,128,384]{3,2,1,0:T(8,128)(2,1)S(1)}, bf16[2,8,128,384]{3,2,1,0:T(8,128)(2,1)}, u32[]{:S(2)}) copy-start(bf16[2,8,128,384]{3,2,1,0:T(8,128)(2,1)} %copy.26) | copy-start | bytes 4718596
  31.3 2.1 %copy-start.19 = (bf16[1,1,3,128,128]{4,3,2,1,0:T(8,128)(2,1)S(1)}, bf16[1,1,3,128,128]{4,3,2,1,0:T(8,128)(2,1)}, u32[]{:S(2)}) copy-start(bf16[1,1,3,128,128]{4,3,2,1,0:T(8,128)(2,1)} %get-tuple-element.35) | copy-start | bytes 294916
  33.4 0.9 copy-start.18
  37.4 2.1 %copy-start.11 = (bf16[3,3,128,128]{3,2,1,0:T(8,128)(2,1)S(1)}, bf16[3,3,128,128]{3,2,1,0:T(8,128)(2,1)}, u32[]{:S(2)}) copy-start(bf16[3,3,128,128]{3,2,1,0:T(8,128)(2,1)} %reverse_bitcast_fusion) | copy-start | bytes 884740
  38.5 3.8 %collective-permute-start.3 = (bf16[2,1,128,128]{2,3,1,0:T(8,128)(2,1)}, bf16[2,1,128,128]{2,3,1,0:T(8,128)(2,1)}, u32[]{:S(2)}, u32[]{:S(2)}) collective-permute-start(bf16[2,1,128,128]{2,3,1,0:T(8,128)(2,1)} %get-tuple-element.40), channel_id=1, source_target_pairs={{1,0},{2,1},{3,2},{4,3},{5,4},{6,5},{7,6},{8,7},{9,8},{10,9},{11,1... | collective-permute-start | bytes 196616 | tf_op jit(solution)/shard_map/ppermute | solution.py:18
  39.5 6.7 %collective-permute-start.2 = (bf16[2,1,128,128]{2,3,1,0:T(8,128)(2,1)}, bf16[2,1,128,128]{2,3,1,0:T(8,128)(2,1)}, u32[]{:S(2)}, u32[]{:S(2)}) collective-permute-start(bf16[2,1,128,128]{2,3,1,0:T(8,128)(2,1)} %get-tuple-element.39), channel_id=1, source_target_pairs={{0,1},{1,2},{2,3},{3,4},{4,5},{5,6},{6,7},{7,8},{8,9},{9,10},{10,1... | collective-permute-start | bytes 196616 | tf_op jit(solution)/shard_map/ppermute | solution.py:15
  48.6 2.8 %copy-start.2 = (bf16[2,10,128,384]{2,3,1,0:T(8,128)(2,1)}, bf16[2,10,128,384]{2,3,1,0:T(8,128)(2,1)S(1)}, u32[]{:S(2)}) copy-start(bf16[2,10,128,384]{2,3,1,0:T(8,128)(2,1)S(1)} %pad_maximum_fusion.1) | copy-start | bytes 5898244
  56.5 2.7 %copy-start.17 = (bf16[1,1,3,128,128]{4,3,2,1,0:T(8,128)(2,1)S(1)}, bf16[1,1,3,128,128]{4,3,2,1,0:T(8,128)(2,1)}, u32[]{:S(2)}) copy-start(bf16[1,1,3,128,128]{4,3,2,1,0:T(8,128)(2,1)} %get-tuple-element.33) | copy-start | bytes 294916
  59.2 2.1 %copy-start.7 = (bf16[2,8,128,384]{3,2,1,0:T(8,128)(2,1)S(1)}, bf16[2,8,128,384]{3,2,1,0:T(8,128)(2,1)}, u32[]{:S(2)}) copy-start(bf16[2,8,128,384]{3,2,1,0:T(8,128)(2,1)} %copy.30) | copy-start | bytes 4718596
  59.2 2.1 %copy-start.16 = (bf16[1,1,3,128,128]{4,3,2,1,0:T(8,128)(2,1)S(1)}, bf16[1,1,3,128,128]{4,3,2,1,0:T(8,128)(2,1)}, u32[]{:S(2)}) copy-start(bf16[1,1,3,128,128]{4,3,2,1,0:T(8,128)(2,1)} %get-tuple-element.32) | copy-start | bytes 294916
  61.3 1.4 copy-start.4
  61.4 1.4 copy-start.14
  66.9 3.1 %copy-start.3 = (bf16[2,10,128,384]{2,3,1,0:T(8,128)(2,1)S(1)}, bf16[2,10,128,384]{2,3,1,0:T(8,128)(2,1)}, u32[]{:S(2)}) copy-start(bf16[2,10,128,384]{2,3,1,0:T(8,128)(2,1)} %copy-done.2) | copy-start | bytes 5898244
  71.7 2.5 %collective-permute-start.5 = (bf16[2,1,128,128]{2,3,1,0:T(8,128)(2,1)S(1)}, bf16[2,1,128,128]{2,3,1,0:T(8,128)(2,1)S(1)}, u32[]{:S(2)}, u32[]{:S(2)}) collective-permute-start(bf16[2,1,128,128]{2,3,1,0:T(8,128)(2,1)S(1)} %get-tuple-element.38), channel_id=1, source_target_pairs={{1,0},{2,1},{3,2},{4,3},{5,4},{6,5},{7,6},{8,7},{9,8},{10,9},{11,1... | collective-permute-start | bytes 196616 | tf_op jit(solution)/shard_map/ppermute | solution.py:18
  72.3 6.4 %collective-permute-start.4 = (bf16[2,1,128,128]{2,3,1,0:T(8,128)(2,1)S(1)}, bf16[2,1,128,128]{2,3,1,0:T(8,128)(2,1)S(1)}, u32[]{:S(2)}, u32[]{:S(2)}) collective-permute-start(bf16[2,1,128,128]{2,3,1,0:T(8,128)(2,1)S(1)} %get-tuple-element.37), channel_id=1, source_target_pairs={{0,1},{1,2},{2,3},{3,4},{4,5},{5,6},{6,7},{7,8},{8,9},{9,10},{10,1... | collective-permute-start | bytes 196616 | tf_op jit(solution)/shard_map/ppermute | solution.py:15
  89.6 2.1 %copy-start.8 = (bf16[2,8,128,384]{3,2,1,0:T(8,128)(2,1)S(1)}, bf16[2,8,128,384]{3,2,1,0:T(8,128)(2,1)}, u32[]{:S(2)}) copy-start(bf16[2,8,128,384]{3,2,1,0:T(8,128)(2,1)} %copy.36) | copy-start | bytes 4718596
  89.6 2.1 %copy-start.15 = (bf16[1,3,128,128]{3,2,1,0:T(8,128)(2,1)S(1)}, bf16[1,3,128,128]{3,2,1,0:T(8,128)(2,1)}, u32[]{:S(2)}) copy-start(bf16[1,3,128,128]{3,2,1,0:T(8,128)(2,1)} %get-tuple-element.44) | copy-start | bytes 294916
  91.7 1.4 copy-start.5
  91.8 1.4 copy-start.13
  101.0 1.1 copy-start.9
  102.1 2.1 %copy-start.21 = (f32[2,128]{1,0:T(2,128)S(1)}, f32[2,128]{1,0:T(2,128)}, u32[]{:S(2)}) copy-start(f32[2,128]{1,0:T(2,128)} %get-tuple-element.11) | copy-start | bytes 3076
  102.1 2.1 %copy-start.22 = (f32[2,128]{1,0:T(2,128)S(1)}, f32[2,128]{1,0:T(2,128)}, u32[]{:S(2)}) copy-start(f32[2,128]{1,0:T(2,128)} %get-tuple-element.12) | copy-start | bytes 3076
  102.1 2.1 %copy-start.23 = (f32[2,128]{1,0:T(2,128)S(1)}, f32[2,128]{1,0:T(2,128)}, u32[]{:S(2)}) copy-start(f32[2,128]{1,0:T(2,128)} %get-tuple-element.10) | copy-start | bytes 3076
  104.3 92.5 %copy-start.1 = (bf16[8,8,128,128]{3,2,1,0:T(8,128)(2,1)S(1)}, bf16[8,8,128,128]{3,2,1,0:T(8,128)(2,1)}, u32[]{:S(2)}) copy-start(bf16[8,8,128,128]{3,2,1,0:T(8,128)(2,1)} %param.7) | copy-start | bytes 6291460
Sparse Core Ops, SparseCore 0:
  103.3 91.0 all-reduce.7
where the time goes:
time: 204 us
  waiting for transfers between devices  71.3 us (35%)
  local copies, waits for them, and re-layouts  51.3 us (25%)
  blocking collectives  30.1 us (15%)
  matrix products  17.2 us (8%)
  between operations  14.5 us (7%)
  other arithmetic  12.1 us (6%)
  starting transfers between devices  7.1 us (3%)
    psum x1, waiting for transfers between devices, local(): all_wgrads, all_stats = lax.psum((all_wgrads, all_stats), 'lon')  58.4 us
    psum x1, blocking collectives, local(): all_wgrads, all_stats = lax.psum((all_wgrads, all_stats), 'lon')  30.1 us
    slice x12, local copies, waits for them, and re-layouts, conv_taps(): window = stacked[:, offset:offset + out_cols].reshape(-1, 3 * channels)  29.8 us
    dot_general x9, matrix products, conv_taps(): jnp.dot(window, weight[offset], preferred_element_type=jnp.float32)  12.6 us
    ppermute x3, waiting for transfers between devices, extended(): lax.ppermute(lax.slice_in_dim(block, block.shape[dim] - width, None, axis...  11.8 us
    unnamed x55, local copies, waits for them, and re-layouts  9.13 us
    ppermute x3, starting transfers between devices, extended(): lax.ppermute(lax.slice_in_dim(block, 0, width, axis=dim), axis, backward)  7.05 us
    reshape x3, local copies, waits for them, and re-layouts, conv_taps(): return (summed.reshape(frames, out_cols, rows, weight.shape[2]), stacked)  6.64 us
  transfers between devices with their start and end apart: 7, of which 5 were waited for; matrix products, arithmetic and copies ran while one was open for 5% of the time, Pallas kernels for 0%

commit v1 on v0

v1 whole, which is shorter than its diff:
```python
import functools
import math

import jax
import jax.numpy as jnp
from jax import lax
from jax.experimental import pallas as pl
from jax.experimental.pallas import tpu as pltpu
from jax.sharding import PartitionSpec as P

AXIS = "lon"
RIM = 3
F32 = jnp.float32
BF16 = jnp.bfloat16


def chunk_of(count, largest):
    return max(size for size in range(1, largest + 1) if count % size == 0)


def shift_stack(values, rows):
    total = values.shape[0]
    place = lax.broadcasted_iota(jnp.int32, values.shape, 0) % rows
    above = jnp.where(place == 0, 0.0, pltpu.roll(values, 1, 0))
    below = jnp.where(place == rows - 1, 0.0, pltpu.roll(values, total - 1, 0))
    return jnp.concatenate([above.astype(BF16), values.astype(BF16), below.astype(BF16)], axis=1)


def windows(stack, frame, starts, size):
    parts = []
    for a in range(3):
        blocks = [stack[frame, start + a : start + a + size] for start in starts]
        blocks = [block.reshape(-1, block.shape[-1]) for block in blocks]
        parts.append(blocks[0] if len(blocks) == 1 else jnp.concatenate(blocks, axis=0))
    return jnp.concatenate(parts, axis=1)


def step_kernel(
    factor,
    identity,
    maps,
    low,
    high,
    dout,
    dlow,
    dhigh,
    film,
    weights,
    decoded,
    taps_0,
    taps_1,
    stats,
    first,
    stack_0,
    stack_1,
    stack_d,
    saved_pre,
    turned,
    sems,
):
    frames, columns, rows, channels = dout.shape
    copies = []
    for f in range(frames):
        copies.append(pltpu.make_async_copy(maps.at[identity[f]], first.at[f], sems.at[f]))
        copies[-1].start()

    def put(stack, f, start, size, values):
        stacked = shift_stack(values, rows)
        stack[f, start : start + size] = stacked.reshape(size, rows, 3 * channels)

    def flat(values):
        return values.reshape(-1, channels)

    def gain_of(layer, f):
        return 1.0 + film[layer, f : f + 1, :channels]

    def offset_of(layer, f):
        return film[layer, f : f + 1, channels:]

    for f in range(frames):
        put(stack_0, f, 0, RIM, flat(low[f].astype(F32)))
        put(stack_0, f, RIM + columns, RIM, flat(high[f].astype(F32)))
    inner = chunk_of(columns, 4)
    for f in range(frames):
        copies[f].wait()
        for c in range(0, columns, inner):
            put(stack_0, f, RIM + c, inner, flat(first[f, c : c + inner].astype(F32)))

    weight_0 = weights[0].reshape(9 * channels, channels)
    weight_1 = weights[1].reshape(9 * channels, channels)

    for f in range(frames):
        gain, offset = gain_of(0, f), offset_of(0, f)

        def forward_0(starts, size):
            pre = jnp.dot(windows(stack_0, f, starts, size), weight_0, preferred_element_type=F32)
            mod = pre * gain + offset
            return pre, mod * jax.nn.sigmoid(mod)

        pre, hidden = forward_0((1 - 1, columns + 2), 2)
        put(stack_1, f, 0, 2, hidden[: 2 * rows])
        put(stack_1, f, columns + 2, 2, hidden[2 * rows :])
        for c in range(0, columns, inner):
            pre, hidden = forward_0((c + 2,), inner)
            saved_pre[f, c : c + inner] = pre.reshape(inner, rows, channels)
            put(stack_1, f, c + 2, inner, hidden)

    sums = {}

    def collect(layer, f, grad_mod, pre):
        product = jnp.sum(grad_mod * pre, axis=0, keepdims=True)
        plain = jnp.sum(grad_mod, axis=0, keepdims=True)
        if (layer, f) in sums:
            before = sums[layer, f]
            sums[layer, f] = (before[0] + product, before[1] + plain)
        else:
            sums[layer, f] = (product, plain)

    for f in range(frames):
        gain, offset = gain_of(1, f), offset_of(1, f)

        def both_1(starts, size, grad):
            pre = jnp.dot(windows(stack_1, f, starts, size), weight_1, preferred_element_type=F32)
            mod = pre * gain + offset
            gate = jax.nn.sigmoid(mod)
            grad_mod = (grad.astype(F32) * factor) * (gate * (1.0 + mod * (1.0 - gate)))
            return pre, mod * gate, grad_mod, grad_mod * gain

        grad = jnp.concatenate([flat(dlow[f]), flat(dhigh[f])], axis=0)
        pre, hidden, grad_mod, grad_pre = both_1((0, columns + 1), 1, grad)
        put(stack_d, f, 0, 1, grad_pre[:rows])
        put(stack_d, f, columns + 1, 1, grad_pre[rows:])
        for c in range(0, columns, inner):
            pre, hidden, grad_mod, grad_pre = both_1((c + 1,), inner, flat(dout[f, c : c + inner]))
            decoded[f, c : c + inner] = hidden.astype(BF16).reshape(inner, rows, channels)
            collect(1, f, grad_mod, pre)
            put(stack_d, f, c + 1, inner, grad_pre)
            turned[f, :, c * rows : (c + inner) * rows] = grad_pre.T.astype(BF16)

    def tap_sums(stack, offset, out):
        for a in range(3):
            total = jnp.zeros((channels, 3 * channels), F32)
            for f in range(frames):
                window = stack[f, offset + a : offset + a + columns].reshape(-1, 3 * channels)
                total = total + jnp.dot(turned[f], window, preferred_element_type=F32)
            out[a * 3 * channels : (a + 1) * 3 * channels, :] = total.T.astype(out.dtype)

    tap_sums(stack_1, 1, taps_1)

    flipped = jnp.concatenate(
        [weights[1, 2 - a, 2 - b] for a in range(3) for b in range(3)], axis=1
    )
    for f in range(frames):
        gain, offset = gain_of(0, f), offset_of(0, f)
        for c in range(0, columns, inner):
            grad = lax.dot_general(
                windows(stack_d, f, (c,), inner),
                flipped,
                (((1,), (1,)), ((), ())),
                preferred_element_type=F32,
            )
            pre = flat(saved_pre[f, c : c + inner])
            mod = pre * gain + offset
            gate = jax.nn.sigmoid(mod)
            grad_mod = grad * (gate * (1.0 + mod * (1.0 - gate)))
            collect(0, f, grad_mod, pre)
            turned[f, :, c * rows : (c + inner) * rows] = (grad_mod * gain).T.astype(BF16)
    tap_sums(stack_0, 2, taps_0)

    for (layer, f), (product, plain) in sums.items():
        stats[layer, f : f + 1, :channels] = product
        stats[layer, f : f + 1, channels:] = plain


def local_step(factor, identity, maps, low, high, dout, dlow, dhigh, film, weights):
    frames, columns, rows, channels = dout.shape
    layers = weights.shape[0]
    vmem = pl.BlockSpec(memory_space=pltpu.VMEM)
    taps = jax.ShapeDtypeStruct((9 * channels, channels), BF16)
    return pl.pallas_call(
        functools.partial(step_kernel, factor),
        out_shape=(
            jax.ShapeDtypeStruct(dout.shape, BF16),
            taps,
            taps,
            jax.ShapeDtypeStruct((layers, frames, 2 * channels), F32),
        ),
        in_specs=[
            pl.BlockSpec(memory_space=pltpu.SMEM),
            pl.BlockSpec(memory_space=pl.ANY),
        ]
        + [vmem] * 7,
        out_specs=(vmem,) * 4,
        scratch_shapes=[
            pltpu.VMEM((frames, columns, rows, channels), BF16),
            pltpu.VMEM((frames, columns + 6, rows, 3 * channels), BF16),
            pltpu.VMEM((frames, columns + 4, rows, 3 * channels), BF16),
            pltpu.VMEM((frames, columns + 2, rows, 3 * channels), BF16),
            pltpu.VMEM((frames, columns, rows, channels), F32),
            pltpu.VMEM((frames, channels, columns * rows), BF16),
            pltpu.SemaphoreType.DMA((frames,)),
        ],
        compiler_params=pltpu.CompilerParams(vmem_limit_bytes=48 << 20),
        cost_estimate=pl.CostEstimate(
            flops=6 * 2 * 9 * channels * channels * frames * columns * rows,
            transcendentals=4 * frames * columns * rows * channels,
            bytes_accessed=8 << 20,
        ),
        name="decoder_step",
    )(identity, maps, low, high, dout, dlow, dhigh, film, weights)


def swap(value, bit):
    count = lax.axis_size(AXIS)
    return lax.ppermute(value, AXIS, [(i, i ^ bit) for i in range(count)])


def halve(value, bit):
    half = value.shape[0] // 2
    mine = (lax.axis_index(AXIS) // bit) % 2
    keep = lax.dynamic_slice_in_dim(value, mine * half, half, 0)
    send = lax.dynamic_slice_in_dim(value, (1 - mine) * half, half, 0)
    return (keep.astype(F32) + swap(send, bit).astype(F32)).astype(value.dtype)


def share(value, bit):
    return (value.astype(F32) + swap(value, bit).astype(F32)).astype(value.dtype)


def join(value, bit):
    other = swap(value, bit)
    mine = (lax.axis_index(AXIS) // bit) % 2
    return jnp.concatenate(
        [jnp.where(mine == 0, value, other), jnp.where(mine == 0, other, value)], axis=0
    )


def all_sums(first, second, small):
    bits = []
    while (1 << len(bits)) < lax.axis_size(AXIS):
        bits.append(1 << len(bits))
    orders = [list(bits), list(bits)]
    if len(bits) > 2:
        orders[1][1], orders[1][2] = bits[2], bits[1]
    values = [first, second]
    for step in range(len(bits)):
        for s in range(2):
            values[s] = (halve if step < 2 else share)(values[s], orders[s][step])
        small = share(small, orders[1][step])
    for step in reversed(range(min(2, len(bits)))):
        for s in range(2):
            values[s] = join(values[s], orders[s][step])
    return values[0], values[1], small


def local(ident_maps, identity, audio, audio_index, film_w, conv_w, dout):
    frames = identity.shape[0]
    layers = conv_w.shape[0]
    channels = conv_w.shape[3]
    columns, rows = ident_maps.shape[1:3]
    count = lax.axis_size(AXIS)
    factor = 1.0 / math.sqrt(frames * columns * count * rows)

    def edge(start):
        size = (1, RIM, rows, channels)
        return jnp.concatenate(
            [lax.dynamic_slice(ident_maps, (identity[f], start, 0, 0), size) for f in range(frames)]
        )

    forward = [(i, (i + 1) % count) for i in range(count)]
    backward = [(i, (i - 1) % count) for i in range(count)]
    low = lax.ppermute(edge(columns - RIM), AXIS, forward)
    high = lax.ppermute(edge(0), AXIS, backward)
    dlow = lax.ppermute(dout[:, columns - 1 :], AXIS, forward)
    dhigh = lax.ppermute(dout[:, :1], AXIS, backward)
    audio_rows = jnp.concatenate(
        [lax.dynamic_slice_in_dim(audio, audio_index[f], 1, 0) for f in range(frames)]
    )
    film = jnp.einsum("fa,lak->lfk", audio_rows, film_w, precision=lax.Precision.HIGHEST)
    decoded, taps_0, taps_1, stats = local_step(
        factor, identity, ident_maps, low, high, dout, dlow, dhigh, film, conv_w
    )
    sum_1, sum_0, stats = all_sums(taps_1, taps_0, stats)
    film_grad = jnp.einsum("fa,lfk->lak", audio_rows, stats, precision=lax.Precision.HIGHEST)
    conv_grad = jnp.stack([sum_0, sum_1]).astype(F32).reshape(layers, 3, 3, channels, channels)
    return decoded, conv_grad, film_grad


def solution(mesh):
    return jax.shard_map(
        local,
        mesh=mesh,
        in_specs=(
            P("groups", "lon", None, None),
            P("groups"),
            P("groups", None),
            P("groups"),
            P(),
            P(),
            P("groups", "lon", None, None),
        ),
        out_specs=(
            P("groups", "lon", None, None),
            P("groups", None, None, None, None),
            P("groups", None, None),
        ),
        check_vma=False,
    )
```

time: 204 us -> 71.3 us (0.35)
  waiting for transfers between devices: 71.3 us -> 21.7 us
  local copies, waits for them, and re-layouts: 51.3 us -> 10.8 us
  blocking collectives: 30.1 us -> 0 us
  matrix products: 17.2 us -> 0.99 us
  starting transfers between devices: 7.1 us -> 18.8 us
  other arithmetic: 12.1 us -> 1.61 us
  Pallas kernels: 0 us -> 8.27 us
  between operations: 14.5 us -> 8.53 us
    psum x1 -> x0, waiting for transfers between devices: 58.4 us -> none  [local(): all_wgrads, all_stats = lax.psum((all_wgrads, all_stats), 'lon')]
    psum x1 -> x0, blocking collectives: 30.1 us -> none  [local(): all_wgrads, all_stats = lax.psum((all_wgrads, all_stats), 'lon')]
    slice x22 -> x3, local copies, waits for them, and re-layouts: 33.2 us -> 4.24 us  [the longest x1 1.53 us: local(): dhigh = lax.ppermute(dout[:, :1], AXIS, backward)]
    dot_general x17 -> x1, matrix products: 16.8 us -> 0.64 us  [local(): jnp.einsum('fa,lfk->lak', audio_rows, stats, precision=lax.Precision.HIGH...]
    ppermute x6 -> x20, starting transfers between devices: 7.06 us -> 18.8 us  [the longest x16 8.84 us: swap(): return lax.ppermute(value, AXIS, [(i, i ^ bit) for i in range(count)])]
    ppermute x6 -> x20, waiting for transfers between devices: 12.9 us -> 21.7 us  [the longest x16 21.7 us: swap(): return lax.ppermute(value, AXIS, [(i, i ^ bit) for i in range(count)])]
    pallas_call x0 -> x1, Pallas kernels: none -> 8.27 us  [local_step(): pl.pallas_call(functools.partial(step_kernel, factor), out_shape=(jax.Sha...]
    reshape x3 -> x0, local copies, waits for them, and re-layouts: 6.64 us -> none  [conv_taps(): return (summed.reshape(frames, out_cols, rows, weight.shape[2]), stacked)]
  transfers between devices with their start and end apart: 7 -> 20, of which waited for: 5 -> 9; matrix products, arithmetic and copies ran while one was open for 5% -> 8% of each run, Pallas kernels for 0% -> 0%
where the time goes in v1:
time: 71.3 us; the launch traced here: 70.8 us
  waiting for transfers between devices  21.7 us (30%)
  starting transfers between devices  18.8 us (26%)
  local copies, waits for them, and re-layouts  10.8 us (15%)
  between operations  8.53 us (12%)
  Pallas kernels  8.27 us (12%)
  other arithmetic  1.61 us (2%)
  matrix products  0.99 us (1%)
    ppermute x16, waiting for transfers between devices, swap(): return lax.ppermute(value, AXIS, [(i, i ^ bit) for i in range(count)])  21.7 us
    ppermute x16, starting transfers between devices, swap(): return lax.ppermute(value, AXIS, [(i, i ^ bit) for i in range(count)])  8.84 us
    pallas_call x1, Pallas kernels, local_step(): pl.pallas_call(functools.partial(step_kernel, factor), out_shape=(jax.Sha...  8.27 us
    ppermute x1, starting transfers between devices, local(): high = lax.ppermute(edge(0), AXIS, backward)  5.04 us
    unnamed x15, local copies, waits for them, and re-layouts  4.72 us
    ppermute x1, starting transfers between devices, local(): dhigh = lax.ppermute(dout[:, :1], AXIS, backward)  4.44 us
    slice x1, local copies, waits for them, and re-layouts, local(): dhigh = lax.ppermute(dout[:, :1], AXIS, backward)  1.53 us
  transfers between devices with their start and end apart: 20, of which 9 were waited for; matrix products, arithmetic and copies ran while one was open for 8% of the time, Pallas kernels for 0%

profile of v1, /device:TPU:0, one launch (start us, length us, event | category | flops | bytes accessed | tf_op | source)
XLA Modules:
  0.0 70.8 jit_solution(8954491299405751704)
XLA Ops:
  0.6 0.0 copy-start
  0.6 0.0 copy-start.3
  0.7 0.0 copy-start.1
  0.7 1.4 %fusion.5 = (s32[1]{0:T(128)}, s32[1]{0:T(128)}) fusion(s32[2]{0:T(128)} %identity.1), kind=kLoop, calls=%fused_computation.41 | loop fusion | bytes 16 | tf_op jit(solution)/shard_map/slice | solution.py:267
  6.0 1.1 %constant_dynamic-slice_fusion.7 = (bf16[1,3,128,128]{3,2,1,0:T(8,128)(2,1)S(1)}, bf16[1,3,128,128]{3,2,1,0:T(8,128)(2,1)S(1)}, bf16[1,3,128,128]{3,2,1,0:T(8,128)(2,1)S(1)}, bf16[1,3,128,128]{3,2,1,0:T(8,128)(2,1)S(1)}) fusion(bf16[8,8,128,128]{3,2,1,0:T(8,128)(2,1)} %maps.1, s32[]{:T(128)S(6)} %select_n.114, s32[]{:T(128)S(6)} %select_n.115), kind=kLoop, calls=%fused_computation.33 | loop fusion | bytes 786440 | tf_op jit(solution)/shard_map/dynamic_slice | solution.py:267
  7.1 0.5 collective-permute-start
  7.6 5.0 %collective-permute-start.1 = (bf16[2,3,128,128]{3,2,1,0:T(8,128)(2,1)S(1)}, bf16[2,3,128,128]{3,2,1,0:T(8,128)(2,1)S(1)}, u32[]{:S(2)}, u32[]{:S(2)}) collective-permute-start(bf16[2,3,128,128]{3,2,1,0:T(8,128)(2,1)S(1)} %pad_maximum_fusion.3), channel_id=1, source_target_pairs={{0,15},{1,0},{2,1},{3,2},{4,3},{5,4},{6,5},{7,6},{8,7},{9,8},{10,9... | collective-permute-start | bytes 589832 | tf_op jit(solution)/shard_map/ppermute | solution.py:273
  12.6 1.5 %fusion.3 = (bf16[2,1,128,128]{3,2,1,0:T(8,128)(2,1)}, bf16[2,1,128,128]{3,2,1,0:T(8,128)(2,1)}) fusion(bf16[2,8,128,128]{3,2,1,0:T(8,128)(2,1)} %dout.1), kind=kLoop, calls=%fused_computation.39 | loop fusion | bytes 262144 | tf_op jit(solution)/shard_map/slice | solution.py:275
  14.2 0.0 collective-permute-start.2
  14.2 4.4 %collective-permute-start.3 = (bf16[2,1,128,128]{3,2,1,0:T(8,128)(2,1)}, bf16[2,1,128,128]{3,2,1,0:T(8,128)(2,1)S(1)}, u32[]{:S(2)}, u32[]{:S(2)}) collective-permute-start(bf16[2,1,128,128]{3,2,1,0:T(8,128)(2,1)} %get-tuple-element.18), channel_id=1, source_target_pairs={{0,15},{1,0},{2,1},{3,2},{4,3},{5,4},{6,5},{7,6},{8,7},{9,8},{10,9... | collective-permute-start | bytes 196616 | tf_op jit(solution)/shard_map/ppermute | solution.py:275
  18.6 1.3 %fusion.4 = (s32[1]{0:T(128)}, s32[1]{0:T(128)}) fusion(s32[2]{0:T(128)} %param.10), kind=kLoop, calls=%fused_computation.40 | loop fusion | bytes 16 | tf_op jit(solution)/shard_map/slice | solution.py:277
  23.5 0.7 %constant_dynamic-slice_fusion.5 = (f32[1,256]{1,0:T(1,128)S(1)}, f32[1,256]{1,0:T(1,128)S(1)}) fusion(f32[64,256]{1,0:T(8,128)} %param.9, s32[]{:T(128)S(6)} %select_n.116, s32[]{:T(128)S(6)} %select_n.117), kind=kLoop, calls=%fused_computation.31 | loop fusion | bytes 4104 | tf_op jit(solution)/shard_map/dynamic_slice | solution.py:277
  24.2 0.0 copy-done
  24.2 0.4 convolution_bitcast_fusion.1.film
  24.6 0.0 collective-permute-done.2.dlow
  24.6 0.0 collective-permute-done.3.dhigh
  24.6 0.0 collective-permute-done.low
  24.6 0.0 collective-permute-done.1.high
  24.6 0.0 copy-start.5
  24.6 0.7 copy-done.5
  25.3 0.0 copy-done.3
  25.3 0.0 copy-done.1
  25.3 0.0 copy-start.2
  25.3 1.0 %copy-done.2 = bf16[2,8,128,128]{3,2,1,0:T(8,128)(2,1)S(1)} copy-done((bf16[2,8,128,128]{3,2,1,0:T(8,128)(2,1)S(1)}, bf16[2,8,128,128]{3,2,1,0:T(8,128)(2,1)}, u32[]{:S(2)}) %copy-start.2) | copy-done | bytes 524312
  26.4 1.1 %copy-done.4 = bf16[2,3,3,128,128]{4,3,2,1,0:T(8,128)(2,1)S(1)} copy-done((bf16[2,3,3,128,128]{4,3,2,1,0:T(8,128)(2,1)S(1)}, bf16[2,3,3,128,128]{4,3,2,1,0:T(8,128)(2,1)}, u32[]{:S(2)}) %copy-start.4) | copy-done | bytes 589848
  27.4 0.0 copy-start.6
  27.4 0.9 %copy-done.6 = bf16[2,3,128,128]{3,2,1,0:T(8,128)(2,1)S(1)} copy-done((bf16[2,3,128,128]{3,2,1,0:T(8,128)(2,1)S(1)}, bf16[2,3,128,128]{3,2,1,0:T(8,128)(2,1)}, u32[]{:S(2)}) %copy-start.6) | copy-done | bytes 196632
  28.4 8.3 %decoder_step.1 = (bf16[2,8,128,128]{3,2,1,0:T(8,128)(2,1)}, bf16[1152,128]{1,0:T(8,128)(2,1)S(1)}, bf16[1152,128]{1,0:T(8,128)(2,1)S(1)}, f32[2,2,256]{2,1,0:T(2,128)S(1)}) custom-call(s32[2]{0:T(128)S(1)} %copy-done.3, bf16[8,8,128,128]{3,2,1,0:T(8,128)(2,1)S(1)} %copy-done.1, bf16[2,3,128,128]{3,2,1,0:T(8,128)(2,1)S(1)} %collective-permute-done.low, ...), custom_call_target="tpu_custom_call" | custom-call | flops 3623878656 | bytes 8388608 | tf_op jit(solution)/shard_map/decoder_step/pallas_call | solution.py:180
  36.7 0.1 collective-permute-start.10
  36.7 0.5 collective-permute-start.16
  37.2 0.9 %collective-permute-done.16 = f32[2,2,256]{2,1,0:T(2,128)S(1)} collective-permute-done((f32[2,2,256]{2,1,0:T(2,128)S(1)}, f32[2,2,256]{2,1,0:T(2,128)S(1)}, u32[]{:S(2)}, u32[]{:S(2)}) %collective-permute-start.16) | collective-permute-done | bytes 4128 | tf_op jit(solution)/shard_map/ppermute | solution.py:215
  38.1 0.0 collective-permute-start.17
  38.2 3.5 %collective-permute-done.17 = f32[2,2,256]{2,1,0:T(2,128)S(1)} collective-permute-done((f32[2,2,256]{2,1,0:T(2,128)S(1)}, f32[2,2,256]{2,1,0:T(2,128)S(1)}, u32[]{:S(2)}, u32[]{:S(2)}) %collective-permute-start.17) | collective-permute-done | bytes 4128 | tf_op jit(solution)/shard_map/ppermute | solution.py:215
  41.7 0.0 collective-permute-start.18
  41.8 0.1 collective-permute-start.4
  41.8 3.5 %collective-permute-done.18 = f32[2,2,256]{2,1,0:T(2,128)S(1)} collective-permute-done((f32[2,2,256]{2,1,0:T(2,128)S(1)}, f32[2,2,256]{2,1,0:T(2,128)S(1)}, u32[]{:S(2)}, u32[]{:S(2)}) %collective-permute-start.18) | collective-permute-done | bytes 4128 | tf_op jit(solution)/shard_map/ppermute | solution.py:215
  45.3 0.0 collective-permute-start.19
  45.3 0.0 collective-permute-done.10
  45.4 0.1 collective-permute-start.11
  45.5 0.0 collective-permute-done.4
  45.6 1.9 %collective-permute-start.5 = (bf16[288,128]{1,0:T(8,128)(2,1)S(1)}, bf16[288,128]{1,0:T(8,128)(2,1)S(1)}, u32[]{:S(2)}, u32[]{:S(2)}) collective-permute-start(bf16[288,128]{1,0:T(8,128)(2,1)S(1)} %constant_dynamic-slice_fusion.2), channel_id=1, source_target_pairs={{0,4},{1,5},{2,6},{3,7},{4,0},{5,1},{6,2},{7,3},{8,12},{9,13},{10,... | collective-permute-start | bytes 221192 | tf_op jit(solution)/shard_map/ppermute | solution.py:215
  47.5 2.4 %collective-permute-done.11 = bf16[288,128]{1,0:T(8,128)(2,1)S(1)} collective-permute-done((bf16[288,128]{1,0:T(8,128)(2,1)S(1)}, bf16[288,128]{1,0:T(8,128)(2,1)S(1)}, u32[]{:S(2)}, u32[]{:S(2)}) %collective-permute-start.11) | collective-permute-done | bytes 73760 | tf_op jit(solution)/shard_map/ppermute | solution.py:215
  49.9 1.1 %collective-permute-start.12 = (bf16[288,128]{1,0:T(8,128)(2,1)S(1)}, bf16[288,128]{1,0:T(8,128)(2,1)S(1)}, u32[]{:S(2)}, u32[]{:S(2)}) collective-permute-start(bf16[288,128]{1,0:T(8,128)(2,1)S(1)} %add_convert_fusion.4), channel_id=1, source_target_pairs={{0,4},{1,5},{2,6},{3,7},{4,0},{5,1},{6,2},{7,3},{8,12},{9,13},{10,... | collective-permute-start | bytes 221192 | tf_op jit(solution)/shard_map/ppermute | solution.py:215
  50.9 0.0 collective-permute-done.5
  51.0 1.2 %collective-permute-start.6 = (bf16[288,128]{1,0:T(8,128)(2,1)S(1)}, bf16[288,128]{1,0:T(8,128)(2,1)S(1)}, u32[]{:S(2)}, u32[]{:S(2)}) collective-permute-start(bf16[288,128]{1,0:T(8,128)(2,1)S(1)} %add_convert_fusion.7), channel_id=1, source_target_pairs={{0,2},{1,3},{2,0},{3,1},{4,6},{5,7},{6,4},{7,5},{8,10},{9,11},{10,... | collective-permute-start | bytes 221192 | tf_op jit(solution)/shard_map/ppermute | solution.py:215
  52.1 2.2 %collective-permute-done.12 = bf16[288,128]{1,0:T(8,128)(2,1)S(1)} collective-permute-done((bf16[288,128]{1,0:T(8,128)(2,1)S(1)}, bf16[288,128]{1,0:T(8,128)(2,1)S(1)}, u32[]{:S(2)}, u32[]{:S(2)}) %collective-permute-start.12) | collective-permute-done | bytes 73760 | tf_op jit(solution)/shard_map/ppermute | solution.py:215
  54.3 3.3 %collective-permute-start.13 = (bf16[288,128]{1,0:T(8,128)(2,1)S(1)}, bf16[288,128]{1,0:T(8,128)(2,1)S(1)}, u32[]{:S(2)}, u32[]{:S(2)}) collective-permute-start(bf16[288,128]{1,0:T(8,128)(2,1)S(1)} %add_convert_fusion.3), channel_id=1, source_target_pairs={{0,8},{1,9},{2,10},{3,11},{4,12},{5,13},{6,14},{7,15},{8,0},{9,1},... | collective-permute-start | bytes 221192 | tf_op jit(solution)/shard_map/ppermute | solution.py:215
  57.6 0.0 collective-permute-done.6
  57.6 0.4 collective-permute-start.7
  58.1 2.7 %collective-permute-done.13 = bf16[288,128]{1,0:T(8,128)(2,1)S(1)} collective-permute-done((bf16[288,128]{1,0:T(8,128)(2,1)S(1)}, bf16[288,128]{1,0:T(8,128)(2,1)S(1)}, u32[]{:S(2)}, u32[]{:S(2)}) %collective-permute-start.13) | collective-permute-done | bytes 73760 | tf_op jit(solution)/shard_map/ppermute | solution.py:215
  60.8 0.1 collective-permute-start.14
  60.8 2.4 %collective-permute-done.7 = bf16[288,128]{1,0:T(8,128)(2,1)S(1)} collective-permute-done((bf16[288,128]{1,0:T(8,128)(2,1)S(1)}, bf16[288,128]{1,0:T(8,128)(2,1)S(1)}, u32[]{:S(2)}, u32[]{:S(2)}) %collective-permute-start.7) | collective-permute-done | bytes 73760 | tf_op jit(solution)/shard_map/ppermute | solution.py:215
  63.3 0.1 collective-permute-start.8
  63.4 1.8 %collective-permute-done.14 = bf16[288,128]{1,0:T(8,128)(2,1)S(1)} collective-permute-done((bf16[288,128]{1,0:T(8,128)(2,1)S(1)}, bf16[288,128]{1,0:T(8,128)(2,1)S(1)}, u32[]{:S(2)}, u32[]{:S(2)}) %collective-permute-start.14) | collective-permute-done | bytes 73760 | tf_op jit(solution)/shard_map/ppermute | solution.py:215
  65.2 0.1 collective-permute-start.15
  65.3 2.4 %collective-permute-done.8 = bf16[288,128]{1,0:T(8,128)(2,1)S(1)} collective-permute-done((bf16[288,128]{1,0:T(8,128)(2,1)S(1)}, bf16[288,128]{1,0:T(8,128)(2,1)S(1)}, u32[]{:S(2)}, u32[]{:S(2)}) %collective-permute-start.8) | collective-permute-done | bytes 73760 | tf_op jit(solution)/shard_map/ppermute | solution.py:215
  67.8 0.1 collective-permute-start.9
  67.8 0.0 collective-permute-done.19
  67.8 0.6 convolution_bitcast_fusion
  68.5 1.0 %copy.10 = f32[2,256,256]{2,1,0:T(8,128)} copy(f32[2,256,256]{1,2,0:T(8,128)S(1)} %convolution_bitcast_fusion) | data formatting | bytes 1048576
  69.5 0.0 collective-permute-done.15
  69.5 0.0 collective-permute-done.9
  69.5 0.1 broadcast_select_fusion.1
  69.7 1.1 %maximum_convert_fusion = f32[2,3,3,128,128]{4,3,2,1,0:T(8,128)} fusion(bf16[1,3,3,128,128]{4,3,2,1,0:T(8,128)(2,1)S(1)} %bitcast.15, bf16[1,3,3,128,128]{4,3,2,1,0:T(8,128)(2,1)S(1)} %bitcast.16), kind=kLoop, calls=%fused_computation.2 | loop fusion | flops 589824 | bytes 1769472 | tf_op jit(solution)/shard_map/convert_element_type | solution.py:285
  (24 shorter events, 0.5 us)
Async XLA Ops:
  0.6 23.6 %copy-start = (f32[2,256,256]{2,1,0:T(8,128)S(1)}, f32[2,256,256]{2,1,0:T(8,128)}, u32[]{:S(2)}) copy-start(f32[2,256,256]{2,1,0:T(8,128)} %param.11) | copy-start | bytes 1572868
  0.6 24.7 %copy-start.3 = (s32[2]{0:T(128)S(1)}, s32[2]{0:T(128)}, u32[]{:S(2)}) copy-start(s32[2]{0:T(128)} %identity.1) | copy-start | bytes 28
  0.7 24.7 %copy-start.1 = (bf16[8,8,128,128]{3,2,1,0:T(8,128)(2,1)S(1)}, bf16[8,8,128,128]{3,2,1,0:T(8,128)(2,1)}, u32[]{:S(2)}) copy-start(bf16[8,8,128,128]{3,2,1,0:T(8,128)(2,1)} %maps.1) | copy-start | bytes 6291460
  7.1 17.6 %collective-permute-start = (bf16[2,3,128,128]{3,2,1,0:T(8,128)(2,1)S(1)}, bf16[2,3,128,128]{3,2,1,0:T(8,128)(2,1)S(1)}, u32[]{:S(2)}, u32[]{:S(2)}) collective-permute-start(bf16[2,3,128,128]{3,2,1,0:T(8,128)(2,1)S(1)} %pad_maximum_fusion.2), channel_id=1, source_target_pairs={{0,1},{1,2},{2,3},{3,4},{4,5},{5,6},{6,7},{7,8},{8,9},{9,10},{10,1... | collective-permute-start | bytes 589832 | tf_op jit(solution)/shard_map/ppermute | solution.py:272
  7.6 17.0 %collective-permute-start.1 = (bf16[2,3,128,128]{3,2,1,0:T(8,128)(2,1)S(1)}, bf16[2,3,128,128]{3,2,1,0:T(8,128)(2,1)S(1)}, u32[]{:S(2)}, u32[]{:S(2)}) collective-permute-start(bf16[2,3,128,128]{3,2,1,0:T(8,128)(2,1)S(1)} %pad_maximum_fusion.3), channel_id=1, source_target_pairs={{0,15},{1,0},{2,1},{3,2},{4,3},{5,4},{6,5},{7,6},{8,7},{9,8},{10,9... | collective-permute-start | bytes 589832 | tf_op jit(solution)/shard_map/ppermute | solution.py:273
  14.2 10.5 %collective-permute-start.2 = (bf16[2,1,128,128]{3,2,1,0:T(8,128)(2,1)}, bf16[2,1,128,128]{3,2,1,0:T(8,128)(2,1)S(1)}, u32[]{:S(2)}, u32[]{:S(2)}) collective-permute-start(bf16[2,1,128,128]{3,2,1,0:T(8,128)(2,1)} %get-tuple-element.19), channel_id=1, source_target_pairs={{0,1},{1,2},{2,3},{3,4},{4,5},{5,6},{6,7},{7,8},{8,9},{9,10},{10,1... | collective-permute-start | bytes 196616 | tf_op jit(solution)/shard_map/ppermute | solution.py:274
  14.2 10.5 %collective-permute-start.3 = (bf16[2,1,128,128]{3,2,1,0:T(8,128)(2,1)}, bf16[2,1,128,128]{3,2,1,0:T(8,128)(2,1)S(1)}, u32[]{:S(2)}, u32[]{:S(2)}) collective-permute-start(bf16[2,1,128,128]{3,2,1,0:T(8,128)(2,1)} %get-tuple-element.18), channel_id=1, source_target_pairs={{0,15},{1,0},{2,1},{3,2},{4,3},{5,4},{6,5},{7,6},{8,7},{9,8},{10,9... | collective-permute-start | bytes 196616 | tf_op jit(solution)/shard_map/ppermute | solution.py:275
  24.6 0.7 copy-start.5
  25.3 1.0 %copy-start.2 = (bf16[2,8,128,128]{3,2,1,0:T(8,128)(2,1)S(1)}, bf16[2,8,128,128]{3,2,1,0:T(8,128)(2,1)}, u32[]{:S(2)}) copy-start(bf16[2,8,128,128]{3,2,1,0:T(8,128)(2,1)} %dout.1) | copy-start | bytes 1572868
  26.4 1.1 %copy-start.4 = (bf16[2,3,3,128,128]{4,3,2,1,0:T(8,128)(2,1)S(1)}, bf16[2,3,3,128,128]{4,3,2,1,0:T(8,128)(2,1)}, u32[]{:S(2)}) copy-start(bf16[2,3,3,128,128]{4,3,2,1,0:T(8,128)(2,1)} %weights.1) | copy-start | bytes 1769476
  27.4 0.9 %copy-start.6 = (bf16[2,3,128,128]{3,2,1,0:T(8,128)(2,1)S(1)}, bf16[2,3,128,128]{3,2,1,0:T(8,128)(2,1)}, u32[]{:S(2)}) copy-start(bf16[2,3,128,128]{3,2,1,0:T(8,128)(2,1)} %copy-done.5) | copy-start | bytes 589828
  36.7 8.7 %collective-permute-start.10 = (bf16[576,128]{1,0:T(8,128)(2,1)S(1)}, bf16[576,128]{1,0:T(8,128)(2,1)S(1)}, u32[]{:S(2)}, u32[]{:S(2)}) collective-permute-start(bf16[576,128]{1,0:T(8,128)(2,1)S(1)} %constant_dynamic-slice_fusion.1), channel_id=1, source_target_pairs={{0,1},{1,0},{2,3},{3,2},{4,5},{5,4},{6,7},{7,6},{8,9},{9,8},{10,11... | collective-permute-start | bytes 442376 | tf_op jit(solution)/shard_map/ppermute | solution.py:215
  36.7 1.4 %collective-permute-start.16 = (f32[2,2,256]{2,1,0:T(2,128)S(1)}, f32[2,2,256]{2,1,0:T(2,128)S(1)}, u32[]{:S(2)}, u32[]{:S(2)}) collective-permute-start(f32[2,2,256]{2,1,0:T(2,128)S(1)} %get-tuple-element.10), channel_id=1, source_target_pairs={{0,1},{1,0},{2,3},{3,2},{4,5},{5,4},{6,7},{7,6},{8,9},{9,8},{10,11... | collective-permute-start | bytes 12296 | tf_op jit(solution)/shard_map/ppermute | solution.py:215
  38.1 3.6 %collective-permute-start.17 = (f32[2,2,256]{2,1,0:T(2,128)S(1)}, f32[2,2,256]{2,1,0:T(2,128)S(1)}, u32[]{:S(2)}, u32[]{:S(2)}) collective-permute-start(f32[2,2,256]{2,1,0:T(2,128)S(1)} %add.109), channel_id=1, source_target_pairs={{0,4},{1,5},{2,6},{3,7},{4,0},{5,1},{6,2},{7,3},{8,12},{9,13},{10,... | collective-permute-start | bytes 12296 | tf_op jit(solution)/shard_map/ppermute | solution.py:215
  41.7 3.6 %collective-permute-start.18 = (f32[2,2,256]{2,1,0:T(2,128)S(1)}, f32[2,2,256]{2,1,0:T(2,128)S(1)}, u32[]{:S(2)}, u32[]{:S(2)}) collective-permute-start(f32[2,2,256]{2,1,0:T(2,128)S(1)} %add.110), channel_id=1, source_target_pairs={{0,2},{1,3},{2,0},{3,1},{4,6},{5,7},{6,4},{7,5},{8,10},{9,11},{10,... | collective-permute-start | bytes 12296 | tf_op jit(solution)/shard_map/ppermute | solution.py:215
  41.8 3.8 %collective-permute-start.4 = (bf16[576,128]{1,0:T(8,128)(2,1)S(1)}, bf16[576,128]{1,0:T(8,128)(2,1)S(1)}, u32[]{:S(2)}, u32[]{:S(2)}) collective-permute-start(bf16[576,128]{1,0:T(8,128)(2,1)S(1)} %constant_dynamic-slice_fusion.3), channel_id=1, source_target_pairs={{0,1},{1,0},{2,3},{3,2},{4,5},{5,4},{6,7},{7,6},{8,9},{9,8},{10,11... | collective-permute-start | bytes 442376 | tf_op jit(solution)/shard_map/ppermute | solution.py:215
  45.3 22.5 %collective-permute-start.19 = (f32[2,2,256]{2,1,0:T(2,128)S(1)}, f32[2,2,256]{2,1,0:T(2,128)S(1)}, u32[]{:S(2)}, u32[]{:S(2)}) collective-permute-start(f32[2,2,256]{2,1,0:T(2,128)S(1)} %add.111), channel_id=1, source_target_pairs={{0,8},{1,9},{2,10},{3,11},{4,12},{5,13},{6,14},{7,15},{8,0},{9,1},... | collective-permute-start | bytes 12296 | tf_op jit(solution)/shard_map/ppermute | solution.py:215
  45.4 4.4 %collective-permute-start.11 = (bf16[288,128]{1,0:T(8,128)(2,1)S(1)}, bf16[288,128]{1,0:T(8,128)(2,1)S(1)}, u32[]{:S(2)}, u32[]{:S(2)}) collective-permute-start(bf16[288,128]{1,0:T(8,128)(2,1)S(1)} %constant_dynamic-slice_fusion), channel_id=1, source_target_pairs={{0,2},{1,3},{2,0},{3,1},{4,6},{5,7},{6,4},{7,5},{8,10},{9,11},{10,... | collective-permute-start | bytes 221192 | tf_op jit(solution)/shard_map/ppermute | solution.py:215
  45.6 5.3 %collective-permute-start.5 = (bf16[288,128]{1,0:T(8,128)(2,1)S(1)}, bf16[288,128]{1,0:T(8,128)(2,1)S(1)}, u32[]{:S(2)}, u32[]{:S(2)}) collective-permute-start(bf16[288,128]{1,0:T(8,128)(2,1)S(1)} %constant_dynamic-slice_fusion.2), channel_id=1, source_target_pairs={{0,4},{1,5},{2,6},{3,7},{4,0},{5,1},{6,2},{7,3},{8,12},{9,13},{10,... | collective-permute-start | bytes 221192 | tf_op jit(solution)/shard_map/ppermute | solution.py:215
  49.9 4.4 %collective-permute-start.12 = (bf16[288,128]{1,0:T(8,128)(2,1)S(1)}, bf16[288,128]{1,0:T(8,128)(2,1)S(1)}, u32[]{:S(2)}, u32[]{:S(2)}) collective-permute-start(bf16[288,128]{1,0:T(8,128)(2,1)S(1)} %add_convert_fusion.4), channel_id=1, source_target_pairs={{0,4},{1,5},{2,6},{3,7},{4,0},{5,1},{6,2},{7,3},{8,12},{9,13},{10,... | collective-permute-start | bytes 221192 | tf_op jit(solution)/shard_map/ppermute | solution.py:215
  51.0 6.6 %collective-permute-start.6 = (bf16[288,128]{1,0:T(8,128)(2,1)S(1)}, bf16[288,128]{1,0:T(8,128)(2,1)S(1)}, u32[]{:S(2)}, u32[]{:S(2)}) collective-permute-start(bf16[288,128]{1,0:T(8,128)(2,1)S(1)} %add_convert_fusion.7), channel_id=1, source_target_pairs={{0,2},{1,3},{2,0},{3,1},{4,6},{5,7},{6,4},{7,5},{8,10},{9,11},{10,... | collective-permute-start | bytes 221192 | tf_op jit(solution)/shard_map/ppermute | solution.py:215
  54.3 6.4 %collective-permute-start.13 = (bf16[288,128]{1,0:T(8,128)(2,1)S(1)}, bf16[288,128]{1,0:T(8,128)(2,1)S(1)}, u32[]{:S(2)}, u32[]{:S(2)}) collective-permute-start(bf16[288,128]{1,0:T(8,128)(2,1)S(1)} %add_convert_fusion.3), channel_id=1, source_target_pairs={{0,8},{1,9},{2,10},{3,11},{4,12},{5,13},{6,14},{7,15},{8,0},{9,1},... | collective-permute-start | bytes 221192 | tf_op jit(solution)/shard_map/ppermute | solution.py:215
  57.6 5.6 %collective-permute-start.7 = (bf16[288,128]{1,0:T(8,128)(2,1)S(1)}, bf16[288,128]{1,0:T(8,128)(2,1)S(1)}, u32[]{:S(2)}, u32[]{:S(2)}) collective-permute-start(bf16[288,128]{1,0:T(8,128)(2,1)S(1)} %add_convert_fusion.6), channel_id=1, source_target_pairs={{0,8},{1,9},{2,10},{3,11},{4,12},{5,13},{6,14},{7,15},{8,0},{9,1},... | collective-permute-start | bytes 221192 | tf_op jit(solution)/shard_map/ppermute | solution.py:215
  60.8 4.4 %collective-permute-start.14 = (bf16[288,128]{1,0:T(8,128)(2,1)S(1)}, bf16[288,128]{1,0:T(8,128)(2,1)S(1)}, u32[]{:S(2)}, u32[]{:S(2)}) collective-permute-start(bf16[288,128]{1,0:T(8,128)(2,1)S(1)} %add_convert_fusion.2), channel_id=1, source_target_pairs={{0,2},{1,3},{2,0},{3,1},{4,6},{5,7},{6,4},{7,5},{8,10},{9,11},{10,... | collective-permute-start | bytes 221192 | tf_op jit(solution)/shard_map/ppermute | solution.py:215
  63.3 4.4 %collective-permute-start.8 = (bf16[288,128]{1,0:T(8,128)(2,1)S(1)}, bf16[288,128]{1,0:T(8,128)(2,1)S(1)}, u32[]{:S(2)}, u32[]{:S(2)}) collective-permute-start(bf16[288,128]{1,0:T(8,128)(2,1)S(1)} %add_convert_fusion.5), channel_id=1, source_target_pairs={{0,4},{1,5},{2,6},{3,7},{4,0},{5,1},{6,2},{7,3},{8,12},{9,13},{10,... | collective-permute-start | bytes 221192 | tf_op jit(solution)/shard_map/ppermute | solution.py:215
  65.2 4.3 %collective-permute-start.15 = (bf16[576,128]{1,0:T(8,128)(2,1)S(1)}, bf16[576,128]{1,0:T(8,128)(2,1)S(1)}, u32[]{:S(2)}, u32[]{:S(2)}) collective-permute-start(bf16[576,128]{1,0:T(8,128)(2,1)S(1)} %pad_maximum_fusion.5), channel_id=1, source_target_pairs={{0,1},{1,0},{2,3},{3,2},{4,5},{5,4},{6,7},{7,6},{8,9},{9,8},{10,11... | collective-permute-start | bytes 442376 | tf_op jit(solution)/shard_map/ppermute | solution.py:215
  67.8 1.7 %collective-permute-start.9 = (bf16[576,128]{1,0:T(8,128)(2,1)S(1)}, bf16[576,128]{1,0:T(8,128)(2,1)S(1)}, u32[]{:S(2)}, u32[]{:S(2)}) collective-permute-start(bf16[576,128]{1,0:T(8,128)(2,1)S(1)} %pad_maximum_fusion.4), channel_id=1, source_target_pairs={{0,1},{1,0},{2,3},{3,2},{4,5},{5,4},{6,7},{7,6},{8,9},{9,8},{10,11... | collective-permute-start | bytes 442376 | tf_op jit(solution)/shard_map/ppermute | solution.py:215

commit v2 on v0

v2 whole, which is shorter than its diff:
```python
import functools
import math

import jax
import jax.numpy as jnp
from jax import lax
from jax.experimental import pallas as pl
from jax.experimental.pallas import tpu as pltpu
from jax.sharding import PartitionSpec as P

AXIS = "lon"
RIM = 3
F32 = jnp.float32
BF16 = jnp.bfloat16
VMEM = pl.BlockSpec(memory_space=pltpu.VMEM)
SMEM = pl.BlockSpec(memory_space=pltpu.SMEM)
HBM = pl.BlockSpec(memory_space=pltpu.HBM)
ANY = pl.BlockSpec(memory_space=pl.ANY)


def parts_of(items, size):
    items = list(items)
    return [items[i : i + size] for i in range(0, len(items), size)]


def flat(values):
    return values.reshape(-1, values.shape[-1])


def shift_stack(values, rows):
    total = values.shape[0]
    place = lax.broadcasted_iota(jnp.int32, values.shape, 0) % rows
    above = jnp.where(place == 0, 0.0, pltpu.roll(values, 1, 0))
    below = jnp.where(place == rows - 1, 0.0, pltpu.roll(values, total - 1, 0))
    return jnp.concatenate([above.astype(BF16), values.astype(BF16), below.astype(BF16)], axis=1)


class Columns:
    def __init__(self, *pieces):
        self.place = {}
        for ref, columns in pieces:
            for i, column in enumerate(columns):
                self.place[column] = (ref, i)

    def get(self, f, column):
        ref, i = self.place[column]
        return ref[f, i]

    def put(self, f, columns, values, rows):
        for n, column in enumerate(columns):
            ref, i = self.place[column]
            ref[f, i] = values[n * rows : (n + 1) * rows]

    def rows_of(self, f, columns):
        blocks = [self.get(f, column) for column in columns]
        return blocks[0] if len(blocks) == 1 else jnp.concatenate(blocks, axis=0)

    def windows(self, f, columns):
        return jnp.concatenate(
            [self.rows_of(f, [column + a - 1 for column in columns]) for a in range(3)], axis=1
        )


def film_of(film, layer, f):
    channels = film.shape[2] // 2
    return 1.0 + film[layer, f : f + 1, :channels], film[layer, f : f + 1, channels:]


def forward_0(film, weights, h_0, h_1, pre_0, f, columns, rows):
    gain, offset = film_of(film, 0, f)
    weight = weights[0].reshape(-1, weights.shape[-1])
    pre = jnp.dot(h_0.windows(f, columns), weight, preferred_element_type=F32)
    mod = pre * gain + offset
    h_1.put(f, columns, shift_stack(mod * jax.nn.sigmoid(mod), rows), rows)
    for n, column in enumerate(columns):
        if column in pre_0.place:
            pre_0.put(f, [column], pre[n * rows : (n + 1) * rows], rows)


def both_1(factor, film, weights, h_1, dout, decoded, d_1, f, columns, rows):
    gain, offset = film_of(film, 1, f)
    weight = weights[1].reshape(-1, weights.shape[-1])
    pre = jnp.dot(h_1.windows(f, columns), weight, preferred_element_type=F32)
    mod = pre * gain + offset
    gate = jax.nn.sigmoid(mod)
    hidden = (mod * gate).astype(BF16)
    for n, column in enumerate(columns):
        if column in decoded.place:
            decoded.put(f, [column], hidden[n * rows : (n + 1) * rows], rows)
    grad = dout.rows_of(f, columns).astype(F32) * factor
    grad_mod = grad * (gate * (1.0 + mod * (1.0 - gate)))
    grad_pre = grad_mod * gain
    d_1.put(f, columns, shift_stack(grad_pre, rows), rows)
    return grad_pre, grad_mod, pre


def back_0(film, weights, d_1, pre_0, f, columns):
    gain, offset = film_of(film, 0, f)
    flipped = jnp.concatenate(
        [weights[1, 2 - a, 2 - b] for a in range(3) for b in range(3)], axis=1
    )
    grad = lax.dot_general(
        d_1.windows(f, columns), flipped, (((1,), (1,)), ((), ())), preferred_element_type=F32
    )
    pre = pre_0.rows_of(f, columns)
    mod = pre * gain + offset
    gate = jax.nn.sigmoid(mod)
    grad_mod = grad * (gate * (1.0 + mod * (1.0 - gate)))
    return grad_mod * gain, grad_mod, pre


class Sums:
    def __init__(self):
        self.stats = {}
        self.turned = []

    def add(self, f, columns, rows, grad_pre, grad_mod, pre):
        product = jnp.sum(grad_mod * pre, axis=0, keepdims=True)
        plain = jnp.sum(grad_mod, axis=0, keepdims=True)
        if f in self.stats:
            before = self.stats[f]
            self.stats[f] = (before[0] + product, before[1] + plain)
        else:
            self.stats[f] = (product, plain)
        self.turned.append((f, columns, grad_pre.T.astype(BF16)))

    def taps(self, field, a):
        total = None
        for f, columns, turned in self.turned:
            window = field.rows_of(f, [column + a - 1 for column in columns])
            term = jnp.dot(turned, window, preferred_element_type=F32)
            total = term if total is None else total + term
        return total

    def rows_of_stats(self):
        return jnp.concatenate([row for f in sorted(self.stats) for row in self.stats[f]], axis=0)


def put_message(mine, totals, stats, whole, keep, send):
    size = totals[0].shape[1]
    half = 3 * size // 2
    for a in range(3):
        whole[a * size : (a + 1) * size, :] = totals[a].T
    low, high = whole[:half, :], whole[half:, :]
    keep[:half, :] = jnp.where(mine == 0, low, high)
    send[:half, :] = jnp.where(mine == 0, high, low)
    tail = keep.shape[0] - half
    padded = jnp.concatenate([stats, jnp.zeros((tail - stats.shape[0], stats.shape[1]), F32)], axis=0)
    keep[half:, :] = padded
    send[half:, :] = padded


def edge_kernel(identity, maps, dout, outer, inner, sems):
    frames, columns = dout.shape[:2]
    mine = lax.rem(lax.axis_index(AXIS), 2)
    copies = []
    for side, out in enumerate((outer, inner)):
        at_end = mine if side == 0 else 1 - mine
        for f in range(frames):
            source = maps.at[identity[f], pl.ds(at_end * (columns - RIM), RIM)]
            copies.append(
                pltpu.make_async_copy(source, out.at[f, pl.ds(0, RIM)], sems.at[side, f, 0])
            )
            source = dout.at[f, pl.ds(at_end * (columns - 1), 1)]
            copies.append(
                pltpu.make_async_copy(source, out.at[f, pl.ds(RIM, 1)], sems.at[side, f, 1])
            )
    for copy in copies:
        copy.start()
    for copy in copies:
        copy.wait()


def inner_kernel(
    factor,
    identity,
    audio_index,
    maps,
    audio,
    film_w,
    weights,
    dout,
    film,
    audio_rows,
    stack_0,
    stack_1,
    stack_d,
    pre_0,
    decoded,
    taps_0,
    taps_1,
    stats,
    first,
    sems,
):
    frames, columns, rows = first.shape[:3]
    copies = []
    for f in range(frames):
        copies.append(pltpu.make_async_copy(maps.at[identity[f]], first.at[f], sems.at[f]))
    for copy in copies:
        copy.start()
    for f in range(frames):
        audio_rows[f : f + 1, :] = audio[pl.ds(audio_index[f], 1), :]
    for layer in range(film.shape[0]):
        film[layer] = jnp.dot(
            audio_rows[...],
            film_w[layer],
            precision=lax.Precision.HIGHEST,
            preferred_element_type=F32,
        )

    h_0 = Columns((stack_0, range(columns)))
    h_1 = Columns((stack_1, range(1, columns - 1)))
    d_1 = Columns((stack_d, range(2, columns - 2)))
    saved = Columns((pre_0, range(1, columns - 1)))
    out = Columns((decoded, range(2, columns - 2)))
    grads = Columns((dout, range(columns)))

    for f in range(frames):
        copies[f].wait()
        for some in parts_of(range(columns), 4):
            values = flat(first[f, some[0] : some[-1] + 1]).astype(F32)
            h_0.put(f, some, shift_stack(values, rows), rows)

    for f in range(frames):
        for some in parts_of(range(1, columns - 1), 3):
            forward_0(film, weights, h_0, h_1, saved, f, some, rows)
    sums_1, sums_0 = Sums(), Sums()
    for f in range(frames):
        some = list(range(2, columns - 2))
        sums_1.add(
            f, some, rows, *both_1(factor, film, weights, h_1, grads, out, d_1, f, some, rows)
        )
    for f in range(frames):
        some = list(range(3, columns - 3))
        sums_0.add(f, some, rows, *back_0(film, weights, d_1, saved, f, some))
    for a in range(3):
        taps_1[a] = sums_1.taps(h_1, a)
        taps_0[a] = sums_0.taps(h_0, a)
    stats[0] = sums_0.rows_of_stats()
    stats[1] = sums_1.rows_of_stats()


def rim_kernel(
    factor,
    outer,
    inner,
    dout,
    weights,
    film,
    stack_0,
    stack_1,
    decoded_a,
    taps_a,
    stats_a,
    decoded,
    rim_0,
    rim_d,
    rim_pre,
    keep,
    send,
    rim_1,
    hidden,
    whole,
    sems,
):
    frames, columns, rows = dout.shape[:3]
    mine = lax.rem(lax.axis_index(AXIS), 2)
    done = pltpu.make_async_copy(decoded_a, decoded.at[:, pl.ds(2, columns - 4)], sems.at[0])
    done.start()
    last = columns - 1
    h_0 = Columns(
        (stack_0, range(columns)), (rim_0, [-3, -2, -1, last + 1, last + 2, last + 3])
    )
    h_1 = Columns(
        (stack_1, range(1, last)), (rim_1, [-2, -1, 0, last, last + 1, last + 2])
    )
    d_1 = Columns((rim_d, [-1, 0, 1, last - 1, last, last + 1]))
    saved = Columns((rim_pre, [0, last]))
    out = Columns((hidden, [0, 1, last - 1, last]))
    grads = Columns((dout, range(columns)))

    def received(f, item, high):
        side = mine if high else 1 - mine
        return jnp.where(side == 0, inner[f, item].astype(F32), outer[f, item].astype(F32))

    class Edges(Columns):
        def get(self, f, column):
            if column in (-1, columns):
                return received(f, RIM, column == columns).astype(BF16)
            return grads.get(f, column)

    for f in range(frames):
        for n in range(RIM):
            low = received(f, n, False)
            h_0.put(f, [n - RIM], shift_stack(low, rows), rows)
            high = received(f, n, True)
            h_0.put(f, [columns + n], shift_stack(high, rows), rows)
    for f in range(frames):
        for some in ([-2, -1, 0], [last, last + 1, last + 2]):
            forward_0(film, weights, h_0, h_1, saved, f, some, rows)
    sums = Sums()
    edges = Edges()
    for f in range(frames):
        both_1(factor, film, weights, h_1, edges, out, d_1, f, [-1, last + 1], rows)
        some = [0, 1, last - 1, last]
        sums.add(f, some, rows, *both_1(factor, film, weights, h_1, edges, out, d_1, f, some, rows))
    ends = [
        pltpu.make_async_copy(
            hidden.at[:, pl.ds(0, 2)], decoded.at[:, pl.ds(0, 2)], sems.at[1]
        ),
        pltpu.make_async_copy(
            hidden.at[:, pl.ds(2, 2)], decoded.at[:, pl.ds(columns - 2, 2)], sems.at[2]
        ),
    ]
    for copy in ends:
        copy.start()
    totals = [taps_a[a] + sums.taps(h_1, a) for a in range(3)]
    put_message(mine, totals, stats_a[1] + sums.rows_of_stats(), whole, keep, send)
    done.wait()
    for copy in ends:
        copy.wait()


def back_kernel(
    weights,
    film,
    stack_0,
    rim_0,
    stack_d,
    rim_d,
    pre_0,
    rim_pre,
    taps_a,
    stats_a,
    keep,
    send,
    whole,
):
    frames, columns, rows = stack_0.shape[:3]
    mine = lax.rem(lax.axis_index(AXIS), 2)
    last = columns - 1
    h_0 = Columns(
        (stack_0, range(columns)), (rim_0, [-3, -2, -1, last + 1, last + 2, last + 3])
    )
    d_1 = Columns(
        (stack_d, range(2, columns - 2)), (rim_d, [-1, 0, 1, last - 1, last, last + 1])
    )
    saved = Columns((pre_0, range(1, last)), (rim_pre, [0, last]))
    sums = Sums()
    for f in range(frames):
        some = [0, 1, 2, last - 2, last - 1, last]
        sums.add(f, some, rows, *back_0(film, weights, d_1, saved, f, some))
    totals = [taps_a[a] + sums.taps(h_0, a) for a in range(3)]
    put_message(mine, totals, stats_a[0] + sums.rows_of_stats(), whole, keep, send)


def call(kernel, name, ins, outs, args, scratch=(), flops=0, out_specs=None, room=36):
    return pl.pallas_call(
        kernel,
        out_shape=tuple(jax.ShapeDtypeStruct(shape, dtype) for shape, dtype in outs),
        in_specs=ins,
        out_specs=tuple(out_specs) if out_specs else (VMEM,) * len(outs),
        scratch_shapes=list(scratch),
        compiler_params=pltpu.CompilerParams(vmem_limit_bytes=room << 20),
        cost_estimate=pl.CostEstimate(flops=flops, transcendentals=0, bytes_accessed=4 << 20),
        name=name,
    )(*args)


def swap(value, bit):
    count = lax.axis_size(AXIS)
    return lax.ppermute(value, AXIS, [(i, i ^ bit) for i in range(count)])


def mine_of(bit):
    return (lax.axis_index(AXIS) // bit) % 2


def rounded(value):
    return lax.reduce_precision(value, 8, 7)


def exchange(taps, stats, bit, split):
    high = rounded(stats)
    low = rounded(stats - high)
    if split:
        half = taps.shape[0] // 2
        mine = mine_of(bit)
        keep = lax.dynamic_slice_in_dim(taps, mine * half, half, 0)
        send = lax.dynamic_slice_in_dim(taps, (1 - mine) * half, half, 0)
    else:
        keep = send = rounded(taps)
    message = jnp.concatenate([send.astype(BF16), high.astype(BF16), low.astype(BF16)], axis=0)
    other = swap(message, bit).astype(F32)
    size, tail = send.shape[0], stats.shape[0]
    stats = (high + low) + (other[size : size + tail] + other[size + tail :])
    return keep + other[:size], stats


def join(value, bit):
    other = swap(value, bit)
    mine = mine_of(bit)
    return jnp.concatenate(
        [jnp.where(mine == 0, value, other), jnp.where(mine == 0, other, value)], axis=0
    )


def all_sums(messages, half):
    bits = []
    while (2 << len(bits)) < lax.axis_size(AXIS):
        bits.append(2 << len(bits))
    orders = [list(bits), list(bits)]
    if len(bits) > 1:
        orders[1][0], orders[1][1] = bits[1], bits[0]
    if len(bits) > 2:
        orders[0][1], orders[0][2] = bits[2], bits[1]
    state = []
    for keep, send in messages:
        total = keep + swap(send, 1)
        state.append((total[:half], total[half:]))
    for step in range(len(bits)):
        for s in range(2):
            state[s] = exchange(*state[s], orders[s][step], step == 0)
    taps = [value.astype(BF16) for value, _ in state]
    if bits:
        taps = [join(taps[s], orders[s][0]) for s in range(2)]
    taps = [join(value, 1) for value in taps]
    return taps, [stats for _, stats in state]


def local(ident_maps, identity, audio, audio_index, film_w, conv_w, dout):
    frames, columns, rows, channels = dout.shape
    layers = conv_w.shape[0]
    width = film_w.shape[1]
    count = lax.axis_size(AXIS)
    factor = 1.0 / math.sqrt(frames * columns * count * rows)
    unit = 2 * 9 * channels * channels * frames * rows

    edges = ((frames, RIM + 1, rows, channels), BF16)
    outer, inner = call(
        edge_kernel,
        "edges",
        [SMEM, HBM, HBM],
        [edges, edges],
        (identity, ident_maps, dout),
        [pltpu.SemaphoreType.DMA((2, frames, 2))],
        room=57,
    )
    pairs = [(i, (i + 1) % count if i % 2 else (i - 1) % count) for i in range(count)]
    outer = lax.ppermute(outer, AXIS, pairs)
    inner = swap(inner, 1)

    def stack(n):
        return ((frames, n, rows, 3 * channels), BF16)

    taps = ((3, channels, 3 * channels), F32)
    stats = ((layers, 2 * frames, channels), F32)
    (
        film,
        audio_rows,
        stack_0,
        stack_1,
        stack_d,
        pre_0,
        decoded_a,
        taps_0,
        taps_1,
        stats_a,
    ) = call(
        functools.partial(inner_kernel, factor),
        "inner_columns",
        [SMEM, SMEM, HBM] + [VMEM] * 4,
        [
            ((layers, frames, 2 * channels), F32),
            ((frames, width), F32),
            stack(columns),
            stack(columns - 2),
            stack(columns - 4),
            ((frames, columns - 2, rows, channels), F32),
            ((frames, columns - 4, rows, channels), BF16),
            taps,
            taps,
            stats,
        ],
        (identity, audio_index, ident_maps, audio, film_w, conv_w, dout),
        [
            pltpu.VMEM((frames, columns, rows, channels), BF16),
            pltpu.SemaphoreType.DMA((frames,)),
        ],
        18 * unit,
        room=46,
    )
    half = 9 * channels // 2
    message = ((half + 8, channels), F32)
    whole = pltpu.VMEM((9 * channels, channels), F32)
    decoded, rim_0, rim_d, rim_pre, keep_1, send_1 = call(
        functools.partial(rim_kernel, factor),
        "rim_columns",
        [VMEM] * 10,
        [
            (dout.shape, BF16),
            stack(6),
            stack(6),
            ((frames, 2, rows, channels), F32),
            message,
            message,
        ],
        (outer, inner, dout, conv_w, film, stack_0, stack_1, decoded_a, taps_1, stats_a),
        [
            pltpu.VMEM(stack(6)[0], BF16),
            pltpu.VMEM((frames, 4, rows, channels), BF16),
            whole,
            pltpu.SemaphoreType.DMA((3,)),
        ],
        16 * unit,
        [HBM] + [VMEM] * 5,
    )
    keep_0, send_0 = call(
        back_kernel,
        "back_columns",
        [VMEM] * 10,
        [message, message],
        (conv_w, film, stack_0, rim_0, stack_d, rim_d, pre_0, rim_pre, taps_0, stats_a),
        [whole],
        12 * unit,
    )
    (sum_1, sum_0), (stats_1, stats_0) = all_sums([(keep_1, send_1), (keep_0, send_0)], half)
    totals = jnp.stack([stats_0, stats_1])[:, : 2 * frames].reshape(layers, frames, 1, 2 * channels)
    film_grad = jnp.sum(audio_rows[None, :, :, None] * totals, axis=1)
    conv_grad = jnp.stack([sum_0, sum_1]).astype(F32).reshape(layers, 3, 3, channels, channels)
    return decoded, conv_grad, film_grad


def solution(mesh):
    return jax.shard_map(
        local,
        mesh=mesh,
        in_specs=(
            P("groups", "lon", None, None),
            P("groups"),
            P("groups", None),
            P("groups"),
            P(),
            P(),
            P("groups", "lon", None, None),
        ),
        out_specs=(
            P("groups", "lon", None, None),
            P("groups", None, None, None, None),
            P("groups", None, None),
        ),
        check_vma=False,
    )
```

time: 204 us -> 47.4 us (0.23)
  waiting for transfers between devices: 71.3 us -> 7.98 us
  local copies, waits for them, and re-layouts: 51.3 us -> 0.11 us
  blocking collectives: 30.1 us -> 0 us
  matrix products: 17.2 us -> 0 us
  starting transfers between devices: 7.1 us -> 21.9 us
  between operations: 14.5 us -> 1.04 us
  Pallas kernels: 0 us -> 13.3 us
  other arithmetic: 12.1 us -> 2.72 us
    psum x1 -> x0, waiting for transfers between devices: 58.4 us -> none  [local(): all_wgrads, all_stats = lax.psum((all_wgrads, all_stats), 'lon')]
    slice x22 -> x2, local copies, waits for them, and re-layouts: 33.2 us -> 0.04 us  [all_sums(): state.append((total[:half], total[half:]))]
    psum x1 -> x0, blocking collectives: 30.1 us -> none  [local(): all_wgrads, all_stats = lax.psum((all_wgrads, all_stats), 'lon')]
    dot_general x18 -> x0, matrix products: 17.2 us -> none  [the longest x9 12.6 us: conv_taps(): jnp.dot(window, weight[offset], preferred_element_type=jnp.float32)]
    ppermute x6 -> x14, starting transfers between devices: 7.06 us -> 21.9 us  [the longest x13 16.4 us: swap(): return lax.ppermute(value, AXIS, [(i, i ^ bit) for i in range(count)])]
    pallas_call x0 -> x4, Pallas kernels: none -> 13.3 us  [call(): pl.pallas_call(kernel, out_shape=tuple((jax.ShapeDtypeStruct(shape, dtype...]
    unnamed x55 -> x12, local copies, waits for them, and re-layouts: 9.13 us -> 0.03 us
    reshape x3 -> x0, local copies, waits for them, and re-layouts: 6.64 us -> none  [conv_taps(): return (summed.reshape(frames, out_cols, rows, weight.shape[2]), stacked)]
  transfers between devices with their start and end apart: 7 -> 14, of which waited for: 5 -> 9; matrix products, arithmetic and copies ran while one was open for 5% -> 3% of each run, Pallas kernels for 0% -> 10%
where the time goes in v2:
time: 47.4 us; the launch traced here: 47.1 us
  starting transfers between devices  21.9 us (46%)
  Pallas kernels  13.3 us (28%)
  waiting for transfers between devices  7.98 us (17%)
  other arithmetic  2.72 us (6%)
  between operations  1.04 us (2%)
    ppermute x13, starting transfers between devices, swap(): return lax.ppermute(value, AXIS, [(i, i ^ bit) for i in range(count)])  16.4 us
    pallas_call x4, Pallas kernels, call(): pl.pallas_call(kernel, out_shape=tuple((jax.ShapeDtypeStruct(shape, dtype...  13.3 us
    ppermute x13, waiting for transfers between devices, swap(): return lax.ppermute(value, AXIS, [(i, i ^ bit) for i in range(count)])  7.98 us
    ppermute x1, starting transfers between devices, local(): outer = lax.ppermute(outer, AXIS, pairs)  5.48 us
    convert_element_type x1, other arithmetic, local(): jnp.stack([sum_0, sum_1]).astype(F32)  1.09 us
  transfers between devices with their start and end apart: 14, of which 9 were waited for; matrix products, arithmetic and copies ran while one was open for 3% of the time, Pallas kernels for 10%

profile of v2, /device:TPU:0, one launch (start us, length us, event | category | flops | bytes accessed | tf_op | source)
XLA Modules:
  0.0 47.1 jit_solution(6346673676162879507)
XLA Ops:
  0.6 0.0 copy-start.1
  0.6 0.0 copy-start.2
  0.7 0.0 copy-start.5
  0.7 0.0 copy-start.3
  0.7 0.0 copy-start
  0.7 0.0 copy-start.4
  0.7 2.8 %edges.1 = (bf16[2,4,128,128]{3,2,1,0:T(8,128)(2,1)}, bf16[2,4,128,128]{3,2,1,0:T(8,128)(2,1)}) custom-call(s32[2]{0:T(128)} %identity.3, bf16[8,8,128,128]{3,2,1,0:T(8,128)(2,1)} %maps.3, bf16[2,8,128,128]{3,2,1,0:T(8,128)(2,1)} %dout.5), custom_call_target="tpu_custom_call" | custom-call | bytes 4194304 | tf_op jit(solution)/shard_map/edges/pallas_call | solution.py:359
  3.5 5.5 %collective-permute-start = (bf16[2,4,128,128]{3,2,1,0:T(8,128)(2,1)}, bf16[2,4,128,128]{3,2,1,0:T(8,128)(2,1)S(1)}, u32[]{:S(2)}, u32[]{:S(2)}) collective-permute-start(bf16[2,4,128,128]{3,2,1,0:T(8,128)(2,1)} %get-tuple-element.23), channel_id=1, source_target_pairs={{0,15},{1,2},{2,1},{3,4},{4,3},{5,6},{6,5},{7,8},{8,7},{9,10},{10,... | collective-permute-start | bytes 786440 | tf_op jit(solution)/shard_map/ppermute | solution.py:451
  8.9 0.0 collective-permute-start.1
  8.9 0.0 copy-done.1
  8.9 0.0 copy-done.2
  8.9 0.0 copy-done.5
  9.0 0.0 copy-done.3
  9.0 0.0 copy-done
  9.0 0.0 copy-done.4
  9.0 4.8 %inner_columns.1 = (f32[2,2,256]{2,1,0:T(2,128)S(1)}, f32[2,256]{1,0:T(2,128)S(1)}, bf16[2,8,128,384]{3,2,1,0:T(8,128)(2,1)S(1)}, bf16[2,6,128,384]{3,2,1,0:T(8,...) custom-call(s32[2]{0:T(128)S(1)} %copy-done.2, ...), custom_call_target="tpu_custom_call" | custom-call | flops 1358954496 | bytes 4194304 | tf_op jit(solution)/shard_map/inner_columns/pallas_call | solution.py:359
  13.8 0.0 collective-permute-done.outer
  13.8 0.0 collective-permute-done.1.inner
  13.9 3.7 %rim_columns.1 = (bf16[2,8,128,128]{3,2,1,0:T(8,128)(2,1)}, bf16[2,6,128,384]{3,2,1,0:T(8,128)(2,1)S(1)}, bf16[2,6,128,384]{3,2,1,0:T(8,128)(2,1)S(1)}, f32[2,2,...) custom-call(bf16[2,4,128,128]{3,2,1,0:T(8,128)(2,1)S(1)} %collective-permute-done.outer, ...), custom_call_target="tpu_custom_call" | custom-call | flops 1207959552 | bytes 4194304 | tf_op jit(solution)/shard_map/rim_columns/pallas_call | solution.py:359
  17.6 2.0 %back_columns.1 = (f32[584,128]{1,0:T(8,128)S(1)}, f32[584,128]{1,0:T(8,128)S(1)}) custom-call(bf16[2,3,3,128,128]{4,3,2,1,0:T(8,128)(2,1)S(1)} %copy-done, f32[2,2,256]{2,1,0:T(2,128)S(1)} %get-tuple-element.25.film, bf16[2,8,128,384]{3,2,1,0:T(8,128)(2,1)S(1)} %get-tuple-element.26.stack_0, bf16[2,6,128,384]{3,2,1,0:T(8,128)(2,1)S(1)} %get-tuple-element.32.rim_0, ...), custom_call_target="tpu_custom_call" | custom-call | flops 905969664 | bytes 4194304 | tf_op jit(solution)/shard_map/back_columns/pallas_call | solution.py:359
  19.6 0.6 %collective-permute-start.2 = (f32[584,128]{1,0:T(8,128)S(1)}, f32[584,128]{1,0:T(8,128)S(1)}, u32[]{:S(2)}, u32[]{:S(2)}) collective-permute-start(f32[584,128]{1,0:T(8,128)S(1)} %get-tuple-element.39), channel_id=1, source_target_pairs={{0,1},{1,0},{2,3},{3,2},{4,5},{5,4},{6,7},{7,6},{8,9},{9,8},{10,11... | collective-permute-start | bytes 897032 | tf_op jit(solution)/shard_map/ppermute | solution.py:373
  20.2 0.1 collective-permute-start.8
  20.2 1.1 %collective-permute-done.2 = f32[584,128]{1,0:T(8,128)S(1)} collective-permute-done((f32[584,128]{1,0:T(8,128)S(1)}, f32[584,128]{1,0:T(8,128)S(1)}, u32[]{:S(2)}, u32[]{:S(2)}) %collective-permute-start.2) | collective-permute-done | bytes 299040 | tf_op jit(solution)/shard_map/ppermute | solution.py:373
  21.5 0.3 collective-permute-done.8
  21.9 1.0 %collective-permute-start.3 = (bf16[304,128]{1,0:T(8,128)(2,1)S(1)}, bf16[304,128]{1,0:T(8,128)(2,1)S(1)}, u32[]{:S(2)}, u32[]{:S(2)}) collective-permute-start(bf16[304,128]{1,0:T(8,128)(2,1)S(1)} %pad_maximum_fusion.4), channel_id=1, source_target_pairs={{0,4},{1,5},{2,6},{3,7},{4,0},{5,1},{6,2},{7,3},{8,12},{9,13},{10,... | collective-permute-start | bytes 233480 | tf_op jit(solution)/shard_map/ppermute | solution.py:373
  22.9 2.0 %collective-permute-start.9 = (bf16[304,128]{1,0:T(8,128)(2,1)S(1)}, bf16[304,128]{1,0:T(8,128)(2,1)S(1)}, u32[]{:S(2)}, u32[]{:S(2)}) collective-permute-start(bf16[304,128]{1,0:T(8,128)(2,1)S(1)} %pad_maximum_fusion.7), channel_id=1, source_target_pairs={{0,2},{1,3},{2,0},{3,1},{4,6},{5,7},{6,4},{7,5},{8,10},{9,11},{10,... | collective-permute-start | bytes 233480 | tf_op jit(solution)/shard_map/ppermute | solution.py:373
  25.0 1.7 %collective-permute-done.3 = bf16[304,128]{1,0:T(8,128)(2,1)S(1)} collective-permute-done((bf16[304,128]{1,0:T(8,128)(2,1)S(1)}, bf16[304,128]{1,0:T(8,128)(2,1)S(1)}, u32[]{:S(2)}, u32[]{:S(2)}) %collective-permute-start.3) | collective-permute-done | bytes 77856 | tf_op jit(solution)/shard_map/ppermute | solution.py:373
  26.7 1.1 %collective-permute-start.4 = (bf16[304,128]{1,0:T(8,128)(2,1)S(1)}, bf16[304,128]{1,0:T(8,128)(2,1)S(1)}, u32[]{:S(2)}, u32[]{:S(2)}) collective-permute-start(bf16[304,128]{1,0:T(8,128)(2,1)S(1)} %pad_maximum_fusion.5), channel_id=1, source_target_pairs={{0,2},{1,3},{2,0},{3,1},{4,6},{5,7},{6,4},{7,5},{8,10},{9,11},{10,... | collective-permute-start | bytes 233480 | tf_op jit(solution)/shard_map/ppermute | solution.py:373
  27.9 0.0 collective-permute-done.9
  28.0 2.6 %collective-permute-start.10 = (bf16[304,128]{1,0:T(8,128)(2,1)S(1)}, bf16[304,128]{1,0:T(8,128)(2,1)S(1)}, u32[]{:S(2)}, u32[]{:S(2)}) collective-permute-start(bf16[304,128]{1,0:T(8,128)(2,1)S(1)} %pad_maximum_fusion.8), channel_id=1, source_target_pairs={{0,8},{1,9},{2,10},{3,11},{4,12},{5,13},{6,14},{7,15},{8,0},{9,1},... | collective-permute-start | bytes 233480 | tf_op jit(solution)/shard_map/ppermute | solution.py:373
  30.6 0.6 %collective-permute-done.4 = bf16[304,128]{1,0:T(8,128)(2,1)S(1)} collective-permute-done((bf16[304,128]{1,0:T(8,128)(2,1)S(1)}, bf16[304,128]{1,0:T(8,128)(2,1)S(1)}, u32[]{:S(2)}, u32[]{:S(2)}) %collective-permute-start.4) | collective-permute-done | bytes 77856 | tf_op jit(solution)/shard_map/ppermute | solution.py:373
  31.3 2.0 %collective-permute-start.5 = (bf16[304,128]{1,0:T(8,128)(2,1)S(1)}, bf16[304,128]{1,0:T(8,128)(2,1)S(1)}, u32[]{:S(2)}, u32[]{:S(2)}) collective-permute-start(bf16[304,128]{1,0:T(8,128)(2,1)S(1)} %pad_maximum_fusion.6), channel_id=1, source_target_pairs={{0,8},{1,9},{2,10},{3,11},{4,12},{5,13},{6,14},{7,15},{8,0},{9,1},... | collective-permute-start | bytes 233480 | tf_op jit(solution)/shard_map/ppermute | solution.py:373
  33.2 0.2 collective-permute-done.10
  33.5 2.6 %collective-permute-start.11 = (bf16[304,128]{1,0:T(8,128)(2,1)S(1)}, bf16[304,128]{1,0:T(8,128)(2,1)S(1)}, u32[]{:S(2)}, u32[]{:S(2)}) collective-permute-start(bf16[304,128]{1,0:T(8,128)(2,1)S(1)} %pad_maximum_fusion.9), channel_id=1, source_target_pairs={{0,4},{1,5},{2,6},{3,7},{4,0},{5,1},{6,2},{7,3},{8,12},{9,13},{10,... | collective-permute-start | bytes 233480 | tf_op jit(solution)/shard_map/ppermute | solution.py:373
  36.2 1.1 %collective-permute-done.5 = bf16[304,128]{1,0:T(8,128)(2,1)S(1)} collective-permute-done((bf16[304,128]{1,0:T(8,128)(2,1)S(1)}, bf16[304,128]{1,0:T(8,128)(2,1)S(1)}, u32[]{:S(2)}, u32[]{:S(2)}) %collective-permute-start.5) | collective-permute-done | bytes 77856 | tf_op jit(solution)/shard_map/ppermute | solution.py:373
  37.3 1.1 %collective-permute-start.6 = (bf16[288,128]{1,0:T(8,128)(2,1)S(1)}, bf16[288,128]{1,0:T(8,128)(2,1)S(1)}, u32[]{:S(2)}, u32[]{:S(2)}) collective-permute-start(bf16[288,128]{1,0:T(8,128)(2,1)S(1)} %fusion.3), channel_id=1, source_target_pairs={{0,4},{1,5},{2,6},{3,7},{4,0},{5,1},{6,2},{7,3},{8,12},{9,13},{10,... | collective-permute-start | bytes 221192 | tf_op jit(solution)/shard_map/ppermute | solution.py:373
  38.4 0.3 collective-permute-done.11
  38.8 3.2 %collective-permute-start.12 = (bf16[288,128]{1,0:T(8,128)(2,1)S(1)}, bf16[288,128]{1,0:T(8,128)(2,1)S(1)}, u32[]{:S(2)}, u32[]{:S(2)}) collective-permute-start(bf16[288,128]{1,0:T(8,128)(2,1)S(1)} %fusion), channel_id=1, source_target_pairs={{0,2},{1,3},{2,0},{3,1},{4,6},{5,7},{6,4},{7,5},{8,10},{9,11},{10,... | collective-permute-start | bytes 221192 | tf_op jit(solution)/shard_map/ppermute | solution.py:373
  42.0 0.0 collective-permute-done.6
  42.0 0.1 collective-permute-start.7
  42.1 2.2 %collective-permute-done.12 = bf16[288,128]{1,0:T(8,128)(2,1)S(1)} collective-permute-done((bf16[288,128]{1,0:T(8,128)(2,1)S(1)}, bf16[288,128]{1,0:T(8,128)(2,1)S(1)}, u32[]{:S(2)}, u32[]{:S(2)}) %collective-permute-start.12) | collective-permute-done | bytes 73760 | tf_op jit(solution)/shard_map/ppermute | solution.py:373
  44.4 0.1 collective-permute-start.13
  44.5 0.9 %multiply_reduce_fusion = f32[2,256,256]{2,1,0:T(8,128)} fusion(f32[2,2,256]{2,1,0:T(2,128)S(1)} %mul.32, f32[2,256]{1,0:T(2,128)S(1)} %get-tuple-element.42), kind=kLoop, calls=%fused_computation | loop fusion | flops 393216 | bytes 530432 | tf_op jit(solution)/shard_map/reduce_sum | solution.py:530
  45.4 0.0 collective-permute-done.7
  45.4 0.4 collective-permute-done.13
  45.8 0.1 broadcast_select_fusion.1
  46.0 1.1 %maximum_convert_fusion = f32[2,3,3,128,128]{4,3,2,1,0:T(8,128)} fusion(bf16[1,3,3,128,128]{4,3,2,1,0:T(8,128)(2,1)S(1)} %bitcast.7, bf16[1,3,3,128,128]{4,3,2,1,0:T(8,128)(2,1)S(1)} %bitcast.6), kind=kLoop, calls=%fused_computation.1 | loop fusion | flops 589824 | bytes 1769472 | tf_op jit(solution)/shard_map/convert_element_type | solution.py:531
  (44 shorter events, 0.7 us)
Async XLA Ops:
  0.6 8.3 %copy-start.1 = (bf16[2,8,128,128]{3,2,1,0:T(8,128)(2,1)S(1)}, bf16[2,8,128,128]{3,2,1,0:T(8,128)(2,1)}, u32[]{:S(2)}) copy-start(bf16[2,8,128,128]{3,2,1,0:T(8,128)(2,1)} %dout.5) | copy-start | bytes 1572868
  0.6 8.3 %copy-start.2 = (s32[2]{0:T(128)S(1)}, s32[2]{0:T(128)}, u32[]{:S(2)}) copy-start(s32[2]{0:T(128)} %identity.3) | copy-start | bytes 28
  0.7 8.3 %copy-start.5 = (s32[2]{0:T(128)S(1)}, s32[2]{0:T(128)}, u32[]{:S(2)}) copy-start(s32[2]{0:T(128)} %audio_index.1) | copy-start | bytes 28
  0.7 8.3 %copy-start.3 = (f32[2,256,256]{2,1,0:T(8,128)S(1)}, f32[2,256,256]{2,1,0:T(8,128)}, u32[]{:S(2)}) copy-start(f32[2,256,256]{2,1,0:T(8,128)} %film_w.1) | copy-start | bytes 1572868
  0.7 8.3 %copy-start = (bf16[2,3,3,128,128]{4,3,2,1,0:T(8,128)(2,1)S(1)}, bf16[2,3,3,128,128]{4,3,2,1,0:T(8,128)(2,1)}, u32[]{:S(2)}) copy-start(bf16[2,3,3,128,128]{4,3,2,1,0:T(8,128)(2,1)} %weights.5) | copy-start | bytes 1769476
  0.7 8.3 %copy-start.4 = (f32[64,256]{1,0:T(8,128)S(1)}, f32[64,256]{1,0:T(8,128)}, u32[]{:S(2)}) copy-start(f32[64,256]{1,0:T(8,128)} %audio.1) | copy-start | bytes 196612
  3.5 10.4 %collective-permute-start = (bf16[2,4,128,128]{3,2,1,0:T(8,128)(2,1)}, bf16[2,4,128,128]{3,2,1,0:T(8,128)(2,1)S(1)}, u32[]{:S(2)}, u32[]{:S(2)}) collective-permute-start(bf16[2,4,128,128]{3,2,1,0:T(8,128)(2,1)} %get-tuple-element.23), channel_id=1, source_target_pairs={{0,15},{1,2},{2,1},{3,4},{4,3},{5,6},{6,5},{7,8},{8,7},{9,10},{10,... | collective-permute-start | bytes 786440 | tf_op jit(solution)/shard_map/ppermute | solution.py:451
  8.9 4.9 %collective-permute-start.1 = (bf16[2,4,128,128]{3,2,1,0:T(8,128)(2,1)}, bf16[2,4,128,128]{3,2,1,0:T(8,128)(2,1)S(1)}, u32[]{:S(2)}, u32[]{:S(2)}) collective-permute-start(bf16[2,4,128,128]{3,2,1,0:T(8,128)(2,1)} %get-tuple-element.24), channel_id=1, source_target_pairs={{0,1},{1,0},{2,3},{3,2},{4,5},{5,4},{6,7},{7,6},{8,9},{9,8},{10,11... | collective-permute-start | bytes 786440 | tf_op jit(solution)/shard_map/ppermute | solution.py:373
  19.6 1.8 %collective-permute-start.2 = (f32[584,128]{1,0:T(8,128)S(1)}, f32[584,128]{1,0:T(8,128)S(1)}, u32[]{:S(2)}, u32[]{:S(2)}) collective-permute-start(f32[584,128]{1,0:T(8,128)S(1)} %get-tuple-element.39), channel_id=1, source_target_pairs={{0,1},{1,0},{2,3},{3,2},{4,5},{5,4},{6,7},{7,6},{8,9},{9,8},{10,11... | collective-permute-start | bytes 897032 | tf_op jit(solution)/shard_map/ppermute | solution.py:373
  20.2 1.6 %collective-permute-start.8 = (f32[584,128]{1,0:T(8,128)S(1)}, f32[584,128]{1,0:T(8,128)S(1)}, u32[]{:S(2)}, u32[]{:S(2)}) collective-permute-start(f32[584,128]{1,0:T(8,128)S(1)} %get-tuple-element.41), channel_id=1, source_target_pairs={{0,1},{1,0},{2,3},{3,2},{4,5},{5,4},{6,7},{7,6},{8,9},{9,8},{10,11... | collective-permute-start | bytes 897032 | tf_op jit(solution)/shard_map/ppermute | solution.py:373
  21.9 4.7 %collective-permute-start.3 = (bf16[304,128]{1,0:T(8,128)(2,1)S(1)}, bf16[304,128]{1,0:T(8,128)(2,1)S(1)}, u32[]{:S(2)}, u32[]{:S(2)}) collective-permute-start(bf16[304,128]{1,0:T(8,128)(2,1)S(1)} %pad_maximum_fusion.4), channel_id=1, source_target_pairs={{0,4},{1,5},{2,6},{3,7},{4,0},{5,1},{6,2},{7,3},{8,12},{9,13},{10,... | collective-permute-start | bytes 233480 | tf_op jit(solution)/shard_map/ppermute | solution.py:373
  22.9 4.9 %collective-permute-start.9 = (bf16[304,128]{1,0:T(8,128)(2,1)S(1)}, bf16[304,128]{1,0:T(8,128)(2,1)S(1)}, u32[]{:S(2)}, u32[]{:S(2)}) collective-permute-start(bf16[304,128]{1,0:T(8,128)(2,1)S(1)} %pad_maximum_fusion.7), channel_id=1, source_target_pairs={{0,2},{1,3},{2,0},{3,1},{4,6},{5,7},{6,4},{7,5},{8,10},{9,11},{10,... | collective-permute-start | bytes 233480 | tf_op jit(solution)/shard_map/ppermute | solution.py:373
  26.7 4.5 %collective-permute-start.4 = (bf16[304,128]{1,0:T(8,128)(2,1)S(1)}, bf16[304,128]{1,0:T(8,128)(2,1)S(1)}, u32[]{:S(2)}, u32[]{:S(2)}) collective-permute-start(bf16[304,128]{1,0:T(8,128)(2,1)S(1)} %pad_maximum_fusion.5), channel_id=1, source_target_pairs={{0,2},{1,3},{2,0},{3,1},{4,6},{5,7},{6,4},{7,5},{8,10},{9,11},{10,... | collective-permute-start | bytes 233480 | tf_op jit(solution)/shard_map/ppermute | solution.py:373
  28.0 5.5 %collective-permute-start.10 = (bf16[304,128]{1,0:T(8,128)(2,1)S(1)}, bf16[304,128]{1,0:T(8,128)(2,1)S(1)}, u32[]{:S(2)}, u32[]{:S(2)}) collective-permute-start(bf16[304,128]{1,0:T(8,128)(2,1)S(1)} %pad_maximum_fusion.8), channel_id=1, source_target_pairs={{0,8},{1,9},{2,10},{3,11},{4,12},{5,13},{6,14},{7,15},{8,0},{9,1},... | collective-permute-start | bytes 233480 | tf_op jit(solution)/shard_map/ppermute | solution.py:373
  31.3 6.0 %collective-permute-start.5 = (bf16[304,128]{1,0:T(8,128)(2,1)S(1)}, bf16[304,128]{1,0:T(8,128)(2,1)S(1)}, u32[]{:S(2)}, u32[]{:S(2)}) collective-permute-start(bf16[304,128]{1,0:T(8,128)(2,1)S(1)} %pad_maximum_fusion.6), channel_id=1, source_target_pairs={{0,8},{1,9},{2,10},{3,11},{4,12},{5,13},{6,14},{7,15},{8,0},{9,1},... | collective-permute-start | bytes 233480 | tf_op jit(solution)/shard_map/ppermute | solution.py:373
  33.5 5.2 %collective-permute-start.11 = (bf16[304,128]{1,0:T(8,128)(2,1)S(1)}, bf16[304,128]{1,0:T(8,128)(2,1)S(1)}, u32[]{:S(2)}, u32[]{:S(2)}) collective-permute-start(bf16[304,128]{1,0:T(8,128)(2,1)S(1)} %pad_maximum_fusion.9), channel_id=1, source_target_pairs={{0,4},{1,5},{2,6},{3,7},{4,0},{5,1},{6,2},{7,3},{8,12},{9,13},{10,... | collective-permute-start | bytes 233480 | tf_op jit(solution)/shard_map/ppermute | solution.py:373
  37.3 4.7 %collective-permute-start.6 = (bf16[288,128]{1,0:T(8,128)(2,1)S(1)}, bf16[288,128]{1,0:T(8,128)(2,1)S(1)}, u32[]{:S(2)}, u32[]{:S(2)}) collective-permute-start(bf16[288,128]{1,0:T(8,128)(2,1)S(1)} %fusion.3), channel_id=1, source_target_pairs={{0,4},{1,5},{2,6},{3,7},{4,0},{5,1},{6,2},{7,3},{8,12},{9,13},{10,... | collective-permute-start | bytes 221192 | tf_op jit(solution)/shard_map/ppermute | solution.py:373
  38.8 5.6 %collective-permute-start.12 = (bf16[288,128]{1,0:T(8,128)(2,1)S(1)}, bf16[288,128]{1,0:T(8,128)(2,1)S(1)}, u32[]{:S(2)}, u32[]{:S(2)}) collective-permute-start(bf16[288,128]{1,0:T(8,128)(2,1)S(1)} %fusion), channel_id=1, source_target_pairs={{0,2},{1,3},{2,0},{3,1},{4,6},{5,7},{6,4},{7,5},{8,10},{9,11},{10,... | collective-permute-start | bytes 221192 | tf_op jit(solution)/shard_map/ppermute | solution.py:373
  42.0 3.4 %collective-permute-start.7 = (bf16[576,128]{1,0:T(8,128)(2,1)S(1)}, bf16[576,128]{1,0:T(8,128)(2,1)S(1)}, u32[]{:S(2)}, u32[]{:S(2)}) collective-permute-start(bf16[576,128]{1,0:T(8,128)(2,1)S(1)} %pad_maximum_fusion.2), channel_id=1, source_target_pairs={{0,1},{1,0},{2,3},{3,2},{4,5},{5,4},{6,7},{7,6},{8,9},{9,8},{10,11... | collective-permute-start | bytes 442376 | tf_op jit(solution)/shard_map/ppermute | solution.py:373
  44.4 1.4 %collective-permute-start.13 = (bf16[576,128]{1,0:T(8,128)(2,1)S(1)}, bf16[576,128]{1,0:T(8,128)(2,1)S(1)}, u32[]{:S(2)}, u32[]{:S(2)}) collective-permute-start(bf16[576,128]{1,0:T(8,128)(2,1)S(1)} %pad_maximum_fusion.3), channel_id=1, source_target_pairs={{0,1},{1,0},{2,3},{3,2},{4,5},{5,4},{6,7},{7,6},{8,9},{9,8},{10,11... | collective-permute-start | bytes 442376 | tf_op jit(solution)/shard_map/ppermute | solution.py:373

commit v3 on v2

--- a/solution.py
+++ b/solution.py
@@ -223,7 +223,7 @@
             h_0.put(f, some, shift_stack(values, rows), rows)
 
     for f in range(frames):
-        for some in parts_of(range(1, columns - 1), 3):
+        for some in parts_of(range(1, columns - 1), 6):
             forward_0(film, weights, h_0, h_1, saved, f, some, rows)
     sums_1, sums_0 = Sums(), Sums()
     for f in range(frames):
@@ -250,16 +250,21 @@
     film,
     stack_0,
     stack_1,
+    stack_d,
+    pre_0,
     decoded_a,
-    taps_a,
+    taps_0,
+    taps_1,
     stats_a,
     decoded,
+    keep_1,
+    send_1,
+    keep_0,
+    send_0,
     rim_0,
+    rim_1,
     rim_d,
     rim_pre,
-    keep,
-    send,
-    rim_1,
     hidden,
     whole,
     sems,
@@ -275,8 +280,10 @@
     h_1 = Columns(
         (stack_1, range(1, last)), (rim_1, [-2, -1, 0, last, last + 1, last + 2])
     )
-    d_1 = Columns((rim_d, [-1, 0, 1, last - 1, last, last + 1]))
-    saved = Columns((rim_pre, [0, last]))
+    d_1 = Columns(
+        (stack_d, range(2, columns - 2)), (rim_d, [-1, 0, 1, last - 1, last, last + 1])
+    )
+    saved = Columns((pre_0, range(1, last)), (rim_pre, [0, last]))
     out = Columns((hidden, [0, 1, last - 1, last]))
     grads = Columns((dout, range(columns)))
 
@@ -297,14 +304,16 @@
             high = received(f, n, True)
             h_0.put(f, [columns + n], shift_stack(high, rows), rows)
     for f in range(frames):
-        for some in ([-2, -1, 0], [last, last + 1, last + 2]):
+        for some in ([-2, -1, 0, last, last + 1, last + 2],):
             forward_0(film, weights, h_0, h_1, saved, f, some, rows)
-    sums = Sums()
+    sums_0, sums_1 = Sums(), Sums()
     edges = Edges()
     for f in range(frames):
         both_1(factor, film, weights, h_1, edges, out, d_1, f, [-1, last + 1], rows)
         some = [0, 1, last - 1, last]
-        sums.add(f, some, rows, *both_1(factor, film, weights, h_1, edges, out, d_1, f, some, rows))
+        sums_1.add(
+            f, some, rows, *both_1(factor, film, weights, h_1, edges, out, d_1, f, some, rows)
+        )
     ends = [
         pltpu.make_async_copy(
             hidden.at[:, pl.ds(0, 2)], decoded.at[:, pl.ds(0, 2)], sems.at[1]
@@ -315,44 +324,16 @@
     ]
     for copy in ends:
         copy.start()
-    totals = [taps_a[a] + sums.taps(h_1, a) for a in range(3)]
-    put_message(mine, totals, stats_a[1] + sums.rows_of_stats(), whole, keep, send)
+    for f in range(frames):
+        some = [0, 1, 2, last - 2, last - 1, last]
+        sums_0.add(f, some, rows, *back_0(film, weights, d_1, saved, f, some))
+    totals = [taps_1[a] + sums_1.taps(h_1, a) for a in range(3)]
+    put_message(mine, totals, stats_a[1] + sums_1.rows_of_stats(), whole, keep_1, send_1)
+    totals = [taps_0[a] + sums_0.taps(h_0, a) for a in range(3)]
+    put_message(mine, totals, stats_a[0] + sums_0.rows_of_stats(), whole, keep_0, send_0)
     done.wait()
     for copy in ends:
         copy.wait()
-
-
-def back_kernel(
-    weights,
-    film,
-    stack_0,
-    rim_0,
-    stack_d,
-    rim_d,
-    pre_0,
-    rim_pre,
-    taps_a,
-    stats_a,
-    keep,
-    send,
-    whole,
-):
-    frames, columns, rows = stack_0.shape[:3]
-    mine = lax.rem(lax.axis_index(AXIS), 2)
-    last = columns - 1
-    h_0 = Columns(
-        (stack_0, range(columns)), (rim_0, [-3, -2, -1, last + 1, last + 2, last + 3])
-    )
-    d_1 = Columns(
-        (stack_d, range(2, columns - 2)), (rim_d, [-1, 0, 1, last - 1, last, last + 1])
-    )
-    saved = Columns((pre_0, range(1, last)), (rim_pre, [0, last]))
-    sums = Sums()
-    for f in range(frames):
-        some = [0, 1, 2, last - 2, last - 1, last]
-        sums.add(f, some, rows, *back_0(film, weights, d_1, saved, f, some))
-    totals = [taps_a[a] + sums.taps(h_0, a) for a in range(3)]
-    put_message(mine, totals, stats_a[0] + sums.rows_of_stats(), whole, keep, send)
 
 
 def call(kernel, name, ins, outs, args, scratch=(), flops=0, out_specs=None, room=36):
@@ -368,13 +349,16 @@
     )(*args)
 
 
-def swap(value, bit):
+def swap(value, bits):
     count = lax.axis_size(AXIS)
-    return lax.ppermute(value, AXIS, [(i, i ^ bit) for i in range(count)])
-
-
-def mine_of(bit):
-    return (lax.axis_index(AXIS) // bit) % 2
+    return lax.ppermute(value, AXIS, [(i, i ^ bits[i % 2]) for i in range(count)])
+
+
+def mine_of(bits):
+    place = lax.axis_index(AXIS)
+    if bits[0] == bits[1]:
+        return (place // bits[0]) % 2
+    return jnp.where(place % 2 == 0, (place // bits[0]) % 2, (place // bits[1]) % 2)
 
 
 def rounded(value):
@@ -410,14 +394,12 @@
     bits = []
     while (2 << len(bits)) < lax.axis_size(AXIS):
         bits.append(2 << len(bits))
-    orders = [list(bits), list(bits)]
-    if len(bits) > 1:
-        orders[1][0], orders[1][1] = bits[1], bits[0]
-    if len(bits) > 2:
-        orders[0][1], orders[0][2] = bits[2], bits[1]
+    one = bits[:1] + bits[2:] + bits[1:2]
+    other = bits[1:2] + bits[:1] + bits[2:]
+    orders = [list(zip(one, other)), list(zip(other, one))]
     state = []
     for keep, send in messages:
-        total = keep + swap(send, 1)
+        total = keep + swap(send, (1, 1))
         state.append((total[:half], total[half:]))
     for step in range(len(bits)):
         for s in range(2):
@@ -425,7 +407,7 @@
     taps = [value.astype(BF16) for value, _ in state]
     if bits:
         taps = [join(taps[s], orders[s][0]) for s in range(2)]
-    taps = [join(value, 1) for value in taps]
+    taps = [join(value, (1, 1)) for value in taps]
     return taps, [stats for _, stats in state]
 
 
@@ -445,11 +427,11 @@
         [edges, edges],
         (identity, ident_maps, dout),
         [pltpu.SemaphoreType.DMA((2, frames, 2))],
-        room=57,
+        room=53,
     )
     pairs = [(i, (i + 1) % count if i % 2 else (i - 1) % count) for i in range(count)]
     outer = lax.ppermute(outer, AXIS, pairs)
-    inner = swap(inner, 1)
+    inner = swap(inner, (1, 1))
 
     def stack(n):
         return ((frames, n, rows, 3 * channels), BF16)
@@ -494,38 +476,26 @@
     half = 9 * channels // 2
     message = ((half + 8, channels), F32)
     whole = pltpu.VMEM((9 * channels, channels), F32)
-    decoded, rim_0, rim_d, rim_pre, keep_1, send_1 = call(
+    decoded, keep_1, send_1, keep_0, send_0 = call(
         functools.partial(rim_kernel, factor),
         "rim_columns",
-        [VMEM] * 10,
-        [
-            (dout.shape, BF16),
-            stack(6),
-            stack(6),
-            ((frames, 2, rows, channels), F32),
-            message,
-            message,
-        ],
-        (outer, inner, dout, conv_w, film, stack_0, stack_1, decoded_a, taps_1, stats_a),
+        [VMEM] * 13,
+        [(dout.shape, BF16)] + [message] * 4,
+        (outer, inner, dout, conv_w, film, stack_0, stack_1, stack_d, pre_0, decoded_a)
+        + (taps_0, taps_1, stats_a),
         [
             pltpu.VMEM(stack(6)[0], BF16),
+            pltpu.VMEM(stack(6)[0], BF16),
+            pltpu.VMEM(stack(6)[0], BF16),
+            pltpu.VMEM((frames, 2, rows, channels), F32),
             pltpu.VMEM((frames, 4, rows, channels), BF16),
             whole,
             pltpu.SemaphoreType.DMA((3,)),
         ],
-        16 * unit,
-        [HBM] + [VMEM] * 5,
-    )
-    keep_0, send_0 = call(
-        back_kernel,
-        "back_columns",
-        [VMEM] * 10,
-        [message, message],
-        (conv_w, film, stack_0, rim_0, stack_d, rim_d, pre_0, rim_pre, taps_0, stats_a),
-        [whole],
-        12 * unit,
-    )
-    (sum_1, sum_0), (stats_1, stats_0) = all_sums([(keep_1, send_1), (keep_0, send_0)], half)
+        28 * unit,
+        [HBM] + [VMEM] * 4,
+    )
+    (sum_0, sum_1), (stats_0, stats_1) = all_sums([(keep_0, send_0), (keep_1, send_1)], half)
     totals = jnp.stack([stats_0, stats_1])[:, : 2 * frames].reshape(layers, frames, 1, 2 * channels)
     film_grad = jnp.sum(audio_rows[None, :, :, None] * totals, axis=1)
     conv_grad = jnp.stack([sum_0, sum_1]).astype(F32).reshape(layers, 3, 3, channels, channels)

time: 47.4 us -> 46 us (0.970)
  starting transfers between devices: 21.9 us -> 15.7 us
  waiting for transfers between devices: 7.98 us -> 13.8 us
  Pallas kernels: 13.3 us -> 11.8 us
  local copies, waits for them, and re-layouts: 0.11 us -> 0.81 us
    ppermute x13, starting transfers between devices: 16.4 us -> 10.3 us  [swap(): lax.ppermute(value, AXIS, [(i, i ^ bits[i % 2]) for i in range(count)])]
    ppermute x13, waiting for transfers between devices: 7.98 us -> 13.8 us  [swap(): lax.ppermute(value, AXIS, [(i, i ^ bits[i % 2]) for i in range(count)])]
    pallas_call x4 -> x3, Pallas kernels: 13.3 us -> 11.8 us  [call(): pl.pallas_call(kernel, out_shape=tuple((jax.ShapeDtypeStruct(shape, dtype...]
    unnamed x12 -> x14, local copies, waits for them, and re-layouts: 0.03 us -> 0.73 us
  transfers between devices with their start and end apart: 14 -> 14, of which waited for: 9 -> 10; matrix products, arithmetic and copies ran while one was open for 3% -> 3% of each run, Pallas kernels for 10% -> 11%
where the time goes in v3:
time: 46 us; the launch traced here: 45.8 us
  starting transfers between devices  15.7 us (34%)
  waiting for transfers between devices  13.8 us (30%)
  Pallas kernels  11.8 us (26%)
  other arithmetic  2.72 us (6%)
  between operations  1.02 us (2%)
  local copies, waits for them, and re-layouts  0.81 us (2%)
    ppermute x13, waiting for transfers between devices, swap(): lax.ppermute(value, AXIS, [(i, i ^ bits[i % 2]) for i in range(count)])  13.8 us
    pallas_call x3, Pallas kernels, call(): pl.pallas_call(kernel, out_shape=tuple((jax.ShapeDtypeStruct(shape, dtype...  11.8 us
    ppermute x13, starting transfers between devices, swap(): lax.ppermute(value, AXIS, [(i, i ^ bits[i % 2]) for i in range(count)])  10.3 us
    ppermute x1, starting transfers between devices, local(): outer = lax.ppermute(outer, AXIS, pairs)  5.48 us
    convert_element_type x1, other arithmetic, local(): jnp.stack([sum_0, sum_1]).astype(F32)  1.09 us
    reduce_sum x1, other arithmetic, local(): film_grad = jnp.sum(audio_rows[None, :, :, None] * totals, axis=1)  0.93 us
  transfers between devices with their start and end apart: 14, of which 10 were waited for; matrix products, arithmetic and copies ran while one was open for 3% of the time, Pallas kernels for 11%

profile of v3, /device:TPU:0, one launch (start us, length us, event | category | flops | bytes accessed | tf_op | source)
XLA Modules:
  0.0 45.8 jit_solution(13686645734572186950)
XLA Ops:
  0.6 0.0 copy-start
  0.6 0.0 copy-start.1
  0.7 0.7 %copy-done.1 = s32[2]{0:T(128)S(1)} copy-done((s32[2]{0:T(128)S(1)}, s32[2]{0:T(128)}, u32[]{:S(2)}) %copy-start.1) | copy-done | bytes 32
  1.4 0.0 copy-start.2
  1.4 0.0 copy-start.3
  1.4 0.0 copy-start.4
  1.4 0.0 copy-start.5
  1.4 0.0 copy-start.6
  1.4 1.7 %edges.1 = (bf16[2,4,128,128]{3,2,1,0:T(8,128)(2,1)S(1)}, bf16[2,4,128,128]{3,2,1,0:T(8,128)(2,1)S(1)}) custom-call(s32[2]{0:T(128)S(1)} %copy-done.1, bf16[8,8,128,128]{3,2,1,0:T(8,128)(2,1)} %maps.3, bf16[2,8,128,128]{3,2,1,0:T(8,128)(2,1)} %dout.5), custom_call_target="tpu_custom_call" | custom-call | bytes 4194304 | tf_op jit(solution)/shard_map/edges/pallas_call | solution.py:340
  3.1 5.5 %collective-permute-start = (bf16[2,4,128,128]{3,2,1,0:T(8,128)(2,1)S(1)}, bf16[2,4,128,128]{3,2,1,0:T(8,128)(2,1)S(1)}, u32[]{:S(2)}, u32[]{:S(2)}) collective-permute-start(bf16[2,4,128,128]{3,2,1,0:T(8,128)(2,1)S(1)} %get-tuple-element.20), channel_id=1, source_target_pairs={{0,15},{1,2},{2,1},{3,4},{4,3},{5,6},{6,5},{7,8},{8,7},{9,10},{10,... | collective-permute-start | bytes 786440 | tf_op jit(solution)/shard_map/ppermute | solution.py:433
  8.6 0.0 collective-permute-start.1
  8.6 0.0 copy-done
  8.6 0.0 copy-done.2
  8.6 0.0 copy-done.3
  8.6 0.0 copy-done.4
  8.6 0.0 copy-done.5
  8.6 0.0 copy-done.6
  8.6 4.8 %inner_columns.1 = (f32[2,2,256]{2,1,0:T(2,128)S(1)}, f32[2,256]{1,0:T(2,128)S(1)}, bf16[2,8,128,384]{3,2,1,0:T(8,128)(2,1)S(1)}, bf16[2,6,128,384]{3,2,1,0:T(8,...) custom-call(s32[2]{0:T(128)S(1)} %copy-done.2, ...), custom_call_target="tpu_custom_call" | custom-call | flops 1358954496 | bytes 4194304 | tf_op jit(solution)/shard_map/inner_columns/pallas_call | solution.py:340
  13.5 0.0 collective-permute-done.outer
  13.5 0.0 collective-permute-done.1.inner
  13.5 5.2 %rim_columns.1 = (bf16[2,8,128,128]{3,2,1,0:T(8,128)(2,1)}, f32[584,128]{1,0:T(8,128)S(1)}, f32[584,128]{1,0:T(8,128)S(1)}, f32[584,128]{1,0:T(8,128)S(1)}, f32[584,128]{1,0:T(8,128)S(1)}) custom-call(bf16[2,4,128,128]{3,2,1,0:T(8,128)(2,1)S(1)} %collective-permute-done.outer, bf16[2,4,128,128]{3,2,1,0:T(8,128)(2,1)S(1)} %collective-permute-done.1.inner, ...), custom_call_target="tpu_custom_call" | custom-call | flops 2113929216 | bytes 4194304 | tf_op jit(solution)/shard_map/rim_columns/pallas_call | solution.py:340
  18.7 0.6 %collective-permute-start.8 = (f32[584,128]{1,0:T(8,128)S(1)}, f32[584,128]{1,0:T(8,128)S(1)}, u32[]{:S(2)}, u32[]{:S(2)}) collective-permute-start(f32[584,128]{1,0:T(8,128)S(1)} %get-tuple-element.35), channel_id=1, source_target_pairs={{0,1},{1,0},{2,3},{3,2},{4,5},{5,4},{6,7},{7,6},{8,9},{9,8},{10,11... | collective-permute-start | bytes 897032 | tf_op jit(solution)/shard_map/ppermute | solution.py:354
  19.3 0.1 collective-permute-start.2
  19.4 1.1 %collective-permute-done.8 = f32[584,128]{1,0:T(8,128)S(1)} collective-permute-done((f32[584,128]{1,0:T(8,128)S(1)}, f32[584,128]{1,0:T(8,128)S(1)}, u32[]{:S(2)}, u32[]{:S(2)}) %collective-permute-start.8) | collective-permute-done | bytes 299040 | tf_op jit(solution)/shard_map/ppermute | solution.py:354
  20.6 0.3 collective-permute-done.2
  21.1 0.7 %collective-permute-start.9 = (bf16[304,128]{1,0:T(8,128)(2,1)S(1)}, bf16[304,128]{1,0:T(8,128)(2,1)S(1)}, u32[]{:S(2)}, u32[]{:S(2)}) collective-permute-start(bf16[304,128]{1,0:T(8,128)(2,1)S(1)} %pad_maximum_fusion.7), channel_id=1, source_target_pairs={{0,4},{1,3},{2,6},{3,1},{4,0},{5,7},{6,2},{7,5},{8,12},{9,11},{10,... | collective-permute-start | bytes 233480 | tf_op jit(solution)/shard_map/ppermute | solution.py:354
  21.8 2.1 %collective-permute-start.3 = (bf16[304,128]{1,0:T(8,128)(2,1)S(1)}, bf16[304,128]{1,0:T(8,128)(2,1)S(1)}, u32[]{:S(2)}, u32[]{:S(2)}) collective-permute-start(bf16[304,128]{1,0:T(8,128)(2,1)S(1)} %pad_maximum_fusion.4), channel_id=1, source_target_pairs={{0,2},{1,5},{2,0},{3,7},{4,6},{5,1},{6,4},{7,3},{8,10},{9,13},{10,... | collective-permute-start | bytes 233480 | tf_op jit(solution)/shard_map/ppermute | solution.py:354
  23.9 2.4 %collective-permute-done.9 = bf16[304,128]{1,0:T(8,128)(2,1)S(1)} collective-permute-done((bf16[304,128]{1,0:T(8,128)(2,1)S(1)}, bf16[304,128]{1,0:T(8,128)(2,1)S(1)}, u32[]{:S(2)}, u32[]{:S(2)}) %collective-permute-start.9) | collective-permute-done | bytes 77856 | tf_op jit(solution)/shard_map/ppermute | solution.py:354
  26.4 1.0 %collective-permute-start.10 = (bf16[304,128]{1,0:T(8,128)(2,1)S(1)}, bf16[304,128]{1,0:T(8,128)(2,1)S(1)}, u32[]{:S(2)}, u32[]{:S(2)}) collective-permute-start(bf16[304,128]{1,0:T(8,128)(2,1)S(1)} %pad_maximum_fusion.8), channel_id=1, source_target_pairs={{0,2},{1,9},{2,0},{3,11},{4,6},{5,13},{6,4},{7,15},{8,10},{9,1},{1... | collective-permute-start | bytes 233480 | tf_op jit(solution)/shard_map/ppermute | solution.py:354
  27.5 0.0 collective-permute-done.3
  27.6 2.1 %collective-permute-start.4 = (bf16[304,128]{1,0:T(8,128)(2,1)S(1)}, bf16[304,128]{1,0:T(8,128)(2,1)S(1)}, u32[]{:S(2)}, u32[]{:S(2)}) collective-permute-start(bf16[304,128]{1,0:T(8,128)(2,1)S(1)} %pad_maximum_fusion.5), channel_id=1, source_target_pairs={{0,8},{1,3},{2,10},{3,1},{4,12},{5,7},{6,14},{7,5},{8,0},{9,11},{1... | collective-permute-start | bytes 233480 | tf_op jit(solution)/shard_map/ppermute | solution.py:354
  29.7 1.4 %collective-permute-done.10 = bf16[304,128]{1,0:T(8,128)(2,1)S(1)} collective-permute-done((bf16[304,128]{1,0:T(8,128)(2,1)S(1)}, bf16[304,128]{1,0:T(8,128)(2,1)S(1)}, u32[]{:S(2)}, u32[]{:S(2)}) %collective-permute-start.10) | collective-permute-done | bytes 77856 | tf_op jit(solution)/shard_map/ppermute | solution.py:354
  31.1 1.7 %collective-permute-start.11 = (bf16[304,128]{1,0:T(8,128)(2,1)S(1)}, bf16[304,128]{1,0:T(8,128)(2,1)S(1)}, u32[]{:S(2)}, u32[]{:S(2)}) collective-permute-start(bf16[304,128]{1,0:T(8,128)(2,1)S(1)} %pad_maximum_fusion.9), channel_id=1, source_target_pairs={{0,8},{1,5},{2,10},{3,7},{4,12},{5,1},{6,14},{7,3},{8,0},{9,13},{1... | collective-permute-start | bytes 233480 | tf_op jit(solution)/shard_map/ppermute | solution.py:354
  32.8 1.0 %collective-permute-done.4 = bf16[304,128]{1,0:T(8,128)(2,1)S(1)} collective-permute-done((bf16[304,128]{1,0:T(8,128)(2,1)S(1)}, bf16[304,128]{1,0:T(8,128)(2,1)S(1)}, u32[]{:S(2)}, u32[]{:S(2)}) %collective-permute-start.4) | collective-permute-done | bytes 77856 | tf_op jit(solution)/shard_map/ppermute | solution.py:354
  33.9 0.3 collective-permute-start.5
  34.2 3.5 %collective-permute-done.11 = bf16[304,128]{1,0:T(8,128)(2,1)S(1)} collective-permute-done((bf16[304,128]{1,0:T(8,128)(2,1)S(1)}, bf16[304,128]{1,0:T(8,128)(2,1)S(1)}, u32[]{:S(2)}, u32[]{:S(2)}) %collective-permute-start.11) | collective-permute-done | bytes 77856 | tf_op jit(solution)/shard_map/ppermute | solution.py:354
  37.8 0.1 collective-permute-start.12
  37.8 0.8 %collective-permute-done.5 = bf16[304,128]{1,0:T(8,128)(2,1)S(1)} collective-permute-done((bf16[304,128]{1,0:T(8,128)(2,1)S(1)}, bf16[304,128]{1,0:T(8,128)(2,1)S(1)}, u32[]{:S(2)}, u32[]{:S(2)}) %collective-permute-start.5) | collective-permute-done | bytes 77856 | tf_op jit(solution)/shard_map/ppermute | solution.py:354
  38.7 1.5 %collective-permute-start.6 = (bf16[288,128]{1,0:T(8,128)(2,1)S(1)}, bf16[288,128]{1,0:T(8,128)(2,1)S(1)}, u32[]{:S(2)}, u32[]{:S(2)}) collective-permute-start(bf16[288,128]{1,0:T(8,128)(2,1)S(1)} %fusion.3), channel_id=1, source_target_pairs={{0,2},{1,5},{2,0},{3,7},{4,6},{5,1},{6,4},{7,3},{8,10},{9,13},{10,... | collective-permute-start | bytes 221192 | tf_op jit(solution)/shard_map/ppermute | solution.py:354
  40.2 2.0 %collective-permute-done.12 = bf16[288,128]{1,0:T(8,128)(2,1)S(1)} collective-permute-done((bf16[288,128]{1,0:T(8,128)(2,1)S(1)}, bf16[288,128]{1,0:T(8,128)(2,1)S(1)}, u32[]{:S(2)}, u32[]{:S(2)}) %collective-permute-start.12) | collective-permute-done | bytes 73760 | tf_op jit(solution)/shard_map/ppermute | solution.py:354
  42.2 0.1 collective-permute-start.13
  42.3 0.8 %collective-permute-done.6 = bf16[288,128]{1,0:T(8,128)(2,1)S(1)} collective-permute-done((bf16[288,128]{1,0:T(8,128)(2,1)S(1)}, bf16[288,128]{1,0:T(8,128)(2,1)S(1)}, u32[]{:S(2)}, u32[]{:S(2)}) %collective-permute-start.6) | collective-permute-done | bytes 73760 | tf_op jit(solution)/shard_map/ppermute | solution.py:354
  43.1 0.1 collective-permute-start.7
  43.2 0.9 %multiply_reduce_fusion = f32[2,256,256]{2,1,0:T(8,128)} fusion(f32[2,2,256]{2,1,0:T(2,128)S(1)} %mul.32, f32[2,256]{1,0:T(2,128)S(1)} %get-tuple-element.36), kind=kLoop, calls=%fused_computation | loop fusion | flops 393216 | bytes 530432 | tf_op jit(solution)/shard_map/reduce_sum | solution.py:500
  44.2 0.0 collective-permute-done.13
  44.2 0.4 collective-permute-done.7
  44.6 0.1 broadcast_select_fusion.1
  44.7 1.1 %maximum_convert_fusion = f32[2,3,3,128,128]{4,3,2,1,0:T(8,128)} fusion(bf16[1,3,3,128,128]{4,3,2,1,0:T(8,128)(2,1)S(1)} %bitcast.6, bf16[1,3,3,128,128]{4,3,2,1,0:T(8,128)(2,1)S(1)} %bitcast.7), kind=kLoop, calls=%fused_computation.1 | loop fusion | flops 589824 | bytes 1769472 | tf_op jit(solution)/shard_map/convert_element_type | solution.py:501
  (44 shorter events, 0.7 us)
Async XLA Ops:
  0.6 8.0 %copy-start = (bf16[2,8,128,128]{3,2,1,0:T(8,128)(2,1)S(1)}, bf16[2,8,128,128]{3,2,1,0:T(8,128)(2,1)}, u32[]{:S(2)}) copy-start(bf16[2,8,128,128]{3,2,1,0:T(8,128)(2,1)} %dout.5) | copy-start | bytes 1572868
  0.6 0.7 %copy-start.1 = (s32[2]{0:T(128)S(1)}, s32[2]{0:T(128)}, u32[]{:S(2)}) copy-start(s32[2]{0:T(128)} %identity.3) | copy-start | bytes 28
  1.4 7.2 %copy-start.2 = (s32[2]{0:T(128)S(1)}, s32[2]{0:T(128)}, u32[]{:S(2)}) copy-start(s32[2]{0:T(128)} %identity.3) | copy-start | bytes 28
  1.4 7.2 %copy-start.3 = (bf16[2,3,3,128,128]{4,3,2,1,0:T(8,128)(2,1)S(1)}, bf16[2,3,3,128,128]{4,3,2,1,0:T(8,128)(2,1)}, u32[]{:S(2)}) copy-start(bf16[2,3,3,128,128]{4,3,2,1,0:T(8,128)(2,1)} %weights.3) | copy-start | bytes 1769476
  1.4 7.2 %copy-start.4 = (f32[2,256,256]{2,1,0:T(8,128)S(1)}, f32[2,256,256]{2,1,0:T(8,128)}, u32[]{:S(2)}) copy-start(f32[2,256,256]{2,1,0:T(8,128)} %film_w.1) | copy-start | bytes 1572868
  1.4 7.2 %copy-start.5 = (f32[64,256]{1,0:T(8,128)S(1)}, f32[64,256]{1,0:T(8,128)}, u32[]{:S(2)}) copy-start(f32[64,256]{1,0:T(8,128)} %audio.1) | copy-start | bytes 196612
  1.4 7.3 %copy-start.6 = (s32[2]{0:T(128)S(1)}, s32[2]{0:T(128)}, u32[]{:S(2)}) copy-start(s32[2]{0:T(128)} %audio_index.1) | copy-start | bytes 28
  3.1 10.4 %collective-permute-start = (bf16[2,4,128,128]{3,2,1,0:T(8,128)(2,1)S(1)}, bf16[2,4,128,128]{3,2,1,0:T(8,128)(2,1)S(1)}, u32[]{:S(2)}, u32[]{:S(2)}) collective-permute-start(bf16[2,4,128,128]{3,2,1,0:T(8,128)(2,1)S(1)} %get-tuple-element.20), channel_id=1, source_target_pairs={{0,15},{1,2},{2,1},{3,4},{4,3},{5,6},{6,5},{7,8},{8,7},{9,10},{10,... | collective-permute-start | bytes 786440 | tf_op jit(solution)/shard_map/ppermute | solution.py:433
  8.6 4.9 %collective-permute-start.1 = (bf16[2,4,128,128]{3,2,1,0:T(8,128)(2,1)S(1)}, bf16[2,4,128,128]{3,2,1,0:T(8,128)(2,1)S(1)}, u32[]{:S(2)}, u32[]{:S(2)}) collective-permute-start(bf16[2,4,128,128]{3,2,1,0:T(8,128)(2,1)S(1)} %get-tuple-element.21), channel_id=1, source_target_pairs={{0,1},{1,0},{2,3},{3,2},{4,5},{5,4},{6,7},{7,6},{8,9},{9,8},{10,11... | collective-permute-start | bytes 786440 | tf_op jit(solution)/shard_map/ppermute | solution.py:354
  18.7 1.8 %collective-permute-start.8 = (f32[584,128]{1,0:T(8,128)S(1)}, f32[584,128]{1,0:T(8,128)S(1)}, u32[]{:S(2)}, u32[]{:S(2)}) collective-permute-start(f32[584,128]{1,0:T(8,128)S(1)} %get-tuple-element.35), channel_id=1, source_target_pairs={{0,1},{1,0},{2,3},{3,2},{4,5},{5,4},{6,7},{7,6},{8,9},{9,8},{10,11... | collective-permute-start | bytes 897032 | tf_op jit(solution)/shard_map/ppermute | solution.py:354
  19.3 1.6 %collective-permute-start.2 = (f32[584,128]{1,0:T(8,128)S(1)}, f32[584,128]{1,0:T(8,128)S(1)}, u32[]{:S(2)}, u32[]{:S(2)}) collective-permute-start(f32[584,128]{1,0:T(8,128)S(1)} %get-tuple-element.33), channel_id=1, source_target_pairs={{0,1},{1,0},{2,3},{3,2},{4,5},{5,4},{6,7},{7,6},{8,9},{9,8},{10,11... | collective-permute-start | bytes 897032 | tf_op jit(solution)/shard_map/ppermute | solution.py:354
  21.1 5.2 %collective-permute-start.9 = (bf16[304,128]{1,0:T(8,128)(2,1)S(1)}, bf16[304,128]{1,0:T(8,128)(2,1)S(1)}, u32[]{:S(2)}, u32[]{:S(2)}) collective-permute-start(bf16[304,128]{1,0:T(8,128)(2,1)S(1)} %pad_maximum_fusion.7), channel_id=1, source_target_pairs={{0,4},{1,3},{2,6},{3,1},{4,0},{5,7},{6,2},{7,5},{8,12},{9,11},{10,... | collective-permute-start | bytes 233480 | tf_op jit(solution)/shard_map/ppermute | solution.py:354
  21.8 5.6 %collective-permute-start.3 = (bf16[304,128]{1,0:T(8,128)(2,1)S(1)}, bf16[304,128]{1,0:T(8,128)(2,1)S(1)}, u32[]{:S(2)}, u32[]{:S(2)}) collective-permute-start(bf16[304,128]{1,0:T(8,128)(2,1)S(1)} %pad_maximum_fusion.4), channel_id=1, source_target_pairs={{0,2},{1,5},{2,0},{3,7},{4,6},{5,1},{6,4},{7,3},{8,10},{9,13},{10,... | collective-permute-start | bytes 233480 | tf_op jit(solution)/shard_map/ppermute | solution.py:354
  26.4 4.6 %collective-permute-start.10 = (bf16[304,128]{1,0:T(8,128)(2,1)S(1)}, bf16[304,128]{1,0:T(8,128)(2,1)S(1)}, u32[]{:S(2)}, u32[]{:S(2)}) collective-permute-start(bf16[304,128]{1,0:T(8,128)(2,1)S(1)} %pad_maximum_fusion.8), channel_id=1, source_target_pairs={{0,2},{1,9},{2,0},{3,11},{4,6},{5,13},{6,4},{7,15},{8,10},{9,1},{1... | collective-permute-start | bytes 233480 | tf_op jit(solution)/shard_map/ppermute | solution.py:354
  27.6 6.3 %collective-permute-start.4 = (bf16[304,128]{1,0:T(8,128)(2,1)S(1)}, bf16[304,128]{1,0:T(8,128)(2,1)S(1)}, u32[]{:S(2)}, u32[]{:S(2)}) collective-permute-start(bf16[304,128]{1,0:T(8,128)(2,1)S(1)} %pad_maximum_fusion.5), channel_id=1, source_target_pairs={{0,8},{1,3},{2,10},{3,1},{4,12},{5,7},{6,14},{7,5},{8,0},{9,11},{1... | collective-permute-start | bytes 233480 | tf_op jit(solution)/shard_map/ppermute | solution.py:354
  31.1 6.5 %collective-permute-start.11 = (bf16[304,128]{1,0:T(8,128)(2,1)S(1)}, bf16[304,128]{1,0:T(8,128)(2,1)S(1)}, u32[]{:S(2)}, u32[]{:S(2)}) collective-permute-start(bf16[304,128]{1,0:T(8,128)(2,1)S(1)} %pad_maximum_fusion.9), channel_id=1, source_target_pairs={{0,8},{1,5},{2,10},{3,7},{4,12},{5,1},{6,14},{7,3},{8,0},{9,13},{1... | collective-permute-start | bytes 233480 | tf_op jit(solution)/shard_map/ppermute | solution.py:354
  33.9 4.7 %collective-permute-start.5 = (bf16[304,128]{1,0:T(8,128)(2,1)S(1)}, bf16[304,128]{1,0:T(8,128)(2,1)S(1)}, u32[]{:S(2)}, u32[]{:S(2)}) collective-permute-start(bf16[304,128]{1,0:T(8,128)(2,1)S(1)} %pad_maximum_fusion.6), channel_id=1, source_target_pairs={{0,4},{1,9},{2,6},{3,11},{4,0},{5,13},{6,2},{7,15},{8,12},{9,1},{1... | collective-permute-start | bytes 233480 | tf_op jit(solution)/shard_map/ppermute | solution.py:354
  37.8 4.4 %collective-permute-start.12 = (bf16[288,128]{1,0:T(8,128)(2,1)S(1)}, bf16[288,128]{1,0:T(8,128)(2,1)S(1)}, u32[]{:S(2)}, u32[]{:S(2)}) collective-permute-start(bf16[288,128]{1,0:T(8,128)(2,1)S(1)} %fusion), channel_id=1, source_target_pairs={{0,4},{1,3},{2,6},{3,1},{4,0},{5,7},{6,2},{7,5},{8,12},{9,11},{10,... | collective-permute-start | bytes 221192 | tf_op jit(solution)/shard_map/ppermute | solution.py:354
  38.7 4.4 %collective-permute-start.6 = (bf16[288,128]{1,0:T(8,128)(2,1)S(1)}, bf16[288,128]{1,0:T(8,128)(2,1)S(1)}, u32[]{:S(2)}, u32[]{:S(2)}) collective-permute-start(bf16[288,128]{1,0:T(8,128)(2,1)S(1)} %fusion.3), channel_id=1, source_target_pairs={{0,2},{1,5},{2,0},{3,7},{4,6},{5,1},{6,4},{7,3},{8,10},{9,13},{10,... | collective-permute-start | bytes 221192 | tf_op jit(solution)/shard_map/ppermute | solution.py:354
  42.2 1.9 %collective-permute-start.13 = (bf16[576,128]{1,0:T(8,128)(2,1)S(1)}, bf16[576,128]{1,0:T(8,128)(2,1)S(1)}, u32[]{:S(2)}, u32[]{:S(2)}) collective-permute-start(bf16[576,128]{1,0:T(8,128)(2,1)S(1)} %pad_maximum_fusion.3), channel_id=1, source_target_pairs={{0,1},{1,0},{2,3},{3,2},{4,5},{5,4},{6,7},{7,6},{8,9},{9,8},{10,11... | collective-permute-start | bytes 442376 | tf_op jit(solution)/shard_map/ppermute | solution.py:354
  43.1 1.4 %collective-permute-start.7 = (bf16[576,128]{1,0:T(8,128)(2,1)S(1)}, bf16[576,128]{1,0:T(8,128)(2,1)S(1)}, u32[]{:S(2)}, u32[]{:S(2)}) collective-permute-start(bf16[576,128]{1,0:T(8,128)(2,1)S(1)} %pad_maximum_fusion.2), channel_id=1, source_target_pairs={{0,1},{1,0},{2,3},{3,2},{4,5},{5,4},{6,7},{7,6},{8,9},{9,8},{10,11... | collective-permute-start | bytes 442376 | tf_op jit(solution)/shard_map/ppermute | solution.py:354

commit v4 on v3

--- a/solution.py
+++ b/solution.py
@@ -143,11 +143,15 @@
         whole[a * size : (a + 1) * size, :] = totals[a].T
     low, high = whole[:half, :], whole[half:, :]
     keep[:half, :] = jnp.where(mine == 0, low, high)
-    send[:half, :] = jnp.where(mine == 0, high, low)
+    send[:half, :] = jnp.where(mine == 0, high, low).astype(BF16)
     tail = keep.shape[0] - half
-    padded = jnp.concatenate([stats, jnp.zeros((tail - stats.shape[0], stats.shape[1]), F32)], axis=0)
-    keep[half:, :] = padded
-    send[half:, :] = padded
+    if tail > stats.shape[0]:
+        blank = jnp.zeros((tail - stats.shape[0], stats.shape[1]), F32)
+        stats = jnp.concatenate([stats, blank], axis=0)
+    coarse = stats.astype(BF16)
+    rest = (stats - coarse.astype(F32)).astype(BF16)
+    keep[half:, :] = coarse.astype(F32) + rest.astype(F32)
+    send[half:, :] = jnp.concatenate([coarse, rest], axis=0)
 
 
 def edge_kernel(identity, maps, dout, outer, inner, sems):
@@ -399,8 +403,10 @@
     orders = [list(zip(one, other)), list(zip(other, one))]
     state = []
     for keep, send in messages:
-        total = keep + swap(send, (1, 1))
-        state.append((total[:half], total[half:]))
+        other = swap(send, (1, 1)).astype(F32)
+        tail = keep.shape[0] - half
+        stats = keep[half:] + (other[half : half + tail] + other[half + tail :])
+        state.append((keep[:half] + other[:half], stats))
     for step in range(len(bits)):
         for s in range(2):
             state[s] = exchange(*state[s], orders[s][step], step == 0)
@@ -474,13 +480,14 @@
         room=46,
     )
     half = 9 * channels // 2
-    message = ((half + 8, channels), F32)
+    tail = (2 * frames + 7) // 8 * 8
+    message = [((half + tail, channels), F32), ((half + 2 * tail, channels), BF16)]
     whole = pltpu.VMEM((9 * channels, channels), F32)
     decoded, keep_1, send_1, keep_0, send_0 = call(
         functools.partial(rim_kernel, factor),
         "rim_columns",
         [VMEM] * 13,
-        [(dout.shape, BF16)] + [message] * 4,
+        [(dout.shape, BF16)] + message * 2,
         (outer, inner, dout, conv_w, film, stack_0, stack_1, stack_d, pre_0, decoded_a)
         + (taps_0, taps_1, stats_a),
         [

time: 46 us -> 45.5 us (0.989)
  no operation moved by 1% of the time
where the time goes in v4:
time: 45.5 us; the launch traced here: 45.3 us
  starting transfers between devices  15.5 us (34%)
  waiting for transfers between devices  13.7 us (30%)
  Pallas kernels  11.6 us (25%)
  other arithmetic  2.76 us (6%)
  between operations  1.03 us (2%)
  local copies, waits for them, and re-layouts  0.77 us (2%)
    ppermute x13, waiting for transfers between devices, swap(): lax.ppermute(value, AXIS, [(i, i ^ bits[i % 2]) for i in range(count)])  13.7 us
    pallas_call x3, Pallas kernels, call(): pl.pallas_call(kernel, out_shape=tuple((jax.ShapeDtypeStruct(shape, dtype...  11.6 us
    ppermute x13, starting transfers between devices, swap(): lax.ppermute(value, AXIS, [(i, i ^ bits[i % 2]) for i in range(count)])  10 us
    ppermute x1, starting transfers between devices, local(): outer = lax.ppermute(outer, AXIS, pairs)  5.48 us
    convert_element_type x1, other arithmetic, local(): jnp.stack([sum_0, sum_1]).astype(F32)  1.09 us
    reduce_sum x1, other arithmetic, local(): film_grad = jnp.sum(audio_rows[None, :, :, None] * totals, axis=1)  0.93 us
  transfers between devices with their start and end apart: 14, of which 10 were waited for; matrix products, arithmetic and copies ran while one was open for 3% of the time, Pallas kernels for 11%

profile of v4, /device:TPU:0, one launch (start us, length us, event | category | flops | bytes accessed | tf_op | source)
XLA Modules:
  0.0 45.3 jit_solution(12085376032337884535)
XLA Ops:
  0.6 0.0 copy-start
  0.6 0.0 copy-start.1
  0.7 0.7 %copy-done.1 = s32[2]{0:T(128)S(1)} copy-done((s32[2]{0:T(128)S(1)}, s32[2]{0:T(128)}, u32[]{:S(2)}) %copy-start.1) | copy-done | bytes 32
  1.4 0.0 copy-start.2
  1.4 0.0 copy-start.3
  1.4 0.0 copy-start.4
  1.4 0.0 copy-start.5
  1.4 0.0 copy-start.6
  1.4 1.7 %edges.1 = (bf16[2,4,128,128]{3,2,1,0:T(8,128)(2,1)S(1)}, bf16[2,4,128,128]{3,2,1,0:T(8,128)(2,1)S(1)}) custom-call(s32[2]{0:T(128)S(1)} %copy-done.1, bf16[8,8,128,128]{3,2,1,0:T(8,128)(2,1)} %maps.3, bf16[2,8,128,128]{3,2,1,0:T(8,128)(2,1)} %dout.5), custom_call_target="tpu_custom_call" | custom-call | bytes 4194304 | tf_op jit(solution)/shard_map/edges/pallas_call | solution.py:344
  3.1 5.5 %collective-permute-start = (bf16[2,4,128,128]{3,2,1,0:T(8,128)(2,1)S(1)}, bf16[2,4,128,128]{3,2,1,0:T(8,128)(2,1)S(1)}, u32[]{:S(2)}, u32[]{:S(2)}) collective-permute-start(bf16[2,4,128,128]{3,2,1,0:T(8,128)(2,1)S(1)} %get-tuple-element.20), channel_id=1, source_target_pairs={{0,15},{1,2},{2,1},{3,4},{4,3},{5,6},{6,5},{7,8},{8,7},{9,10},{10,... | collective-permute-start | bytes 786440 | tf_op jit(solution)/shard_map/ppermute | solution.py:439
  8.6 0.0 collective-permute-start.1
  8.6 0.0 copy-done
  8.6 0.0 copy-done.2
  8.6 0.0 copy-done.3
  8.6 0.0 copy-done.4
  8.6 0.0 copy-done.5
  8.6 0.0 copy-done.6
  8.6 4.8 %inner_columns.1 = (f32[2,2,256]{2,1,0:T(2,128)S(1)}, f32[2,256]{1,0:T(2,128)S(1)}, bf16[2,8,128,384]{3,2,1,0:T(8,128)(2,1)S(1)}, bf16[2,6,128,384]{3,2,1,0:T(8,...) custom-call(s32[2]{0:T(128)S(1)} %copy-done.2, ...), custom_call_target="tpu_custom_call" | custom-call | flops 1358954496 | bytes 4194304 | tf_op jit(solution)/shard_map/inner_columns/pallas_call | solution.py:344
  13.5 0.0 collective-permute-done.outer
  13.5 0.0 collective-permute-done.1.inner
  13.5 5.0 %rim_columns.1 = (bf16[2,8,128,128]{3,2,1,0:T(8,128)(2,1)}, f32[584,128]{1,0:T(8,128)S(1)}, bf16[592,128]{1,0:T(8,128)(2,1)S(1)}, f32[584,128]{1,0:T(8,128)S(1)}, bf16[592,128]{1,0:T(8,128)(2,1)S(1)}) custom-call(bf16[2,4,128,128]{3,2,1,0:T(8,128)(2,1)S(1)} %collective-permute-done.outer, bf16[2,4,128,128]{3,2,1,0:T(8,128)(2,1)S(1)} %collective-permute-done.1.inner, ...), custom_call_target="tpu_custom_call" | custom-call | flops 2113929216 | bytes 4194304 | tf_op jit(solution)/shard_map/rim_columns/pallas_call | solution.py:344
  18.5 0.6 %collective-permute-start.8 = (bf16[592,128]{1,0:T(8,128)(2,1)S(1)}, bf16[592,128]{1,0:T(8,128)(2,1)S(1)}, u32[]{:S(2)}, u32[]{:S(2)}) collective-permute-start(bf16[592,128]{1,0:T(8,128)(2,1)S(1)} %get-tuple-element.35), channel_id=1, source_target_pairs={{0,1},{1,0},{2,3},{3,2},{4,5},{5,4},{6,7},{7,6},{8,9},{9,8},{10,11... | collective-permute-start | bytes 454664 | tf_op jit(solution)/shard_map/ppermute | solution.py:358
  19.1 0.2 collective-permute-start.2
  19.2 0.8 %collective-permute-done.8 = bf16[592,128]{1,0:T(8,128)(2,1)S(1)} collective-permute-done((bf16[592,128]{1,0:T(8,128)(2,1)S(1)}, bf16[592,128]{1,0:T(8,128)(2,1)S(1)}, u32[]{:S(2)}, u32[]{:S(2)}) %collective-permute-start.8) | collective-permute-done | bytes 151584 | tf_op jit(solution)/shard_map/ppermute | solution.py:358
  20.2 0.3 collective-permute-done.2
  20.6 0.7 %collective-permute-start.9 = (bf16[304,128]{1,0:T(8,128)(2,1)S(1)}, bf16[304,128]{1,0:T(8,128)(2,1)S(1)}, u32[]{:S(2)}, u32[]{:S(2)}) collective-permute-start(bf16[304,128]{1,0:T(8,128)(2,1)S(1)} %pad_maximum_fusion.7), channel_id=1, source_target_pairs={{0,4},{1,3},{2,6},{3,1},{4,0},{5,7},{6,2},{7,5},{8,12},{9,11},{10,... | collective-permute-start | bytes 233480 | tf_op jit(solution)/shard_map/ppermute | solution.py:358
  21.3 1.9 %collective-permute-start.3 = (bf16[304,128]{1,0:T(8,128)(2,1)S(1)}, bf16[304,128]{1,0:T(8,128)(2,1)S(1)}, u32[]{:S(2)}, u32[]{:S(2)}) collective-permute-start(bf16[304,128]{1,0:T(8,128)(2,1)S(1)} %pad_maximum_fusion.4), channel_id=1, source_target_pairs={{0,2},{1,5},{2,0},{3,7},{4,6},{5,1},{6,4},{7,3},{8,10},{9,13},{10,... | collective-permute-start | bytes 233480 | tf_op jit(solution)/shard_map/ppermute | solution.py:358
  23.3 2.6 %collective-permute-done.9 = bf16[304,128]{1,0:T(8,128)(2,1)S(1)} collective-permute-done((bf16[304,128]{1,0:T(8,128)(2,1)S(1)}, bf16[304,128]{1,0:T(8,128)(2,1)S(1)}, u32[]{:S(2)}, u32[]{:S(2)}) %collective-permute-start.9) | collective-permute-done | bytes 77856 | tf_op jit(solution)/shard_map/ppermute | solution.py:358
  25.9 0.9 %collective-permute-start.10 = (bf16[304,128]{1,0:T(8,128)(2,1)S(1)}, bf16[304,128]{1,0:T(8,128)(2,1)S(1)}, u32[]{:S(2)}, u32[]{:S(2)}) collective-permute-start(bf16[304,128]{1,0:T(8,128)(2,1)S(1)} %pad_maximum_fusion.8), channel_id=1, source_target_pairs={{0,2},{1,9},{2,0},{3,11},{4,6},{5,13},{6,4},{7,15},{8,10},{9,1},{1... | collective-permute-start | bytes 233480 | tf_op jit(solution)/shard_map/ppermute | solution.py:358
  26.8 0.0 collective-permute-done.3
  26.9 2.3 %collective-permute-start.4 = (bf16[304,128]{1,0:T(8,128)(2,1)S(1)}, bf16[304,128]{1,0:T(8,128)(2,1)S(1)}, u32[]{:S(2)}, u32[]{:S(2)}) collective-permute-start(bf16[304,128]{1,0:T(8,128)(2,1)S(1)} %pad_maximum_fusion.5), channel_id=1, source_target_pairs={{0,8},{1,3},{2,10},{3,1},{4,12},{5,7},{6,14},{7,5},{8,0},{9,11},{1... | collective-permute-start | bytes 233480 | tf_op jit(solution)/shard_map/ppermute | solution.py:358
  29.2 1.4 %collective-permute-done.10 = bf16[304,128]{1,0:T(8,128)(2,1)S(1)} collective-permute-done((bf16[304,128]{1,0:T(8,128)(2,1)S(1)}, bf16[304,128]{1,0:T(8,128)(2,1)S(1)}, u32[]{:S(2)}, u32[]{:S(2)}) %collective-permute-start.10) | collective-permute-done | bytes 77856 | tf_op jit(solution)/shard_map/ppermute | solution.py:358
  30.7 1.7 %collective-permute-start.11 = (bf16[304,128]{1,0:T(8,128)(2,1)S(1)}, bf16[304,128]{1,0:T(8,128)(2,1)S(1)}, u32[]{:S(2)}, u32[]{:S(2)}) collective-permute-start(bf16[304,128]{1,0:T(8,128)(2,1)S(1)} %pad_maximum_fusion.9), channel_id=1, source_target_pairs={{0,8},{1,5},{2,10},{3,7},{4,12},{5,1},{6,14},{7,3},{8,0},{9,13},{1... | collective-permute-start | bytes 233480 | tf_op jit(solution)/shard_map/ppermute | solution.py:358
  32.4 0.8 %collective-permute-done.4 = bf16[304,128]{1,0:T(8,128)(2,1)S(1)} collective-permute-done((bf16[304,128]{1,0:T(8,128)(2,1)S(1)}, bf16[304,128]{1,0:T(8,128)(2,1)S(1)}, u32[]{:S(2)}, u32[]{:S(2)}) %collective-permute-start.4) | collective-permute-done | bytes 77856 | tf_op jit(solution)/shard_map/ppermute | solution.py:358
  33.3 0.5 collective-permute-start.5
  33.7 3.4 %collective-permute-done.11 = bf16[304,128]{1,0:T(8,128)(2,1)S(1)} collective-permute-done((bf16[304,128]{1,0:T(8,128)(2,1)S(1)}, bf16[304,128]{1,0:T(8,128)(2,1)S(1)}, u32[]{:S(2)}, u32[]{:S(2)}) %collective-permute-start.11) | collective-permute-done | bytes 77856 | tf_op jit(solution)/shard_map/ppermute | solution.py:358
  37.2 0.1 collective-permute-start.12
  37.2 0.8 %collective-permute-done.5 = bf16[304,128]{1,0:T(8,128)(2,1)S(1)} collective-permute-done((bf16[304,128]{1,0:T(8,128)(2,1)S(1)}, bf16[304,128]{1,0:T(8,128)(2,1)S(1)}, u32[]{:S(2)}, u32[]{:S(2)}) %collective-permute-start.5) | collective-permute-done | bytes 77856 | tf_op jit(solution)/shard_map/ppermute | solution.py:358
  38.1 1.1 %collective-permute-start.6 = (bf16[288,128]{1,0:T(8,128)(2,1)S(1)}, bf16[288,128]{1,0:T(8,128)(2,1)S(1)}, u32[]{:S(2)}, u32[]{:S(2)}) collective-permute-start(bf16[288,128]{1,0:T(8,128)(2,1)S(1)} %fusion.3), channel_id=1, source_target_pairs={{0,2},{1,5},{2,0},{3,7},{4,6},{5,1},{6,4},{7,3},{8,10},{9,13},{10,... | collective-permute-start | bytes 221192 | tf_op jit(solution)/shard_map/ppermute | solution.py:358
  39.3 2.3 %collective-permute-done.12 = bf16[288,128]{1,0:T(8,128)(2,1)S(1)} collective-permute-done((bf16[288,128]{1,0:T(8,128)(2,1)S(1)}, bf16[288,128]{1,0:T(8,128)(2,1)S(1)}, u32[]{:S(2)}, u32[]{:S(2)}) %collective-permute-start.12) | collective-permute-done | bytes 73760 | tf_op jit(solution)/shard_map/ppermute | solution.py:358
  41.6 0.1 collective-permute-start.13
  41.7 0.9 %collective-permute-done.6 = bf16[288,128]{1,0:T(8,128)(2,1)S(1)} collective-permute-done((bf16[288,128]{1,0:T(8,128)(2,1)S(1)}, bf16[288,128]{1,0:T(8,128)(2,1)S(1)}, u32[]{:S(2)}, u32[]{:S(2)}) %collective-permute-start.6) | collective-permute-done | bytes 73760 | tf_op jit(solution)/shard_map/ppermute | solution.py:358
  42.6 0.1 collective-permute-start.7
  42.7 0.9 %multiply_reduce_fusion = f32[2,256,256]{2,1,0:T(8,128)} fusion(f32[2,2,256]{2,1,0:T(2,128)S(1)} %mul.32, f32[2,256]{1,0:T(2,128)S(1)} %get-tuple-element.36), kind=kLoop, calls=%fused_computation | loop fusion | flops 393216 | bytes 530432 | tf_op jit(solution)/shard_map/reduce_sum | solution.py:507
  43.6 0.0 collective-permute-done.13
  43.6 0.4 collective-permute-done.7
  44.0 0.1 broadcast_select_fusion.1
  44.2 1.1 %maximum_convert_fusion = f32[2,3,3,128,128]{4,3,2,1,0:T(8,128)} fusion(bf16[1,3,3,128,128]{4,3,2,1,0:T(8,128)(2,1)S(1)} %bitcast.6, bf16[1,3,3,128,128]{4,3,2,1,0:T(8,128)(2,1)S(1)} %bitcast.7), kind=kLoop, calls=%fused_computation.1 | loop fusion | flops 589824 | bytes 1769472 | tf_op jit(solution)/shard_map/convert_element_type | solution.py:508
  (46 shorter events, 0.7 us)
Async XLA Ops:
  0.6 8.0 %copy-start = (bf16[2,8,128,128]{3,2,1,0:T(8,128)(2,1)S(1)}, bf16[2,8,128,128]{3,2,1,0:T(8,128)(2,1)}, u32[]{:S(2)}) copy-start(bf16[2,8,128,128]{3,2,1,0:T(8,128)(2,1)} %dout.5) | copy-start | bytes 1572868
  0.6 0.7 %copy-start.1 = (s32[2]{0:T(128)S(1)}, s32[2]{0:T(128)}, u32[]{:S(2)}) copy-start(s32[2]{0:T(128)} %identity.3) | copy-start | bytes 28
  1.4 7.2 %copy-start.2 = (s32[2]{0:T(128)S(1)}, s32[2]{0:T(128)}, u32[]{:S(2)}) copy-start(s32[2]{0:T(128)} %identity.3) | copy-start | bytes 28
  1.4 7.2 %copy-start.3 = (bf16[2,3,3,128,128]{4,3,2,1,0:T(8,128)(2,1)S(1)}, bf16[2,3,3,128,128]{4,3,2,1,0:T(8,128)(2,1)}, u32[]{:S(2)}) copy-start(bf16[2,3,3,128,128]{4,3,2,1,0:T(8,128)(2,1)} %weights.3) | copy-start | bytes 1769476
  1.4 7.2 %copy-start.4 = (f32[2,256,256]{2,1,0:T(8,128)S(1)}, f32[2,256,256]{2,1,0:T(8,128)}, u32[]{:S(2)}) copy-start(f32[2,256,256]{2,1,0:T(8,128)} %film_w.1) | copy-start | bytes 1572868
  1.4 7.2 %copy-start.5 = (f32[64,256]{1,0:T(8,128)S(1)}, f32[64,256]{1,0:T(8,128)}, u32[]{:S(2)}) copy-start(f32[64,256]{1,0:T(8,128)} %audio.1) | copy-start | bytes 196612
  1.4 7.3 %copy-start.6 = (s32[2]{0:T(128)S(1)}, s32[2]{0:T(128)}, u32[]{:S(2)}) copy-start(s32[2]{0:T(128)} %audio_index.1) | copy-start | bytes 28
  3.1 10.4 %collective-permute-start = (bf16[2,4,128,128]{3,2,1,0:T(8,128)(2,1)S(1)}, bf16[2,4,128,128]{3,2,1,0:T(8,128)(2,1)S(1)}, u32[]{:S(2)}, u32[]{:S(2)}) collective-permute-start(bf16[2,4,128,128]{3,2,1,0:T(8,128)(2,1)S(1)} %get-tuple-element.20), channel_id=1, source_target_pairs={{0,15},{1,2},{2,1},{3,4},{4,3},{5,6},{6,5},{7,8},{8,7},{9,10},{10,... | collective-permute-start | bytes 786440 | tf_op jit(solution)/shard_map/ppermute | solution.py:439
  8.6 4.9 %collective-permute-start.1 = (bf16[2,4,128,128]{3,2,1,0:T(8,128)(2,1)S(1)}, bf16[2,4,128,128]{3,2,1,0:T(8,128)(2,1)S(1)}, u32[]{:S(2)}, u32[]{:S(2)}) collective-permute-start(bf16[2,4,128,128]{3,2,1,0:T(8,128)(2,1)S(1)} %get-tuple-element.21), channel_id=1, source_target_pairs={{0,1},{1,0},{2,3},{3,2},{4,5},{5,4},{6,7},{7,6},{8,9},{9,8},{10,11... | collective-permute-start | bytes 786440 | tf_op jit(solution)/shard_map/ppermute | solution.py:358
  18.5 1.6 %collective-permute-start.8 = (bf16[592,128]{1,0:T(8,128)(2,1)S(1)}, bf16[592,128]{1,0:T(8,128)(2,1)S(1)}, u32[]{:S(2)}, u32[]{:S(2)}) collective-permute-start(bf16[592,128]{1,0:T(8,128)(2,1)S(1)} %get-tuple-element.35), channel_id=1, source_target_pairs={{0,1},{1,0},{2,3},{3,2},{4,5},{5,4},{6,7},{7,6},{8,9},{9,8},{10,11... | collective-permute-start | bytes 454664 | tf_op jit(solution)/shard_map/ppermute | solution.py:358
  19.1 1.4 %collective-permute-start.2 = (bf16[592,128]{1,0:T(8,128)(2,1)S(1)}, bf16[592,128]{1,0:T(8,128)(2,1)S(1)}, u32[]{:S(2)}, u32[]{:S(2)}) collective-permute-start(bf16[592,128]{1,0:T(8,128)(2,1)S(1)} %get-tuple-element.33), channel_id=1, source_target_pairs={{0,1},{1,0},{2,3},{3,2},{4,5},{5,4},{6,7},{7,6},{8,9},{9,8},{10,11... | collective-permute-start | bytes 454664 | tf_op jit(solution)/shard_map/ppermute | solution.py:358
  20.6 5.2 %collective-permute-start.9 = (bf16[304,128]{1,0:T(8,128)(2,1)S(1)}, bf16[304,128]{1,0:T(8,128)(2,1)S(1)}, u32[]{:S(2)}, u32[]{:S(2)}) collective-permute-start(bf16[304,128]{1,0:T(8,128)(2,1)S(1)} %pad_maximum_fusion.7), channel_id=1, source_target_pairs={{0,4},{1,3},{2,6},{3,1},{4,0},{5,7},{6,2},{7,5},{8,12},{9,11},{10,... | collective-permute-start | bytes 233480 | tf_op jit(solution)/shard_map/ppermute | solution.py:358
  21.3 5.5 %collective-permute-start.3 = (bf16[304,128]{1,0:T(8,128)(2,1)S(1)}, bf16[304,128]{1,0:T(8,128)(2,1)S(1)}, u32[]{:S(2)}, u32[]{:S(2)}) collective-permute-start(bf16[304,128]{1,0:T(8,128)(2,1)S(1)} %pad_maximum_fusion.4), channel_id=1, source_target_pairs={{0,2},{1,5},{2,0},{3,7},{4,6},{5,1},{6,4},{7,3},{8,10},{9,13},{10,... | collective-permute-start | bytes 233480 | tf_op jit(solution)/shard_map/ppermute | solution.py:358
  25.9 4.7 %collective-permute-start.10 = (bf16[304,128]{1,0:T(8,128)(2,1)S(1)}, bf16[304,128]{1,0:T(8,128)(2,1)S(1)}, u32[]{:S(2)}, u32[]{:S(2)}) collective-permute-start(bf16[304,128]{1,0:T(8,128)(2,1)S(1)} %pad_maximum_fusion.8), channel_id=1, source_target_pairs={{0,2},{1,9},{2,0},{3,11},{4,6},{5,13},{6,4},{7,15},{8,10},{9,1},{1... | collective-permute-start | bytes 233480 | tf_op jit(solution)/shard_map/ppermute | solution.py:358
  26.9 6.3 %collective-permute-start.4 = (bf16[304,128]{1,0:T(8,128)(2,1)S(1)}, bf16[304,128]{1,0:T(8,128)(2,1)S(1)}, u32[]{:S(2)}, u32[]{:S(2)}) collective-permute-start(bf16[304,128]{1,0:T(8,128)(2,1)S(1)} %pad_maximum_fusion.5), channel_id=1, source_target_pairs={{0,8},{1,3},{2,10},{3,1},{4,12},{5,7},{6,14},{7,5},{8,0},{9,11},{1... | collective-permute-start | bytes 233480 | tf_op jit(solution)/shard_map/ppermute | solution.py:358
  30.7 6.4 %collective-permute-start.11 = (bf16[304,128]{1,0:T(8,128)(2,1)S(1)}, bf16[304,128]{1,0:T(8,128)(2,1)S(1)}, u32[]{:S(2)}, u32[]{:S(2)}) collective-permute-start(bf16[304,128]{1,0:T(8,128)(2,1)S(1)} %pad_maximum_fusion.9), channel_id=1, source_target_pairs={{0,8},{1,5},{2,10},{3,7},{4,12},{5,1},{6,14},{7,3},{8,0},{9,13},{1... | collective-permute-start | bytes 233480 | tf_op jit(solution)/shard_map/ppermute | solution.py:358
  33.3 4.8 %collective-permute-start.5 = (bf16[304,128]{1,0:T(8,128)(2,1)S(1)}, bf16[304,128]{1,0:T(8,128)(2,1)S(1)}, u32[]{:S(2)}, u32[]{:S(2)}) collective-permute-start(bf16[304,128]{1,0:T(8,128)(2,1)S(1)} %pad_maximum_fusion.6), channel_id=1, source_target_pairs={{0,4},{1,9},{2,6},{3,11},{4,0},{5,13},{6,2},{7,15},{8,12},{9,1},{1... | collective-permute-start | bytes 233480 | tf_op jit(solution)/shard_map/ppermute | solution.py:358
  37.2 4.4 %collective-permute-start.12 = (bf16[288,128]{1,0:T(8,128)(2,1)S(1)}, bf16[288,128]{1,0:T(8,128)(2,1)S(1)}, u32[]{:S(2)}, u32[]{:S(2)}) collective-permute-start(bf16[288,128]{1,0:T(8,128)(2,1)S(1)} %fusion), channel_id=1, source_target_pairs={{0,4},{1,3},{2,6},{3,1},{4,0},{5,7},{6,2},{7,5},{8,12},{9,11},{10,... | collective-permute-start | bytes 221192 | tf_op jit(solution)/shard_map/ppermute | solution.py:358
  38.1 4.4 %collective-permute-start.6 = (bf16[288,128]{1,0:T(8,128)(2,1)S(1)}, bf16[288,128]{1,0:T(8,128)(2,1)S(1)}, u32[]{:S(2)}, u32[]{:S(2)}) collective-permute-start(bf16[288,128]{1,0:T(8,128)(2,1)S(1)} %fusion.3), channel_id=1, source_target_pairs={{0,2},{1,5},{2,0},{3,7},{4,6},{5,1},{6,4},{7,3},{8,10},{9,13},{10,... | collective-permute-start | bytes 221192 | tf_op jit(solution)/shard_map/ppermute | solution.py:358
  41.6 2.0 %collective-permute-start.13 = (bf16[576,128]{1,0:T(8,128)(2,1)S(1)}, bf16[576,128]{1,0:T(8,128)(2,1)S(1)}, u32[]{:S(2)}, u32[]{:S(2)}) collective-permute-start(bf16[576,128]{1,0:T(8,128)(2,1)S(1)} %pad_maximum_fusion.3), channel_id=1, source_target_pairs={{0,1},{1,0},{2,3},{3,2},{4,5},{5,4},{6,7},{7,6},{8,9},{9,8},{10,11... | collective-permute-start | bytes 442376 | tf_op jit(solution)/shard_map/ppermute | solution.py:358
  42.6 1.4 %collective-permute-start.7 = (bf16[576,128]{1,0:T(8,128)(2,1)S(1)}, bf16[576,128]{1,0:T(8,128)(2,1)S(1)}, u32[]{:S(2)}, u32[]{:S(2)}) collective-permute-start(bf16[576,128]{1,0:T(8,128)(2,1)S(1)} %pad_maximum_fusion.2), channel_id=1, source_target_pairs={{0,1},{1,0},{2,3},{3,2},{4,5},{5,4},{6,7},{7,6},{8,9},{9,8},{10,11... | collective-permute-start | bytes 442376 | tf_op jit(solution)/shard_map/ppermute | solution.py:358

commit v5 on v4

--- a/solution.py
+++ b/solution.py
@@ -313,11 +313,12 @@
     sums_0, sums_1 = Sums(), Sums()
     edges = Edges()
     for f in range(frames):
-        both_1(factor, film, weights, h_1, edges, out, d_1, f, [-1, last + 1], rows)
         some = [0, 1, last - 1, last]
         sums_1.add(
             f, some, rows, *both_1(factor, film, weights, h_1, edges, out, d_1, f, some, rows)
         )
+    for f in range(frames):
+        both_1(factor, film, weights, h_1, edges, out, d_1, f, [-1, last + 1], rows)
     ends = [
         pltpu.make_async_copy(
             hidden.at[:, pl.ds(0, 2)], decoded.at[:, pl.ds(0, 2)], sems.at[1]

time: 45.5 us -> 45.6 us (level)
  no operation moved by 1% of the time
where the time goes in v5:
time: 45.6 us; the launch traced here: 45.5 us
  starting transfers between devices  15.5 us (34%)
  waiting for transfers between devices  13.7 us (30%)
  Pallas kernels  11.7 us (26%)
  other arithmetic  2.76 us (6%)
  between operations  1.03 us (2%)
  local copies, waits for them, and re-layouts  0.77 us (2%)
    ppermute x13, waiting for transfers between devices, swap(): lax.ppermute(value, AXIS, [(i, i ^ bits[i % 2]) for i in range(count)])  13.7 us
    pallas_call x3, Pallas kernels, call(): pl.pallas_call(kernel, out_shape=tuple((jax.ShapeDtypeStruct(shape, dtype...  11.7 us
    ppermute x13, starting transfers between devices, swap(): lax.ppermute(value, AXIS, [(i, i ^ bits[i % 2]) for i in range(count)])  10 us
    ppermute x1, starting transfers between devices, local(): outer = lax.ppermute(outer, AXIS, pairs)  5.48 us
    convert_element_type x1, other arithmetic, local(): jnp.stack([sum_0, sum_1]).astype(F32)  1.09 us
    reduce_sum x1, other arithmetic, local(): film_grad = jnp.sum(audio_rows[None, :, :, None] * totals, axis=1)  0.93 us
  transfers between devices with their start and end apart: 14, of which 10 were waited for; matrix products, arithmetic and copies ran while one was open for 3% of the time, Pallas kernels for 11%

profile of v5, /device:TPU:0, one launch (start us, length us, event | category | flops | bytes accessed | tf_op | source)
XLA Modules:
  0.0 45.5 jit_solution(3714539359361396077)
XLA Ops:
  0.6 0.0 copy-start
  0.6 0.0 copy-start.1
  0.7 0.7 %copy-done.1 = s32[2]{0:T(128)S(1)} copy-done((s32[2]{0:T(128)S(1)}, s32[2]{0:T(128)}, u32[]{:S(2)}) %copy-start.1) | copy-done | bytes 32
  1.4 0.0 copy-start.2
  1.4 0.0 copy-start.3
  1.4 0.0 copy-start.4
  1.4 0.0 copy-start.5
  1.4 0.0 copy-start.6
  1.4 1.7 %edges.1 = (bf16[2,4,128,128]{3,2,1,0:T(8,128)(2,1)S(1)}, bf16[2,4,128,128]{3,2,1,0:T(8,128)(2,1)S(1)}) custom-call(s32[2]{0:T(128)S(1)} %copy-done.1, bf16[8,8,128,128]{3,2,1,0:T(8,128)(2,1)} %maps.3, bf16[2,8,128,128]{3,2,1,0:T(8,128)(2,1)} %dout.5), custom_call_target="tpu_custom_call" | custom-call | bytes 4194304 | tf_op jit(solution)/shard_map/edges/pallas_call | solution.py:345
  3.1 5.5 %collective-permute-start = (bf16[2,4,128,128]{3,2,1,0:T(8,128)(2,1)S(1)}, bf16[2,4,128,128]{3,2,1,0:T(8,128)(2,1)S(1)}, u32[]{:S(2)}, u32[]{:S(2)}) collective-permute-start(bf16[2,4,128,128]{3,2,1,0:T(8,128)(2,1)S(1)} %get-tuple-element.20), channel_id=1, source_target_pairs={{0,15},{1,2},{2,1},{3,4},{4,3},{5,6},{6,5},{7,8},{8,7},{9,10},{10,... | collective-permute-start | bytes 786440 | tf_op jit(solution)/shard_map/ppermute | solution.py:440
  8.6 0.0 collective-permute-start.1
  8.6 0.0 copy-done
  8.6 0.0 copy-done.2
  8.6 0.0 copy-done.3
  8.6 0.0 copy-done.4
  8.6 0.0 copy-done.5
  8.6 0.0 copy-done.6
  8.6 4.8 %inner_columns.1 = (f32[2,2,256]{2,1,0:T(2,128)S(1)}, f32[2,256]{1,0:T(2,128)S(1)}, bf16[2,8,128,384]{3,2,1,0:T(8,128)(2,1)S(1)}, bf16[2,6,128,384]{3,2,1,0:T(8,...) custom-call(s32[2]{0:T(128)S(1)} %copy-done.2, ...), custom_call_target="tpu_custom_call" | custom-call | flops 1358954496 | bytes 4194304 | tf_op jit(solution)/shard_map/inner_columns/pallas_call | solution.py:345
  13.5 0.0 collective-permute-done.outer
  13.5 0.0 collective-permute-done.1.inner
  13.5 5.1 %rim_columns.1 = (bf16[2,8,128,128]{3,2,1,0:T(8,128)(2,1)}, f32[584,128]{1,0:T(8,128)S(1)}, bf16[592,128]{1,0:T(8,128)(2,1)S(1)}, f32[584,128]{1,0:T(8,128)S(1)}, bf16[592,128]{1,0:T(8,128)(2,1)S(1)}) custom-call(bf16[2,4,128,128]{3,2,1,0:T(8,128)(2,1)S(1)} %collective-permute-done.outer, bf16[2,4,128,128]{3,2,1,0:T(8,128)(2,1)S(1)} %collective-permute-done.1.inner, ...), custom_call_target="tpu_custom_call" | custom-call | flops 2113929216 | bytes 4194304 | tf_op jit(solution)/shard_map/rim_columns/pallas_call | solution.py:345
  18.6 0.6 %collective-permute-start.8 = (bf16[592,128]{1,0:T(8,128)(2,1)S(1)}, bf16[592,128]{1,0:T(8,128)(2,1)S(1)}, u32[]{:S(2)}, u32[]{:S(2)}) collective-permute-start(bf16[592,128]{1,0:T(8,128)(2,1)S(1)} %get-tuple-element.35), channel_id=1, source_target_pairs={{0,1},{1,0},{2,3},{3,2},{4,5},{5,4},{6,7},{7,6},{8,9},{9,8},{10,11... | collective-permute-start | bytes 454664 | tf_op jit(solution)/shard_map/ppermute | solution.py:359
  19.2 0.2 collective-permute-start.2
  19.4 0.8 %collective-permute-done.8 = bf16[592,128]{1,0:T(8,128)(2,1)S(1)} collective-permute-done((bf16[592,128]{1,0:T(8,128)(2,1)S(1)}, bf16[592,128]{1,0:T(8,128)(2,1)S(1)}, u32[]{:S(2)}, u32[]{:S(2)}) %collective-permute-start.8) | collective-permute-done | bytes 151584 | tf_op jit(solution)/shard_map/ppermute | solution.py:359
  20.3 0.3 collective-permute-done.2
  20.7 0.7 %collective-permute-start.9 = (bf16[304,128]{1,0:T(8,128)(2,1)S(1)}, bf16[304,128]{1,0:T(8,128)(2,1)S(1)}, u32[]{:S(2)}, u32[]{:S(2)}) collective-permute-start(bf16[304,128]{1,0:T(8,128)(2,1)S(1)} %pad_maximum_fusion.7), channel_id=1, source_target_pairs={{0,4},{1,3},{2,6},{3,1},{4,0},{5,7},{6,2},{7,5},{8,12},{9,11},{10,... | collective-permute-start | bytes 233480 | tf_op jit(solution)/shard_map/ppermute | solution.py:359
  21.5 1.9 %collective-permute-start.3 = (bf16[304,128]{1,0:T(8,128)(2,1)S(1)}, bf16[304,128]{1,0:T(8,128)(2,1)S(1)}, u32[]{:S(2)}, u32[]{:S(2)}) collective-permute-start(bf16[304,128]{1,0:T(8,128)(2,1)S(1)} %pad_maximum_fusion.4), channel_id=1, source_target_pairs={{0,2},{1,5},{2,0},{3,7},{4,6},{5,1},{6,4},{7,3},{8,10},{9,13},{10,... | collective-permute-start | bytes 233480 | tf_op jit(solution)/shard_map/ppermute | solution.py:359
  23.4 2.6 %collective-permute-done.9 = bf16[304,128]{1,0:T(8,128)(2,1)S(1)} collective-permute-done((bf16[304,128]{1,0:T(8,128)(2,1)S(1)}, bf16[304,128]{1,0:T(8,128)(2,1)S(1)}, u32[]{:S(2)}, u32[]{:S(2)}) %collective-permute-start.9) | collective-permute-done | bytes 77856 | tf_op jit(solution)/shard_map/ppermute | solution.py:359
  26.0 0.9 %collective-permute-start.10 = (bf16[304,128]{1,0:T(8,128)(2,1)S(1)}, bf16[304,128]{1,0:T(8,128)(2,1)S(1)}, u32[]{:S(2)}, u32[]{:S(2)}) collective-permute-start(bf16[304,128]{1,0:T(8,128)(2,1)S(1)} %pad_maximum_fusion.8), channel_id=1, source_target_pairs={{0,2},{1,9},{2,0},{3,11},{4,6},{5,13},{6,4},{7,15},{8,10},{9,1},{1... | collective-permute-start | bytes 233480 | tf_op jit(solution)/shard_map/ppermute | solution.py:359
  26.9 0.0 collective-permute-done.3
  27.0 2.3 %collective-permute-start.4 = (bf16[304,128]{1,0:T(8,128)(2,1)S(1)}, bf16[304,128]{1,0:T(8,128)(2,1)S(1)}, u32[]{:S(2)}, u32[]{:S(2)}) collective-permute-start(bf16[304,128]{1,0:T(8,128)(2,1)S(1)} %pad_maximum_fusion.5), channel_id=1, source_target_pairs={{0,8},{1,3},{2,10},{3,1},{4,12},{5,7},{6,14},{7,5},{8,0},{9,11},{1... | collective-permute-start | bytes 233480 | tf_op jit(solution)/shard_map/ppermute | solution.py:359
  29.3 1.4 %collective-permute-done.10 = bf16[304,128]{1,0:T(8,128)(2,1)S(1)} collective-permute-done((bf16[304,128]{1,0:T(8,128)(2,1)S(1)}, bf16[304,128]{1,0:T(8,128)(2,1)S(1)}, u32[]{:S(2)}, u32[]{:S(2)}) %collective-permute-start.10) | collective-permute-done | bytes 77856 | tf_op jit(solution)/shard_map/ppermute | solution.py:359
  30.8 1.7 %collective-permute-start.11 = (bf16[304,128]{1,0:T(8,128)(2,1)S(1)}, bf16[304,128]{1,0:T(8,128)(2,1)S(1)}, u32[]{:S(2)}, u32[]{:S(2)}) collective-permute-start(bf16[304,128]{1,0:T(8,128)(2,1)S(1)} %pad_maximum_fusion.9), channel_id=1, source_target_pairs={{0,8},{1,5},{2,10},{3,7},{4,12},{5,1},{6,14},{7,3},{8,0},{9,13},{1... | collective-permute-start | bytes 233480 | tf_op jit(solution)/shard_map/ppermute | solution.py:359
  32.5 0.8 %collective-permute-done.4 = bf16[304,128]{1,0:T(8,128)(2,1)S(1)} collective-permute-done((bf16[304,128]{1,0:T(8,128)(2,1)S(1)}, bf16[304,128]{1,0:T(8,128)(2,1)S(1)}, u32[]{:S(2)}, u32[]{:S(2)}) %collective-permute-start.4) | collective-permute-done | bytes 77856 | tf_op jit(solution)/shard_map/ppermute | solution.py:359
  33.4 0.4 collective-permute-start.5
  33.8 3.4 %collective-permute-done.11 = bf16[304,128]{1,0:T(8,128)(2,1)S(1)} collective-permute-done((bf16[304,128]{1,0:T(8,128)(2,1)S(1)}, bf16[304,128]{1,0:T(8,128)(2,1)S(1)}, u32[]{:S(2)}, u32[]{:S(2)}) %collective-permute-start.11) | collective-permute-done | bytes 77856 | tf_op jit(solution)/shard_map/ppermute | solution.py:359
  37.3 0.1 collective-permute-start.12
  37.4 0.9 %collective-permute-done.5 = bf16[304,128]{1,0:T(8,128)(2,1)S(1)} collective-permute-done((bf16[304,128]{1,0:T(8,128)(2,1)S(1)}, bf16[304,128]{1,0:T(8,128)(2,1)S(1)}, u32[]{:S(2)}, u32[]{:S(2)}) %collective-permute-start.5) | collective-permute-done | bytes 77856 | tf_op jit(solution)/shard_map/ppermute | solution.py:359
  38.3 1.1 %collective-permute-start.6 = (bf16[288,128]{1,0:T(8,128)(2,1)S(1)}, bf16[288,128]{1,0:T(8,128)(2,1)S(1)}, u32[]{:S(2)}, u32[]{:S(2)}) collective-permute-start(bf16[288,128]{1,0:T(8,128)(2,1)S(1)} %fusion.3), channel_id=1, source_target_pairs={{0,2},{1,5},{2,0},{3,7},{4,6},{5,1},{6,4},{7,3},{8,10},{9,13},{10,... | collective-permute-start | bytes 221192 | tf_op jit(solution)/shard_map/ppermute | solution.py:359
  39.4 2.3 %collective-permute-done.12 = bf16[288,128]{1,0:T(8,128)(2,1)S(1)} collective-permute-done((bf16[288,128]{1,0:T(8,128)(2,1)S(1)}, bf16[288,128]{1,0:T(8,128)(2,1)S(1)}, u32[]{:S(2)}, u32[]{:S(2)}) %collective-permute-start.12) | collective-permute-done | bytes 73760 | tf_op jit(solution)/shard_map/ppermute | solution.py:359
  41.7 0.1 collective-permute-start.13
  41.8 0.9 %collective-permute-done.6 = bf16[288,128]{1,0:T(8,128)(2,1)S(1)} collective-permute-done((bf16[288,128]{1,0:T(8,128)(2,1)S(1)}, bf16[288,128]{1,0:T(8,128)(2,1)S(1)}, u32[]{:S(2)}, u32[]{:S(2)}) %collective-permute-start.6) | collective-permute-done | bytes 73760 | tf_op jit(solution)/shard_map/ppermute | solution.py:359
  42.7 0.1 collective-permute-start.7
  42.9 0.9 %multiply_reduce_fusion = f32[2,256,256]{2,1,0:T(8,128)} fusion(f32[2,2,256]{2,1,0:T(2,128)S(1)} %mul.32, f32[2,256]{1,0:T(2,128)S(1)} %get-tuple-element.36), kind=kLoop, calls=%fused_computation | loop fusion | flops 393216 | bytes 530432 | tf_op jit(solution)/shard_map/reduce_sum | solution.py:508
  43.8 0.0 collective-permute-done.13
  43.8 0.4 collective-permute-done.7
  44.2 0.1 broadcast_select_fusion.1
  44.4 1.1 %maximum_convert_fusion = f32[2,3,3,128,128]{4,3,2,1,0:T(8,128)} fusion(bf16[1,3,3,128,128]{4,3,2,1,0:T(8,128)(2,1)S(1)} %bitcast.6, bf16[1,3,3,128,128]{4,3,2,1,0:T(8,128)(2,1)S(1)} %bitcast.7), kind=kLoop, calls=%fused_computation.1 | loop fusion | flops 589824 | bytes 1769472 | tf_op jit(solution)/shard_map/convert_element_type | solution.py:509
  (46 shorter events, 0.7 us)
Async XLA Ops:
  0.6 8.0 %copy-start = (bf16[2,8,128,128]{3,2,1,0:T(8,128)(2,1)S(1)}, bf16[2,8,128,128]{3,2,1,0:T(8,128)(2,1)}, u32[]{:S(2)}) copy-start(bf16[2,8,128,128]{3,2,1,0:T(8,128)(2,1)} %dout.5) | copy-start | bytes 1572868
  0.6 0.7 %copy-start.1 = (s32[2]{0:T(128)S(1)}, s32[2]{0:T(128)}, u32[]{:S(2)}) copy-start(s32[2]{0:T(128)} %identity.3) | copy-start | bytes 28
  1.4 7.2 %copy-start.2 = (s32[2]{0:T(128)S(1)}, s32[2]{0:T(128)}, u32[]{:S(2)}) copy-start(s32[2]{0:T(128)} %identity.3) | copy-start | bytes 28
  1.4 7.2 %copy-start.3 = (bf16[2,3,3,128,128]{4,3,2,1,0:T(8,128)(2,1)S(1)}, bf16[2,3,3,128,128]{4,3,2,1,0:T(8,128)(2,1)}, u32[]{:S(2)}) copy-start(bf16[2,3,3,128,128]{4,3,2,1,0:T(8,128)(2,1)} %weights.3) | copy-start | bytes 1769476
  1.4 7.2 %copy-start.4 = (f32[2,256,256]{2,1,0:T(8,128)S(1)}, f32[2,256,256]{2,1,0:T(8,128)}, u32[]{:S(2)}) copy-start(f32[2,256,256]{2,1,0:T(8,128)} %film_w.1) | copy-start | bytes 1572868
  1.4 7.2 %copy-start.5 = (f32[64,256]{1,0:T(8,128)S(1)}, f32[64,256]{1,0:T(8,128)}, u32[]{:S(2)}) copy-start(f32[64,256]{1,0:T(8,128)} %audio.1) | copy-start | bytes 196612
  1.4 7.3 %copy-start.6 = (s32[2]{0:T(128)S(1)}, s32[2]{0:T(128)}, u32[]{:S(2)}) copy-start(s32[2]{0:T(128)} %audio_index.1) | copy-start | bytes 28
  3.1 10.4 %collective-permute-start = (bf16[2,4,128,128]{3,2,1,0:T(8,128)(2,1)S(1)}, bf16[2,4,128,128]{3,2,1,0:T(8,128)(2,1)S(1)}, u32[]{:S(2)}, u32[]{:S(2)}) collective-permute-start(bf16[2,4,128,128]{3,2,1,0:T(8,128)(2,1)S(1)} %get-tuple-element.20), channel_id=1, source_target_pairs={{0,15},{1,2},{2,1},{3,4},{4,3},{5,6},{6,5},{7,8},{8,7},{9,10},{10,... | collective-permute-start | bytes 786440 | tf_op jit(solution)/shard_map/ppermute | solution.py:440
  8.6 4.9 %collective-permute-start.1 = (bf16[2,4,128,128]{3,2,1,0:T(8,128)(2,1)S(1)}, bf16[2,4,128,128]{3,2,1,0:T(8,128)(2,1)S(1)}, u32[]{:S(2)}, u32[]{:S(2)}) collective-permute-start(bf16[2,4,128,128]{3,2,1,0:T(8,128)(2,1)S(1)} %get-tuple-element.21), channel_id=1, source_target_pairs={{0,1},{1,0},{2,3},{3,2},{4,5},{5,4},{6,7},{7,6},{8,9},{9,8},{10,11... | collective-permute-start | bytes 786440 | tf_op jit(solution)/shard_map/ppermute | solution.py:359
  18.6 1.6 %collective-permute-start.8 = (bf16[592,128]{1,0:T(8,128)(2,1)S(1)}, bf16[592,128]{1,0:T(8,128)(2,1)S(1)}, u32[]{:S(2)}, u32[]{:S(2)}) collective-permute-start(bf16[592,128]{1,0:T(8,128)(2,1)S(1)} %get-tuple-element.35), channel_id=1, source_target_pairs={{0,1},{1,0},{2,3},{3,2},{4,5},{5,4},{6,7},{7,6},{8,9},{9,8},{10,11... | collective-permute-start | bytes 454664 | tf_op jit(solution)/shard_map/ppermute | solution.py:359
  19.2 1.4 %collective-permute-start.2 = (bf16[592,128]{1,0:T(8,128)(2,1)S(1)}, bf16[592,128]{1,0:T(8,128)(2,1)S(1)}, u32[]{:S(2)}, u32[]{:S(2)}) collective-permute-start(bf16[592,128]{1,0:T(8,128)(2,1)S(1)} %get-tuple-element.33), channel_id=1, source_target_pairs={{0,1},{1,0},{2,3},{3,2},{4,5},{5,4},{6,7},{7,6},{8,9},{9,8},{10,11... | collective-permute-start | bytes 454664 | tf_op jit(solution)/shard_map/ppermute | solution.py:359
  20.7 5.2 %collective-permute-start.9 = (bf16[304,128]{1,0:T(8,128)(2,1)S(1)}, bf16[304,128]{1,0:T(8,128)(2,1)S(1)}, u32[]{:S(2)}, u32[]{:S(2)}) collective-permute-start(bf16[304,128]{1,0:T(8,128)(2,1)S(1)} %pad_maximum_fusion.7), channel_id=1, source_target_pairs={{0,4},{1,3},{2,6},{3,1},{4,0},{5,7},{6,2},{7,5},{8,12},{9,11},{10,... | collective-permute-start | bytes 233480 | tf_op jit(solution)/shard_map/ppermute | solution.py:359
  21.5 5.5 %collective-permute-start.3 = (bf16[304,128]{1,0:T(8,128)(2,1)S(1)}, bf16[304,128]{1,0:T(8,128)(2,1)S(1)}, u32[]{:S(2)}, u32[]{:S(2)}) collective-permute-start(bf16[304,128]{1,0:T(8,128)(2,1)S(1)} %pad_maximum_fusion.4), channel_id=1, source_target_pairs={{0,2},{1,5},{2,0},{3,7},{4,6},{5,1},{6,4},{7,3},{8,10},{9,13},{10,... | collective-permute-start | bytes 233480 | tf_op jit(solution)/shard_map/ppermute | solution.py:359
  26.0 4.7 %collective-permute-start.10 = (bf16[304,128]{1,0:T(8,128)(2,1)S(1)}, bf16[304,128]{1,0:T(8,128)(2,1)S(1)}, u32[]{:S(2)}, u32[]{:S(2)}) collective-permute-start(bf16[304,128]{1,0:T(8,128)(2,1)S(1)} %pad_maximum_fusion.8), channel_id=1, source_target_pairs={{0,2},{1,9},{2,0},{3,11},{4,6},{5,13},{6,4},{7,15},{8,10},{9,1},{1... | collective-permute-start | bytes 233480 | tf_op jit(solution)/shard_map/ppermute | solution.py:359
  27.0 6.3 %collective-permute-start.4 = (bf16[304,128]{1,0:T(8,128)(2,1)S(1)}, bf16[304,128]{1,0:T(8,128)(2,1)S(1)}, u32[]{:S(2)}, u32[]{:S(2)}) collective-permute-start(bf16[304,128]{1,0:T(8,128)(2,1)S(1)} %pad_maximum_fusion.5), channel_id=1, source_target_pairs={{0,8},{1,3},{2,10},{3,1},{4,12},{5,7},{6,14},{7,5},{8,0},{9,11},{1... | collective-permute-start | bytes 233480 | tf_op jit(solution)/shard_map/ppermute | solution.py:359
  30.8 6.4 %collective-permute-start.11 = (bf16[304,128]{1,0:T(8,128)(2,1)S(1)}, bf16[304,128]{1,0:T(8,128)(2,1)S(1)}, u32[]{:S(2)}, u32[]{:S(2)}) collective-permute-start(bf16[304,128]{1,0:T(8,128)(2,1)S(1)} %pad_maximum_fusion.9), channel_id=1, source_target_pairs={{0,8},{1,5},{2,10},{3,7},{4,12},{5,1},{6,14},{7,3},{8,0},{9,13},{1... | collective-permute-start | bytes 233480 | tf_op jit(solution)/shard_map/ppermute | solution.py:359
  33.4 4.8 %collective-permute-start.5 = (bf16[304,128]{1,0:T(8,128)(2,1)S(1)}, bf16[304,128]{1,0:T(8,128)(2,1)S(1)}, u32[]{:S(2)}, u32[]{:S(2)}) collective-permute-start(bf16[304,128]{1,0:T(8,128)(2,1)S(1)} %pad_maximum_fusion.6), channel_id=1, source_target_pairs={{0,4},{1,9},{2,6},{3,11},{4,0},{5,13},{6,2},{7,15},{8,12},{9,1},{1... | collective-permute-start | bytes 233480 | tf_op jit(solution)/shard_map/ppermute | solution.py:359
  37.3 4.4 %collective-permute-start.12 = (bf16[288,128]{1,0:T(8,128)(2,1)S(1)}, bf16[288,128]{1,0:T(8,128)(2,1)S(1)}, u32[]{:S(2)}, u32[]{:S(2)}) collective-permute-start(bf16[288,128]{1,0:T(8,128)(2,1)S(1)} %fusion), channel_id=1, source_target_pairs={{0,4},{1,3},{2,6},{3,1},{4,0},{5,7},{6,2},{7,5},{8,12},{9,11},{10,... | collective-permute-start | bytes 221192 | tf_op jit(solution)/shard_map/ppermute | solution.py:359
  38.3 4.4 %collective-permute-start.6 = (bf16[288,128]{1,0:T(8,128)(2,1)S(1)}, bf16[288,128]{1,0:T(8,128)(2,1)S(1)}, u32[]{:S(2)}, u32[]{:S(2)}) collective-permute-start(bf16[288,128]{1,0:T(8,128)(2,1)S(1)} %fusion.3), channel_id=1, source_target_pairs={{0,2},{1,5},{2,0},{3,7},{4,6},{5,1},{6,4},{7,3},{8,10},{9,13},{10,... | collective-permute-start | bytes 221192 | tf_op jit(solution)/shard_map/ppermute | solution.py:359
  41.7 2.0 %collective-permute-start.13 = (bf16[576,128]{1,0:T(8,128)(2,1)S(1)}, bf16[576,128]{1,0:T(8,128)(2,1)S(1)}, u32[]{:S(2)}, u32[]{:S(2)}) collective-permute-start(bf16[576,128]{1,0:T(8,128)(2,1)S(1)} %pad_maximum_fusion.3), channel_id=1, source_target_pairs={{0,1},{1,0},{2,3},{3,2},{4,5},{5,4},{6,7},{7,6},{8,9},{9,8},{10,11... | collective-permute-start | bytes 442376 | tf_op jit(solution)/shard_map/ppermute | solution.py:359
  42.7 1.4 %collective-permute-start.7 = (bf16[576,128]{1,0:T(8,128)(2,1)S(1)}, bf16[576,128]{1,0:T(8,128)(2,1)S(1)}, u32[]{:S(2)}, u32[]{:S(2)}) collective-permute-start(bf16[576,128]{1,0:T(8,128)(2,1)S(1)} %pad_maximum_fusion.2), channel_id=1, source_target_pairs={{0,1},{1,0},{2,3},{3,2},{4,5},{5,4},{6,7},{7,6},{8,9},{9,8},{10,11... | collective-permute-start | bytes 442376 | tf_op jit(solution)/shard_map/ppermute | solution.py:359
